TPU v7x, 32 devices: a whole 2x2x4 slice. The times are simulated.
32 devices in a mesh: tower: 8 (over z, x), plate: 4 (over y, core).
Axes of the slice: x: 2, y: 2, z: 4, core: 2. Of those that a mesh axis runs over, the one named last changes fastest.
Arguments:
- features: bfloat16 [8, 1024, 128], P('tower', 'plate'), may hold values from -6 to 6
- adjoint: bfloat16 [8, 1024, 128], P('tower', 'plate'), may hold values from -6 to 6
- positions: bfloat16 [3, 8, 1024], P(None, 'tower', 'plate'), may hold values from 0 to 1
- w_rbf: bfloat16 [16, 128], replicated, may hold values from -1.5 to 1.5
- b_rbf: float32 [128], replicated, may hold values from -1 to 1
- w_filter: bfloat16 [128, 128], replicated, may hold values from -0.5 to 0.5
- b_filter: float32 [128], replicated, may hold values from -1 to 1
- atom_counts: int32 [8, 4], P('tower', 'plate'), may hold values from 128 to 256, as said below
- tile_counts: int32 [8, 4], P('tower', 'plate'), may hold values from 1 to 56, as said below
- tower_tiles: int32 [8, 4, 56], P('tower', 'plate'), may hold values from 0 to 23
- plate_tiles: int32 [8, 4, 56], P('tower', 'plate'), may hold values from 0 to 31
- image_shifts: int32 [8, 4, 56], P('tower', 'plate'), may hold values from 0 to 8
Outputs:
- grad_features: float32 [8, 1024, 128], P('tower', 'plate')
- grad_positions: float32 [3, 8, 1024], P(None, 'tower', 'plate')
- grad_w_rbf: float32 [16, 128], replicated
- grad_b_rbf: float32 [128], replicated
- grad_w_filter: float32 [128, 128], replicated
- grad_b_filter: float32 [128], replicated
Inputs may be any that keep to these rules, and one draw needn't show every extreme that they name: `atom_counts`: 256 in at least one brick. `tile_counts`: 56 in at least one brick; entries past the count are unused. `tower_tiles`: tiles below 8 lie in the brick below, the next 8 in the brick itself, the rest in the brick above. `plate_tiles`: tile v lies in brick v // 8 of the same plate. `image_shifts`: shift c moves the receiver by c // 3 - 1 along x and c % 3 - 1 along y.
All inputs are finite; a program needn't handle non-finite values.
Results may differ from a plain program's by a relative error of at most 0.005.
Values may be sent and summed in bfloat16 or wider, within the bound.
No kernel may reach another device: no remote copies, remote signals or barrier semaphores. Data moves between devices by JAX's collectives and lax.ppermute only.
A program may use at most 64 MiB of HBM per device.

v0:
```python
import math

import jax
import jax.numpy as jnp
from jax import lax
from jax.sharding import PartitionSpec as P

TILE = 32


box_side = 1.0
brick_height = 1.0
cutoff_radius = 3.0
soften = 0.01
sharpness = 10.0
log_two = math.log(2.0)


def shifted(block, axis, distance):
    devices = range(lax.axis_size(axis))
    route = [((i - distance) % len(devices), i) for i in devices]
    return lax.ppermute(block, axis, route)


def shift_vector(shift_code, tower_tile, per_brick):
    step_z = tower_tile // per_brick - 1
    return jnp.stack(
        [
            (shift_code // 3 - 1).astype(jnp.float32) * box_side,
            (shift_code % 3 - 1).astype(jnp.float32) * box_side,
            step_z.astype(jnp.float32) * brick_height,
        ]
    )


def pair_tile(adj_rows, recv_pos, feat_rows, send_pos, shift_vec, w_rbf, b_rbf, w_filter, b_filter):
    size_recv = adj_rows.shape[0]
    size_send = feat_rows.shape[0]
    feat_width = adj_rows.shape[1]
    displace = recv_pos[:, :, None] + shift_vec[:, None, None] - send_pos[:, None, :]
    distance = jnp.sqrt(jnp.sum(displace * displace, axis=0) + soften).reshape(-1)
    nbasis = w_rbf.shape[0]
    centres = jnp.arange(nbasis, dtype=jnp.float32) * (cutoff_radius / (nbasis - 1))
    offsets = distance[None, :] - centres[:, None]
    basis = jnp.exp(-sharpness * offsets * offsets)
    basis_b = basis.astype(jnp.bfloat16)
    preact = (
        lax.dot_general(
            basis_b, w_rbf, (((0,), (0,)), ((), ())), preferred_element_type=jnp.float32
        )
        + b_rbf
    )
    softed = (jax.nn.softplus(preact) - log_two).astype(jnp.bfloat16)
    filter_raw = jnp.dot(softed, w_filter, preferred_element_type=jnp.float32) + b_filter
    inside = distance < cutoff_radius
    phase_arg = math.pi / cutoff_radius * distance
    envelope = jnp.where(inside, 0.5 * (jnp.cos(phase_arg) + 1.0), 0.0)
    slope = jnp.where(inside, -0.5 * (math.pi / cutoff_radius) * jnp.sin(phase_arg), 0.0)
    adj_wide = adj_rows.astype(jnp.float32)
    feat_wide = feat_rows.astype(jnp.float32)
    filtered = (filter_raw * envelope[:, None]).reshape(size_recv, size_send, feat_width)
    grad_rows = jnp.einsum("if,ijf->jf", adj_wide, filtered)
    adjoint_pair = (adj_wide[:, None, :] * feat_wide[None, :, :]).reshape(
        size_recv * size_send, feat_width
    )
    d_raw = adjoint_pair * envelope[:, None]
    d_raw_b = d_raw.astype(jnp.bfloat16)
    grad_bf = jnp.sum(d_raw, axis=0)
    grad_wf = lax.dot_general(
        softed, d_raw_b, (((0,), (0,)), ((), ())), preferred_element_type=jnp.float32
    )
    d_soft = lax.dot_general(
        d_raw_b, w_filter, (((1,), (1,)), ((), ())), preferred_element_type=jnp.float32
    )
    d_pre = d_soft * jax.nn.sigmoid(preact)
    d_pre_b = d_pre.astype(jnp.bfloat16)
    grad_br = jnp.sum(d_pre, axis=0)
    grad_wr = lax.dot_general(
        basis_b, d_pre_b, (((1,), (0,)), ((), ())), preferred_element_type=jnp.float32
    )
    d_basis = lax.dot_general(
        w_rbf, d_pre_b, (((1,), (1,)), ((), ())), preferred_element_type=jnp.float32
    )
    d_dist = jnp.sum(d_basis * basis * (-2.0 * sharpness) * offsets, axis=0)
    d_dist = d_dist + jnp.sum(adjoint_pair * filter_raw, axis=1) * slope
    radial = (d_dist / distance).reshape(size_recv, size_send)
    pull = displace * radial[None]
    return (
        grad_rows,
        jnp.sum(pull, axis=2),
        -jnp.sum(pull, axis=1),
        (grad_wr, grad_br, grad_wf, grad_bf),
    )


def add_into(array, piece, starts):
    current = lax.dynamic_slice(array, starts, piece.shape)
    return lax.dynamic_update_slice(array, current + piece, starts)


def add_weights(left, right):
    return jax.tree.map(lambda first_term, second_term: first_term + second_term, left, right)


def local(
    features,
    adjoint,
    positions,
    w_rbf,
    b_rbf,
    w_filter,
    b_filter,
    atom_counts,
    tile_counts,
    tower_tiles,
    plate_tiles,
    image_shifts,
):
    brick_atoms = features.shape[1]
    feat_width = features.shape[2]
    tile_size = TILE
    per_brick = brick_atoms // tile_size
    plate_count = lax.axis_size("plate")
    zero_i = jnp.int32(0)
    live_mask = jnp.arange(brick_atoms, dtype=jnp.int32) < atom_counts[0, 0]
    zero_b = jnp.zeros((), jnp.bfloat16)
    own_feat = jnp.where(live_mask[:, None], features[0], zero_b)
    own_adj = jnp.where(live_mask[:, None], adjoint[0], zero_b)
    own_pos = positions[:, 0, :]
    from_below = shifted((own_adj, own_pos), "tower", 1)
    from_above = shifted((own_adj, own_pos), "tower", -1)
    tower_adj = jnp.concatenate([from_below[0], own_adj, from_above[0]], axis=0)
    tower_pos_b = jnp.concatenate([from_below[1], own_pos, from_above[1]], axis=1)
    tower_pos = tower_pos_b.astype(jnp.float32)
    weight_zero = (
        jnp.zeros(w_rbf.shape, jnp.float32),
        jnp.zeros(b_rbf.shape, jnp.float32),
        jnp.zeros(w_filter.shape, jnp.float32),
        jnp.zeros(b_filter.shape, jnp.float32),
    )
    plate_feat, plate_pos_b = (
        lax.all_gather(own_feat, "plate", axis=0, tiled=True),
        lax.all_gather(own_pos, "plate", axis=1, tiled=True),
    )
    plate_pos = plate_pos_b.astype(jnp.float32)

    def visit_listed(entry, totals):
        acc_dh, acc_gp, acc_tower, acc_weights = totals
        tower_tile = tower_tiles[0, 0, entry]
        plate_tile = plate_tiles[0, 0, entry]
        recv_start = tower_tile * tile_size
        send_start = plate_tile * tile_size
        adj_rows = lax.dynamic_slice_in_dim(tower_adj, recv_start, tile_size, 0)
        recv_pos = lax.dynamic_slice_in_dim(tower_pos, recv_start, tile_size, 1)
        feat_rows = lax.dynamic_slice_in_dim(plate_feat, send_start, tile_size, 0)
        send_pos = lax.dynamic_slice_in_dim(plate_pos, send_start, tile_size, 1)
        shift_vec = shift_vector(image_shifts[0, 0, entry], tower_tile, per_brick)
        grad_rows, grad_recv, grad_send, grad_weights = pair_tile(
            adj_rows, recv_pos, feat_rows, send_pos, shift_vec, w_rbf, b_rbf, w_filter, b_filter
        )
        brick_index = plate_tile // per_brick
        local_start = plate_tile % per_brick * tile_size
        acc_dh = add_into(acc_dh, grad_rows[None], (brick_index, local_start, zero_i))
        acc_gp = add_into(acc_gp, grad_send[None], (brick_index, zero_i, local_start))
        acc_tower = add_into(acc_tower, grad_recv, (zero_i, recv_start))
        return (acc_dh, acc_gp, acc_tower, add_weights(acc_weights, grad_weights))

    initial = (
        jnp.zeros((plate_count, brick_atoms, feat_width), jnp.float32),
        jnp.zeros((plate_count, 3, brick_atoms), jnp.float32),
        jnp.zeros((3, 3 * brick_atoms), jnp.float32),
        weight_zero,
    )
    acc_dh, acc_gp, tower_grad, acc_weights = lax.fori_loop(
        0, tile_counts[0, 0], visit_listed, initial
    )
    home_dh, home_gp = (
        lax.psum_scatter(acc_dh, "plate", scatter_dimension=0, tiled=True),
        lax.psum_scatter(acc_gp, "plate", scatter_dimension=0, tiled=True),
    )
    plate_dh = home_dh[0]
    plate_gp = home_gp[0]
    back_down = shifted(tower_grad[:, :brick_atoms], "tower", -1)
    back_up = shifted(tower_grad[:, 2 * brick_atoms :], "tower", 1)
    total_pos = plate_gp + tower_grad[:, brick_atoms : 2 * brick_atoms] + back_down + back_up
    tile_total = tile_counts[0, 0].astype(jnp.float32)
    summed = lax.psum(
        (acc_weights[0], acc_weights[1], acc_weights[2], acc_weights[3], tile_total),
        ("tower", "plate"),
    )
    scale = lax.rsqrt(summed[4] * (tile_size * tile_size))
    grad_features = jnp.where(live_mask[:, None], plate_dh, 0.0)[None]
    grad_positions = total_pos.reshape(3, 1, brick_atoms)
    return (
        grad_features,
        grad_positions,
        summed[0] * scale,
        summed[1] * scale,
        summed[2] * scale,
        summed[3] * scale,
    )


def solution(mesh):
    in_specs = (
        P("tower", "plate", None),
        P("tower", "plate", None),
        P(None, "tower", "plate"),
        P(),
        P(),
        P(),
        P(),
        P("tower", "plate"),
        P("tower", "plate"),
        P("tower", "plate", None),
        P("tower", "plate", None),
        P("tower", "plate", None),
    )
    out_specs = (P("tower", "plate", None), P(None, "tower", "plate"), P(), P(), P(), P())
    return jax.shard_map(local, mesh=mesh, in_specs=in_specs, out_specs=out_specs, check_vma=False)
```

profile of v0, /device:TPU:0, one launch (start us, length us, event | category | flops | bytes accessed | tf_op | source)
XLA Modules:
  0.0 1105.8 jit_solution(14880807231153509916)
XLA Ops:
  8.7 1.0 bitcast_select_fusion
  9.7 3.0 collective-permute-start.2
  12.7 3.1 collective-permute-start.3
  15.8 4.7 collective-permute-start.1
  20.5 5.2 all-gather
  25.7 5.9 all_gather.7
  31.9 0.6 copy-done.6
  32.5 303.9 %while.25 = (s32[]{:T(128)}, f32[4,256,128]{2,1,0:T(8,128)S(1)}, f32[4,3,256]{2,1,0:T(4,128)S(1)}, f32[3,768]{1,0:T(4,128)S(1)}, f32[16,128]{1,0:T(8,128)S(1)}, ...) while((s32[]{:T(128)}, f32[4,256,128]{2,1,0:T(8,128)S(1)}, ...), condition=%wide.region_8.9_spmd, body=%wide.region_0.8_spmd.sunk | while | flops 118017312 | bytes 6281055 | solution.py:174
  36.4 0.6 fusion.71
  41.6 0.6 constant_dynamic-slice_fusion.10
  43.9 0.6 fusion.73
  53.2 0.6 fusion.71
  58.4 0.6 constant_dynamic-slice_fusion.10
  60.7 0.6 fusion.73
  70.0 0.6 fusion.71
  75.2 0.6 constant_dynamic-slice_fusion.10
  77.5 0.6 fusion.73
  86.9 0.6 fusion.71
  92.2 0.6 constant_dynamic-slice_fusion.10
  94.4 0.6 fusion.73
  103.9 0.6 fusion.71
  109.1 0.6 constant_dynamic-slice_fusion.10
  111.3 0.6 fusion.73
  120.8 0.6 fusion.71
  128.2 0.6 fusion.73
  137.6 0.6 fusion.71
  142.8 0.6 constant_dynamic-slice_fusion.10
  145.1 0.6 fusion.73
  154.4 0.6 fusion.71
  159.6 0.6 constant_dynamic-slice_fusion.10
  161.9 0.6 fusion.73
  171.1 0.6 fusion.71
  178.6 0.6 fusion.73
  188.0 0.6 fusion.71
  195.5 0.6 fusion.73
  204.8 0.6 fusion.71
  212.3 0.6 fusion.73
  221.6 0.6 fusion.71
  229.1 0.6 fusion.73
  238.5 0.6 fusion.71
  245.9 0.6 fusion.73
  255.4 0.6 fusion.71
  262.9 0.6 fusion.73
  272.3 0.6 fusion.71
  277.5 0.6 constant_dynamic-slice_fusion.10
  279.8 0.6 fusion.73
  289.1 0.6 fusion.71
  294.4 0.6 constant_dynamic-slice_fusion.10
  296.6 0.6 fusion.73
  305.9 0.6 fusion.71
  311.2 0.6 constant_dynamic-slice_fusion.10
  313.4 0.6 fusion.73
  322.8 0.6 fusion.71
  330.2 0.6 fusion.73
  336.5 0.6 copy-done.1
  337.8 0.6 copy-done.10
  339.1 677.5 %all-reduce.1 = (f32[16,128]{1,0:T(8,128)S(1)}, f32[]{:T(128)}, f32[128]{0:T(128)S(1)}, f32[128]{0:T(128)S(1)}) all-reduce(f32[16,128]{1,0:T(8,128)S(1)} %get-tuple-element.335, f32[]{:T(128)S(6)} %convert_element_type.74, f32[128]{0:T(128)S(1)} %get-tuple-element.336, ...), channel_id=1, replica_groups=mesh['tower'=8,'plate'=4] {'tower','plate'}, use_global_device_ids=true, to_apply=%region_11.12 | all-reduce | flops 2305 | bytes 18440 | tf_op jit(solution)/shard_map/psum | solution.py:187
  1017.3 4.1 collective-permute-start.4
  1021.9 0.6 broadcast_multiply_fusion.3
  1022.5 10.3 all-reduce
  1032.8 0.7 fusion.28
  1034.0 61.2 %all-reduce.4.cloned.1.call-done = f32[128,128]{1,0:T(8,128)} async-done(((f32[128,128]{1,0:T(8,128)}), f32[128,128]{1,0:T(8,128)}) %all-reduce.4.cloned.1.call-update) | async-done | bytes 65552 | tf_op jit(solution)/shard_map/psum | solution.py:187
  1095.2 1.5 broadcast_multiply_fusion.2
  1096.7 1.7 broadcast_select_fusion
  (541 shorter events, 76.3 us)
Async XLA Ops:
  8.0 1087.2 %all-reduce.4.cloned.1.call-start = ((), (), s32[]{:S(2)}) async-start(), calls=%async_computation.2 | async-start | bytes 131072 | tf_op jit(solution)/shard_map/psum | solution.py:187
  9.7 6.1 copy-start.5
  9.7 21.9 %collective-permute-start.2 = (bf16[256,128]{1,0:T(8,128)(2,1)S(1)}, bf16[256,128]{1,0:T(8,128)(2,1)S(1)}, u32[]{:S(2)}, u32[]{:S(2)}) collective-permute-start(bf16[256,128]{1,0:T(8,128)(2,1)S(1)} %get-tuple-element.416), channel_id=1, source_target_pairs={{28,0},{0,4},{4,8},{8,12},{12,16},{16,20},{20,24},{24,28},{29,1},{... | collective-permute-start | bytes 196616 | tf_op jit(solution)/shard_map/ppermute | solution.py:22
  12.7 18.9 %collective-permute-start.3 = (bf16[256,128]{1,0:T(8,128)(2,1)S(1)}, bf16[256,128]{1,0:T(8,128)(2,1)S(1)}, u32[]{:S(2)}, u32[]{:S(2)}) collective-permute-start(bf16[256,128]{1,0:T(8,128)(2,1)S(1)} %get-tuple-element.416), channel_id=1, source_target_pairs={{4,0},{8,4},{12,8},{16,12},{20,16},{24,20},{28,24},{0,28},{5,1},{9... | collective-permute-start | bytes 196616 | tf_op jit(solution)/shard_map/ppermute | solution.py:22
  15.8 15.8 %collective-permute-start = (bf16[3,256]{1,0:T(4,128)(2,1)S(1)}, bf16[3,256]{1,0:T(4,128)(2,1)S(1)}, u32[]{:S(2)}, u32[]{:S(2)}) collective-permute-start(bf16[3,256]{1,0:T(4,128)(2,1)S(1)} %bitcast.114), channel_id=1, source_target_pairs={{28,0},{0,4},{4,8},{8,12},{12,16},{16,20},{20,24},{24,28},{29,1},{... | collective-permute-start | bytes 4616 | tf_op jit(solution)/shard_map/ppermute | solution.py:22
  15.8 15.8 %collective-permute-start.1 = (bf16[3,256]{1,0:T(4,128)(2,1)S(1)}, bf16[3,256]{1,0:T(4,128)(2,1)S(1)}, u32[]{:S(2)}, u32[]{:S(2)}) collective-permute-start(bf16[3,256]{1,0:T(4,128)(2,1)S(1)} %bitcast.115), channel_id=1, source_target_pairs={{4,0},{8,4},{12,8},{16,12},{20,16},{24,20},{28,24},{0,28},{5,1},{9... | collective-permute-start | bytes 4616 | tf_op jit(solution)/shard_map/ppermute | solution.py:22
  31.7 0.8 copy-start.6
  31.8 0.7 copy-start.8
  31.8 0.7 copy-start.9
  31.8 0.7 copy-start.2
  31.8 0.7 copy-start.3
  31.8 0.7 copy-start.4
  31.9 0.7 copy-start.7
  336.5 0.6 copy-start.1
  336.5 680.7 %copy-start = (f32[4,256,128]{2,1,0:T(8,128)}, f32[4,256,128]{2,1,0:T(8,128)S(1)}, u32[]{:S(2)}) copy-start(f32[4,256,128]{2,1,0:T(8,128)S(1)} %get-tuple-element.332) | copy-start | bytes 1572868
  337.1 759.6 %reduce-scatter.2.cloned.1.call-start = ((), (), s32[]{:S(2)}) async-start(), calls=%async_computation.1 | async-start | bytes 655360 | tf_op jit(solution)/shard_map/reduce_scatter | solution.py:178
  337.8 0.7 copy-start.10
  1017.3 15.5 %collective-permute-start.4 = (f32[3,256]{1,0:T(4,128)S(1)}, f32[3,256]{1,0:T(4,128)S(1)}, u32[]{:S(2)}, u32[]{:S(2)}) collective-permute-start(f32[3,256]{1,0:T(4,128)S(1)} %get-tuple-element.413), channel_id=1, source_target_pairs={{4,0},{8,4},{12,8},{16,12},{20,16},{24,20},{28,24},{0,28},{5,1},{9... | collective-permute-start | bytes 9224 | tf_op jit(solution)/shard_map/ppermute | solution.py:22
  1021.4 11.4 %collective-permute-start.5 = (f32[3,256]{1,0:T(4,128)S(1)}, f32[3,256]{1,0:T(4,128)S(1)}, u32[]{:S(2)}, u32[]{:S(2)}) collective-permute-start(f32[3,256]{1,0:T(4,128)S(1)} %get-tuple-element.414), channel_id=1, source_target_pairs={{28,0},{0,4},{4,8},{8,12},{12,16},{16,20},{20,24},{24,28},{29,1},{... | collective-permute-start | bytes 9224 | tf_op jit(solution)/shard_map/ppermute | solution.py:22
Sparse Core Ops, SparseCore 0:
  337.3 757.9 all-reduce.3
Sparse Core Ops, SparseCore 1:
  1017.3 23.0 reduce-scatter.1
where the time goes:
time: 1120 us; the launch traced here: 1110 us
  blocking collectives  699 us (62%)
  loops' own time  202 us (18%)
  waiting for transfers between devices  61.3 us (5%)
  matrix products  39.8 us (4%)
  other arithmetic  37 us (3%)
  local copies, waits for them, and re-layouts  34.1 us (3%)
  between operations  17.7 us (2%)
  starting transfers between devices  15 us (1%)
    psum x1, blocking collectives, local(): lax.psum((acc_weights[0], acc_weights[1], acc_weights[2], acc_weights[3],...  677 us
    another operation x1, loops' own time, local(): lax.fori_loop(0, tile_counts[0, 0], visit_listed, initial)  202 us
    psum x1, waiting for transfers between devices, local(): lax.psum((acc_weights[0], acc_weights[1], acc_weights[2], acc_weights[3],...  61.2 us
  transfers between devices with their start and end apart: 8, of which 1 were waited for; matrix products, arithmetic and copies ran while one was open for 0% of the time, Pallas kernels for 0%

commit v1 on v0

v1 whole, which is shorter than its diff:
```python
import functools
import math

import jax
import jax.numpy as jnp
from jax import lax
from jax.experimental import pallas as pl
from jax.experimental.pallas import tpu as pltpu
from jax.sharding import PartitionSpec as P

TILE = 32
LANES = 128

box_side = 1.0
brick_height = 1.0
cutoff_radius = 3.0
soften = 0.01
sharpness = 10.0

F32 = jnp.float32
BF16 = jnp.bfloat16


def up(value, unit):
    return -(-value // unit) * unit


def iota(shape, axis):
    return lax.broadcasted_iota(jnp.int32, shape, axis)


def one_hot(cond):
    return jnp.where(cond, 1.0, 0.0).astype(BF16)


def nn(left, right):
    return lax.dot_general(left, right, (((1,), (0,)), ((), ())), preferred_element_type=F32)


def nt(left, right):
    return lax.dot_general(left, right, (((1,), (1,)), ((), ())), preferred_element_type=F32)


def split(value, parts):
    pieces = []
    for _ in range(parts):
        piece = value.astype(BF16)
        pieces.append(piece)
        value = value - piece.astype(F32)
    return pieces


def nn_split(left, right):
    pieces = split(left, 2)
    return nn(pieces[0], right) + nn(pieces[1], right)


def poly(square, coefs):
    total = jnp.full_like(square, coefs[-1])
    for coef in coefs[-2::-1]:
        total = total * square + coef
    return total


SIN = [(-1.0) ** n / math.factorial(2 * n + 1) for n in range(7)]
COS = [(-1.0) ** n / math.factorial(2 * n) for n in range(8)]


def pack_kernel(count_ref, feat_ref, adj_ref, pos_ref, out_feat, out_adj):
    atoms, width = feat_ref.shape[1:]
    live = iota((atoms, width), 0) < count_ref[0, 0]
    rows = atoms // LANES
    extra = out_feat.shape[0] - atoms
    parts = [
        pos_ref[axis, :, r * LANES : (r + 1) * LANES] for axis in range(3) for r in range(rows)
    ]
    parts.append(jnp.zeros((extra - len(parts), width), BF16))
    tail = jnp.concatenate([part.astype(F32) for part in parts], axis=0).astype(BF16)
    for source, target in ((feat_ref, out_feat), (adj_ref, out_adj)):
        kept = jnp.where(live, source[0].astype(F32), 0.0)
        target[:atoms] = kept.astype(BF16)
        target[atoms:] = tail


def tile_kernel(
    plate_count,
    where_ref,
    count_ref,
    tower_ref,
    plate_ref,
    shift_ref,
    *refs,
):
    (own_adj, near_adj, far_adj), refs = refs[:3], refs[3:]
    feats, refs = refs[:plate_count], refs[plate_count:]
    (w_rbf_ref, b_rbf_ref, w_filter_ref, b_filter_ref), refs = refs[:4], refs[4:]
    (keep_out, send_out, weight_out, near_out, far_out), refs = refs[:5], refs[5:]
    (
        adj_wide,
        adj_full,
        feat_wide,
        recv_wide,
        send_wide,
        grad_feat,
        grad_recv,
        grad_send,
        acc_wf,
        acc_wr,
        lhs_x,
        lhs_f,
        lhs_a,
        lhs_d,
    ), refs = refs[:14], refs[14:]
    slots = (refs[: len(refs) // 2], refs[len(refs) // 2 :])
    width = w_filter_ref.shape[0]
    nbasis = w_rbf_ref.shape[0]
    block_rows = own_adj.shape[0]
    groups = LANES // TILE
    chunks = TILE // groups
    pairs = TILE * TILE
    per_brick = adj_wide.shape[0] // 3
    atoms = per_brick * TILE
    rows = atoms // LANES
    spots = 3 * rows
    tower_at = where_ref[0]
    plate_at = where_ref[1]
    odd = lax.rem(tower_at, 2)
    near_slot = 2 - 2 * odd
    far_slot = 2 * odd
    sources = ((far_adj, far_slot), (own_adj, 1), (near_adj, near_slot))

    pick_recv = one_hot(iota((TILE, pairs), 0) == iota((TILE, pairs), 1) // TILE)
    pick_send = one_hot(iota((TILE, LANES), 0) == iota((TILE, LANES), 1) % TILE)
    for source, slot in sources:

        def widen_adj(half, carry, source=source, slot=slot):
            for t in (2 * half, 2 * half + 1):
                start = pl.multiple_of(t * TILE, TILE)
                part = source[pl.ds(start, TILE), :].astype(F32).T.astype(BF16)
                wide = nn(part, pick_recv)
                adj_full[slot * per_brick + t] = wide
                adj_wide[slot * per_brick + t] = wide.astype(BF16)
            return carry

        lax.fori_loop(0, per_brick // 2, widen_adj, 0)
    for q in range(groups):
        pick = one_hot(iota((LANES, pairs), 0) == q * TILE + iota((LANES, pairs), 1) // TILE)
        for source, slot in sources:
            wide = nn(source[atoms:block_rows], pick)
            for c in range(chunks):
                recv_wide[slot, q, :, c, :] = wide[:spots, c * LANES : (c + 1) * LANES]
    for q in range(groups):
        pick = one_hot(iota((LANES, LANES), 0) == q * TILE + iota((LANES, LANES), 1) % TILE)
        for step, source in enumerate(feats):
            send_wide[plate_at ^ step, q] = nn(source[atoms:block_rows], pick)
    for step, source in enumerate(feats):
        brick = plate_at ^ step

        def widen_feat(half, carry, source=source, brick=brick):
            for t in range(4):
                t = 4 * half + t
                start = pl.multiple_of(t * TILE, TILE)
                part = source[pl.ds(start, TILE), :].astype(F32).T.astype(BF16)
                feat_wide[brick * per_brick + t] = nn(part, pick_send).astype(BF16)
            return carry

        lax.fori_loop(0, per_brick // 4, widen_feat, 0)

    w_rbf = w_rbf_ref[...].astype(F32)
    half_bias = [piece.astype(F32) for piece in split(0.5 * b_rbf_ref[...], 3)]
    stacked = jnp.concatenate(
        [0.5 * w_rbf] + half_bias + [jnp.zeros((LANES - nbasis - 3, width), F32)], axis=0
    )
    lhs_x[...] = stacked.T[:, : 2 * nbasis].astype(BF16)
    w_filter = w_filter_ref[...].astype(F32)
    bias = [piece.astype(F32) for piece in split(b_filter_ref[...], 3)]
    bias = jnp.concatenate(bias + [jnp.zeros((LANES - 3, width), F32)], axis=0)
    lhs_f[:, :width] = w_filter.T.astype(BF16)
    lhs_f[:, width:] = bias.T.astype(BF16)
    lhs_a[:width] = w_filter_ref[...]
    lhs_a[width:] = bias[:16].astype(BF16)
    lhs_d[:nbasis, :width] = w_rbf_ref[...]
    lhs_d[nbasis:, :width] = jnp.zeros((nbasis, width), BF16)
    lhs_d[:nbasis, width:] = jnp.zeros((nbasis, width), BF16)
    lhs_d[nbasis:, width:] = one_hot(iota((nbasis, width), 0) == 0)

    grad_feat[...] = jnp.zeros_like(grad_feat)
    grad_recv[...] = jnp.zeros_like(grad_recv)
    grad_send[...] = jnp.zeros_like(grad_send)
    acc_wf[...] = jnp.zeros_like(acc_wf)
    acc_wr[...] = jnp.zeros_like(acc_wr)

    count = count_ref[0, 0]
    span = 2 * LANES
    centres = iota((nbasis, span), 0).astype(F32) * (cutoff_radius / (nbasis - 1))
    ones_rows = jnp.ones((nbasis, span), BF16)

    def places(entry):
        entry = jnp.minimum(entry, count - 1)
        tower_tile = tower_ref[0, 0, entry]
        plate_tile = plate_ref[0, 0, entry]
        recv_t = tower_tile % per_brick
        send_t = plate_tile % per_brick
        recv = (tower_tile // per_brick, recv_t % groups, recv_t // groups)
        send = (plate_tile // per_brick, send_t % groups, send_t // groups)
        return tower_tile, plate_tile, recv, send, shift_ref[0, 0, entry]

    def start_tile(entry, slot):
        stack_ref, soft_ref, gate_ref, basis_ref, slant_ref, geo_ref, _ = slot
        _, _, recv_at, send_at, code = places(entry)
        shifts = (
            (code // 3 - 1).astype(F32) * box_side,
            (code % 3 - 1).astype(F32) * box_side,
            (recv_at[0] - 1).astype(F32) * brick_height,
        )
        square = soften
        for axis in range(3):
            recv = recv_wide[recv_at[0], recv_at[1], axis * rows + recv_at[2]]
            send = send_wide[send_at[0], send_at[1], pl.ds(axis * rows + send_at[2], 1), :]
            disp = recv + shifts[axis] - send
            geo_ref[axis] = disp
            square = square + disp * disp
        dist = jnp.sqrt(square)
        reach = jnp.where(entry < count, cutoff_radius, 0.0)
        inside = dist < reach
        angle = (0.5 * math.pi / cutoff_radius) * (cutoff_radius - dist)
        square = angle * angle
        sine = angle * poly(square, SIN)
        cosine = poly(square, COS)
        envelope = jnp.where(inside, sine * sine, 0.0)
        geo_ref[3] = jnp.where(inside, (-math.pi / cutoff_radius) * sine * cosine, 0.0)
        geo_ref[4] = 1.0 / dist

        def chunk(c):
            def row(value):
                return jnp.concatenate([value[c : c + 1], value[c + 1 : c + 2]], axis=1)

            at = slice(c * LANES, c * LANES + span)
            offsets = row(dist) - centres
            basis = jnp.exp(-sharpness * offsets * offsets)
            basis_b = jnp.concatenate([basis.astype(BF16), ones_rows], axis=0)
            basis_ref[:, at] = basis_b
            slant_ref[:, at] = (-2.0 * sharpness) * basis * offsets
            tanh = jnp.tanh(nn(lhs_x[...], basis_b))
            neg_soft = jnp.log(1.0 - tanh).astype(BF16)
            env = row(envelope)
            env16 = jnp.broadcast_to(env, (16, span))
            soft_ref[:, at] = neg_soft
            gate_ref[:, at] = (tanh + 1.0) * (0.5 * env)
            stack_ref[:width, at] = (
                neg_soft.reshape(-1, 16, span) * (-env16).astype(BF16)[None]
            ).reshape(width, span)
            stack_ref[width:, at] = env16.astype(BF16)

        return chunk

    def finish_tile(entry, slot):
        stack_ref, soft_ref, gate_ref, basis_ref, slant_ref, geo_ref, pull_ref = slot
        tower_tile, plate_tile, recv_at, send_at, _ = places(entry)
        sums = []

        def chunk(c):
            at = slice(c * LANES, c * LANES + span)
            feat = feat_wide[plate_tile]
            pair = adj_wide[tower_tile, :, at] * jnp.concatenate([feat, feat], axis=1)
            stack = stack_ref[:, at]
            filt = nn(lhs_f[:, : width + 16], stack)
            back = nn(lhs_a[...], pair)
            part_wf = nt(stack, pair)
            prod = filt * adj_full[tower_tile, :, at]
            prod = prod[:, :LANES] + prod[:, LANES:]
            d_pre = (back[:width] * gate_ref[:, at]).astype(BF16)
            both = jnp.concatenate([d_pre, soft_ref[:, at] * back[:width].astype(BF16)], axis=0)
            part_wr = nt(basis_ref[:, at], d_pre)
            d_basis = nn(lhs_d[...], both)
            direct = jnp.sum(d_basis[:nbasis] * slant_ref[:, at], axis=0, keepdims=True)
            inner = jnp.sum(back[width : width + 8], axis=0, keepdims=True)
            inner = inner - d_basis[nbasis : nbasis + 1]
            pull_ref[c : c + 1, :] = direct[:, :LANES] + geo_ref[3, c : c + 1] * inner[:, :LANES]
            pull_ref[c + 1 : c + 2, :] = (
                direct[:, LANES:] + geo_ref[3, c + 1 : c + 2] * inner[:, LANES:]
            )
            parts = [prod, part_wf, part_wr]
            sums[:] = [a + b for a, b in zip(sums, parts)] if sums else parts

        def end():
            radial = pull_ref[...] * geo_ref[4]
            for axis in range(3):
                pull = geo_ref[axis] * radial
                grad_recv[recv_at[0], recv_at[1], axis * rows + recv_at[2]] += pull
                grad_send[send_at[0], send_at[1], axis * rows + send_at[2]] += pull
            grad_feat[plate_tile] += sums[0]
            acc_wf[...] += sums[1]
            acc_wr[...] += sums[2]

        return chunk, end

    first = start_tile(0, slots[0])
    for c in range(0, chunks, 2):
        first(c)

    def visit(step, carry):
        for n in range(2):
            entry = 2 * step + n
            ahead = start_tile(entry + 1, slots[1 - n])
            chunk, end = finish_tile(entry, slots[n])
            for c in range(0, chunks, 2):
                ahead(c)
                chunk(c)
            end()
        return carry

    lax.fori_loop(0, (count + 1) // 2, visit, 0)

    digit = iota((1, width), 1)
    count_row = jnp.where(digit == 0, lax.rem(count, 16), 0)
    count_row = jnp.where(digit == 1, count // 16, count_row).astype(F32)
    weights = jnp.concatenate(
        [
            acc_wf[:width],
            acc_wr[:nbasis],
            acc_wf[width : width + 1],
            acc_wr[nbasis : nbasis + 1],
            count_row,
            jnp.zeros((weight_out.shape[0] - width - nbasis - 3, width), F32),
        ],
        axis=0,
    )
    weight_out[...] = weights
    put_split(send_out, weights)

    fold = one_hot(iota((TILE, LANES), 0) == iota((TILE, LANES), 1) % TILE)
    same_slot = one_hot(iota((LANES, LANES), 0) % TILE == iota((LANES, LANES), 1) % TILE)
    same_group = one_hot(iota((LANES, LANES), 0) // TILE == iota((LANES, LANES), 1) % groups)
    group_of = iota((spots, LANES), 1) // TILE
    padding = jnp.zeros((block_rows - atoms - spots, LANES), F32)
    for step in range(plate_count):
        brick = plate_at ^ step
        at = step // 2 * block_rows
        target = send_out if step % 2 else keep_out
        kind = target.dtype

        def fold_feat(half, carry, brick=brick, at=at, target=target, kind=kind):
            for t in range(4):
                t = 4 * half + t
                pieces = split(grad_feat[brick * per_brick + t], 2)
                start = pl.multiple_of(at + t * TILE, 16)
                target[pl.ds(start, TILE), :] = (
                    nt(fold, pieces[0]) + nt(fold, pieces[1])
                ).astype(kind)
            return carry

        lax.fori_loop(0, per_brick // 4, fold_feat, 0)
        total = jnp.zeros((spots, LANES), F32)
        for q in range(groups):
            summed = nn_split(jnp.sum(grad_send[brick, q], axis=1), same_slot)
            total = jnp.where(group_of == q, -summed, total)
        total = jnp.concatenate([total, padding], axis=0)
        target[at + atoms : at + block_rows] = total.astype(kind)
    lane = iota((chunks, LANES), 1)
    own_chunk = (lane // groups) % chunks == iota((chunks, LANES), 0)
    for target, slot in ((far_out, far_slot), (None, 1), (near_out, near_slot)):
        total = jnp.zeros((spots, chunks, LANES), F32)
        for q in range(groups):
            summed = nn_split(grad_recv[slot, q].reshape(spots * chunks, LANES), same_group)
            chosen = own_chunk & (lane // TILE == q)
            total = total + jnp.where(chosen[None], summed.reshape(spots, chunks, LANES), 0.0)
        total = jnp.concatenate([jnp.sum(total, axis=1), padding], axis=0)
        if target is None:
            keep_out[atoms:block_rows] += total
        else:
            target[...] = total


def put_split(target, weights):
    count = weights.shape[0]
    end = target.shape[0]
    high, low = split(weights, 2)
    target[end - 2 * count : end - count] = high
    target[end - count :] = low


def add_kernel(cut, kept_ref, weight_ref, got_ref, kept_out, *outs):
    held, count = kept_ref.shape[0], weight_ref.shape[0]
    got = got_ref[...].astype(F32)
    total = kept_ref[...] + got[:held]
    weights = weight_ref[...] + got[held : held + count] + got[held + count :]
    kept_out[...] = total[:cut]
    outs[-1][...] = weights
    if len(outs) == 2:
        outs[0][: held - cut] = total[cut:].astype(BF16)
        put_split(outs[0], weights)


def finish_kernel(atoms, count_ref, block_ref, near_ref, far_ref, feat_out, pos_out):
    width = block_ref.shape[1]
    live = iota((atoms, width), 0) < count_ref[0, 0]
    feat_out[0] = jnp.where(live, block_ref[:atoms], 0.0)
    spots = block_ref[atoms:] + near_ref[...] + far_ref[...]
    rows = atoms // LANES
    for axis in range(3):
        for r in range(rows):
            at = axis * rows + r
            pos_out[axis, :, r * LANES : (r + 1) * LANES] = spots[at : at + 1]


def weight_kernel(*refs):
    ins, outs = refs[:-4], refs[-4:]
    total = ins[0][...]
    for other in ins[1:]:
        total = total + other[...]
    nbasis, width = outs[0].shape
    row = total[width + nbasis + 2 : width + nbasis + 3]
    tiles = row[:, :1] + 16.0 * row[:, 1:2]
    scale = lax.rsqrt(tiles * (TILE * TILE))
    outs[0][...] = total[width : width + nbasis] * scale
    outs[1][...] = total[width + nbasis + 1 : width + nbasis + 2] * scale
    outs[2][...] = total[:width] * scale
    outs[3][...] = total[width + nbasis : width + nbasis + 1] * scale


def swap(value, axis, route):
    size = lax.axis_size(axis)
    return lax.ppermute(value, axis, [(i, route(i) % size) for i in range(size)])


def across(bits):
    return lambda i: i ^ bits


def beyond(i):
    return i + 1 if i % 2 else i - 1


VMEM = pl.BlockSpec(memory_space=pltpu.VMEM)
SMEM = pl.BlockSpec(memory_space=pltpu.SMEM)


def call(kernel, name, shapes, places, **extra):
    return pl.pallas_call(
        kernel,
        name=name,
        out_shape=[jax.ShapeDtypeStruct(shape, kind) for shape, kind in shapes],
        in_specs=places,
        out_specs=[VMEM] * len(shapes),
        **extra,
    )


def local(
    features,
    adjoint,
    positions,
    w_rbf,
    b_rbf,
    w_filter,
    b_filter,
    atom_counts,
    tile_counts,
    tower_tiles,
    plate_tiles,
    image_shifts,
):
    atoms, width = features.shape[1:]
    nbasis = w_rbf.shape[0]
    per_brick = atoms // TILE
    groups = LANES // TILE
    chunks = TILE // groups
    plate_count = lax.axis_size("plate")
    tower_count = lax.axis_size("tower")
    if plate_count & (plate_count - 1) or tower_count & (tower_count - 1):
        raise ValueError("axis sizes")
    pairs = TILE * TILE
    spots = 3 * (atoms // LANES)
    spot_rows = up(spots, 16)
    block = atoms + spot_rows
    weight_rows = up(width + nbasis + 3, 16)

    feat_block, adj_block = call(
        pack_kernel,
        "pack",
        [((block, width), BF16)] * 2,
        [SMEM, VMEM, VMEM, VMEM],
    )(atom_counts, features, adjoint, positions)
    peers = [swap(feat_block, "plate", across(step)) for step in range(1, plate_count)]
    near_adj = swap(adj_block, "tower", across(1))
    far_adj = swap(adj_block, "tower", beyond)

    at = jnp.stack([lax.axis_index("tower"), lax.axis_index("plate")]).astype(jnp.int32)
    half = plate_count // 2
    keep, send, weights, near_pos, far_pos = call(
        functools.partial(tile_kernel, plate_count),
        "tiles",
        [
            ((half * block, width), F32),
            ((half * block + 2 * weight_rows, width), BF16),
            ((weight_rows, width), F32),
            ((spot_rows, width), F32),
            ((spot_rows, width), F32),
        ],
        [SMEM] * 5 + [VMEM] * (3 + plate_count + 4),
        scratch_shapes=[
            pltpu.VMEM((3 * per_brick, width, pairs), BF16),
            pltpu.VMEM((3 * per_brick, width, pairs), F32),
            pltpu.VMEM((plate_count * per_brick, width, LANES), BF16),
            pltpu.VMEM((3, groups, spots, chunks, LANES), F32),
            pltpu.VMEM((plate_count, groups, spot_rows, LANES), F32),
            pltpu.VMEM((plate_count * per_brick, width, LANES), F32),
            pltpu.VMEM((3, groups, spots, chunks, LANES), F32),
            pltpu.VMEM((plate_count, groups, spots, chunks, LANES), F32),
            pltpu.VMEM((width + 16, width), F32),
            pltpu.VMEM((2 * nbasis, width), F32),
            pltpu.VMEM((width, 2 * nbasis), BF16),
            pltpu.VMEM((width, 2 * width), BF16),
            pltpu.VMEM((width + 16, width), BF16),
            pltpu.VMEM((2 * nbasis, 2 * width), BF16),
        ]
        + [
            pltpu.VMEM((width + 16, pairs), BF16),
            pltpu.VMEM((width, pairs), BF16),
            pltpu.VMEM((width, pairs), F32),
            pltpu.VMEM((2 * nbasis, pairs), BF16),
            pltpu.VMEM((nbasis, pairs), F32),
            pltpu.VMEM((5, chunks, LANES), F32),
            pltpu.VMEM((chunks, LANES), F32),
        ]
        * 2,
    )(
        at,
        tile_counts,
        tower_tiles,
        plate_tiles,
        image_shifts,
        adj_block,
        near_adj,
        far_adj,
        feat_block,
        *peers,
        w_rbf,
        b_rbf[None],
        w_filter,
        b_filter[None],
    )

    got_near, got_far = None, None
    for step in [1] + [1 << n for n in reversed(range(1, plate_count.bit_length() - 1))]:
        got = swap(send, "plate", across(step))
        if got_near is None:
            got_near = swap(near_pos, "tower", across(1))
            got_far = swap(far_pos, "tower", beyond)
        held = keep.shape[0]
        cut = max(held // 2, block)
        shapes = [((cut, width), F32)]
        if held > cut:
            shapes.append(((held - cut + 2 * weight_rows, width), BF16))
        shapes.append(((weight_rows, width), F32))
        keep, *rest = call(functools.partial(add_kernel, cut), "add", shapes, [VMEM] * 3)(
            keep, weights, got
        )
        weights = rest[-1]
        send = rest[0]
    grad_features, grad_positions = call(
        functools.partial(finish_kernel, atoms),
        "finish",
        [((1, atoms, width), F32), ((3, 1, atoms), F32)],
        [SMEM, VMEM, VMEM, VMEM],
    )(atom_counts, keep, got_near, got_far)

    weights = weights + swap(weights, "tower", across(1))
    bits = 2
    parts = [weights]
    while bits < tower_count:
        weights = sum(parts[1:], parts[0])
        stride = [s * bits for s in (1, 2, 3) if s * bits < tower_count]
        parts = [weights] + [swap(weights, "tower", across(s)) for s in stride]
        bits *= 4
    out_wr, out_br, out_wf, out_bf = call(
        weight_kernel,
        "weights",
        [((nbasis, width), F32), ((1, width), F32), ((width, width), F32), ((1, width), F32)],
        [VMEM] * len(parts),
    )(*parts)
    return grad_features, grad_positions, out_wr, out_br[0], out_wf, out_bf[0]


def solution(mesh):
    in_specs = (
        P("tower", "plate", None),
        P("tower", "plate", None),
        P(None, "tower", "plate"),
        P(),
        P(),
        P(),
        P(),
        P("tower", "plate"),
        P("tower", "plate"),
        P("tower", "plate", None),
        P("tower", "plate", None),
        P("tower", "plate", None),
    )
    out_specs = (P("tower", "plate", None), P(None, "tower", "plate"), P(), P(), P(), P())
    return jax.shard_map(local, mesh=mesh, in_specs=in_specs, out_specs=out_specs, check_vma=False)
```

time: 1120 us -> 122 us (0.11); the launches traced: 1110 us -> 121 us
  blocking collectives: 699 us -> 0 us
  loops' own time: 202 us -> 0 us
  Pallas kernels: 0 us -> 48.8 us
  waiting for transfers between devices: 61.3 us -> 18.8 us
  matrix products: 39.8 us -> 0 us
  other arithmetic: 37 us -> 1.49 us
  starting transfers between devices: 15 us -> 44.9 us
  local copies, waits for them, and re-layouts: 34.1 us -> 5.13 us
  between operations: 17.7 us -> 2.02 us
    psum x1 -> x0, blocking collectives: 677 us -> none  [local(): lax.psum((acc_weights[0], acc_weights[1], acc_weights[2], acc_weights[3],...]
    another operation x1 -> x0, loops' own time: 202 us -> none  [local(): lax.fori_loop(0, tile_counts[0, 0], visit_listed, initial)]
    psum x1 -> x0, waiting for transfers between devices: 61.2 us -> none  [local(): lax.psum((acc_weights[0], acc_weights[1], acc_weights[2], acc_weights[3],...]
    pallas_call x0 -> x6, Pallas kernels: none -> 48.8 us  [the longest x1 40.2 us: local(): call(functools.partial(tile_kernel, plate_count), 'tiles', [((half * bloc...]
    dot_general x108 -> x0, matrix products: 39.8 us -> none  [the longest x18 10.9 us: pair_tile(): jnp.dot(softed, w_filter, preferred_element_type=jnp.float32) + b_filter]
    ppermute x6 -> x13, starting transfers between devices: 14.9 us -> 44.9 us  [swap(): lax.ppermute(value, axis, [(i, route(i) % size) for i in range(size)])]
    dynamic_slice x36 -> x0, local copies, waits for them, and re-layouts: 21.1 us -> none  [the longest x18 10.6 us: visit_listed(): plate_tile = plate_tiles[0, 0, entry]]
    ppermute x6 -> x13, waiting for transfers between devices: 0.02 us -> 18.8 us  [swap(): lax.ppermute(value, axis, [(i, route(i) % size) for i in range(size)])]
  transfers between devices with their start and end apart: 8 -> 13, of which waited for: 1 -> 8; matrix products, arithmetic and copies ran while one was open for 0% -> 0% of each run, Pallas kernels for 0% -> 1%
where the time goes in v1:
time: 122 us; the launch traced here: 121 us
  Pallas kernels  48.8 us (40%)
  starting transfers between devices  44.9 us (37%)
  waiting for transfers between devices  18.8 us (15%)
  local copies, waits for them, and re-layouts  5.13 us (4%)
  between operations  2.02 us (2%)
  other arithmetic  1.49 us (1%)
    ppermute x13, starting transfers between devices, swap(): lax.ppermute(value, axis, [(i, route(i) % size) for i in range(size)])  44.9 us
    pallas_call x1, Pallas kernels, local(): call(functools.partial(tile_kernel, plate_count), 'tiles', [((half * bloc...  40.2 us
    ppermute x13, waiting for transfers between devices, swap(): lax.ppermute(value, axis, [(i, route(i) % size) for i in range(size)])  18.8 us
    unnamed x31, local copies, waits for them, and re-layouts  5.13 us
    pallas_call x2, Pallas kernels, local(): call(functools.partial(add_kernel, cut), 'add', shapes, [VMEM] * 3)  3.57 us
  transfers between devices with their start and end apart: 13, of which 8 were waited for; matrix products, arithmetic and copies ran while one was open for 0% of the time, Pallas kernels for 1%

profile of v1, /device:TPU:0, one launch (start us, length us, event | category | flops | bytes accessed | tf_op | source)
XLA Modules:
  0.0 121.1 jit_solution(2089789566735065783)
XLA Ops:
  1.3 1.3 %copy.18.pos_ref = bf16[3,1,256]{2,1,0:T(2,128)(2,1)} copy(bf16[3,1,256]{2,0,1:T(4,128)(2,1)} %param.14) | data formatting | bytes 3072 | tf_op args[2]
  2.5 1.6 %pack.1 = (bf16[272,128]{1,0:T(8,128)(2,1)}, bf16[272,128]{1,0:T(8,128)(2,1)}) custom-call(s32[1,1]{1,0:T(1,128)S(6)} %copy.19.count_ref, bf16[1,256,128]{2,1,0:T(8,128)(2,1)} %feat_ref.1, bf16[1,256,128]{2,1,0:T(8,128)(2,1)} %adj_ref.1, bf16[3,1,256]{2,1,0:T(2,128)(2,1)} %copy.18.pos_ref), custom_call_target="tpu_custom_call" | custom-call | tf_op jit(solution)/shard_map/pack/pallas_call | solution.py:479
  4.1 6.0 %collective-permute-start.1 = (bf16[272,128]{1,0:T(8,128)(2,1)}, bf16[272,128]{1,0:T(8,128)(2,1)S(1)}, u32[]{:S(2)}, u32[]{:S(2)}) collective-permute-start(bf16[272,128]{1,0:T(8,128)(2,1)} %get-tuple-element.24.refs_0_), channel_id=1, source_target_pairs={{0,28},{4,8},{8,4},{12,16},{16,12},{20,24},{24,20},{28,0},{1,29},{... | collective-permute-start | bytes 208904 | tf_op jit(solution)/shard_map/ppermute | solution.py:424
  10.1 0.0 collective-permute-start
  10.1 0.7 collective-permute-start.4
  10.8 0.8 collective-permute-start.3
  11.6 0.3 collective-permute-start.2
  12.6 0.6 pad_add_fusion.where_ref
  13.2 0.0 collective-permute-done.1.refs_2_
  13.2 0.0 copy-start.6
  13.2 1.4 %collective-permute-done.refs_1_ = bf16[272,128]{1,0:T(8,128)(2,1)S(1)} collective-permute-done((bf16[272,128]{1,0:T(8,128)(2,1)}, bf16[272,128]{1,0:T(8,128)(2,1)S(1)}, u32[]{:S(2)}, u32[]{:S(2)}) %collective-permute-start) | collective-permute-done | bytes 69664 | tf_op jit(solution)/shard_map/ppermute | solution.py:424
  14.6 0.0 copy-start.7
  14.6 0.1 collective-permute-done.4.refs_6_
  14.7 0.0 copy-start.8
  14.7 1.6 %collective-permute-done.3.refs_5_ = bf16[272,128]{1,0:T(8,128)(2,1)S(1)} collective-permute-done((bf16[272,128]{1,0:T(8,128)(2,1)}, bf16[272,128]{1,0:T(8,128)(2,1)S(1)}, u32[]{:S(2)}, u32[]{:S(2)}) %collective-permute-start.3) | collective-permute-done | bytes 69664 | tf_op jit(solution)/shard_map/ppermute | solution.py:424
  16.3 0.0 copy-start.9
  16.3 0.0 collective-permute-done.2.refs_4_
  16.3 0.0 copy-start.10
  16.3 0.0 copy-done.6
  16.3 0.0 copy-done.7
  16.3 0.0 copy-done.8
  16.3 0.6 copy-done.9
  16.9 0.0 copy-done.10
  17.0 40.2 %tiles.1 = (f32[544,128]{1,0:T(8,128)}, bf16[864,128]{1,0:T(8,128)(2,1)}, f32[160,128]{1,0:T(8,128)}, f32[16,128]{1,0:T(8,128)}, f32[16,128]{1,0:T(8,128)}) custom-call(s32[2]{0:T(128)} %pad_add_fusion.where_ref, s32[1,1]{1,0:T(1,128)S(6)} %copy.20.count_ref, s32[1,1,56]{2,1,0:T(1,128)} %tower_ref.1, s32[1,1,56]{2,1,0:T(1,128)} %plate_ref.1, ...), custom_call_target="tpu_custom_call" | custom-call | tf_op jit(solution)/shard_map/tiles/pallas_call | solution.py:491
  57.2 0.1 collective-permute-start.5
  57.3 1.7 %collective-permute-done.5.got_ref = bf16[864,128]{1,0:T(8,128)(2,1)S(1)} collective-permute-done((bf16[864,128]{1,0:T(8,128)(2,1)}, bf16[864,128]{1,0:T(8,128)(2,1)S(1)}, u32[]{:S(2)}, u32[]{:S(2)}) %collective-permute-start.5) | collective-permute-done | bytes 221216 | tf_op jit(solution)/shard_map/ppermute | solution.py:424
  59.0 0.0 copy-start.1
  59.0 0.7 copy-done.1
  59.7 1.9 %add.8 = (f32[272,128]{1,0:T(8,128)}, bf16[592,128]{1,0:T(8,128)(2,1)}, f32[160,128]{1,0:T(8,128)}) custom-call(f32[544,128]{1,0:T(8,128)} %get-tuple-element.26.kept_ref, f32[160,128]{1,0:T(8,128)} %get-tuple-element.27.weight_ref, bf16[864,128]{1,0:T(8,128)(2,1)} %copy-done.1), custom_call_target="tpu_custom_call" | custom-call | tf_op jit(solution)/shard_map/add/pallas_call | solution.py:557
  61.5 1.0 collective-permute-start.6
  62.5 5.2 %collective-permute-done.6.got_ref = bf16[592,128]{1,0:T(8,128)(2,1)S(1)} collective-permute-done((bf16[592,128]{1,0:T(8,128)(2,1)}, bf16[592,128]{1,0:T(8,128)(2,1)S(1)}, u32[]{:S(2)}, u32[]{:S(2)}) %collective-permute-start.6) | collective-permute-done | bytes 151584 | tf_op jit(solution)/shard_map/ppermute | solution.py:424
  67.7 0.7 copy-done.2
  68.4 1.7 %add.9 = (f32[272,128]{1,0:T(8,128)}, f32[160,128]{1,0:T(8,128)}) custom-call(f32[272,128]{1,0:T(8,128)} %get-tuple-element.29.kept_ref, f32[160,128]{1,0:T(8,128)} %get-tuple-element.30.weight_ref, bf16[592,128]{1,0:T(8,128)(2,1)} %copy-done.2), custom_call_target="tpu_custom_call" | custom-call | tf_op jit(solution)/shard_map/add/pallas_call | solution.py:557
  70.1 0.0 copy-start.14
  70.1 0.0 copy-start.13
  70.1 29.4 %collective-permute-start.9 = (f32[160,128]{1,0:T(8,128)}, f32[160,128]{1,0:T(8,128)S(1)}, u32[]{:S(2)}, u32[]{:S(2)}) collective-permute-start(f32[160,128]{1,0:T(8,128)} %get-tuple-element.37), channel_id=1, source_target_pairs={{0,4},{4,0},{8,12},{12,8},{16,20},{20,16},{24,28},{28,24},{1,5},{5... | collective-permute-start | bytes 245768 | tf_op jit(solution)/shard_map/ppermute | solution.py:424
  99.4 2.6 %collective-permute-done.9 = f32[160,128]{1,0:T(8,128)S(1)} collective-permute-done((f32[160,128]{1,0:T(8,128)}, f32[160,128]{1,0:T(8,128)S(1)}, u32[]{:S(2)}, u32[]{:S(2)}) %collective-permute-start.9) | collective-permute-done | bytes 81952 | tf_op jit(solution)/shard_map/ppermute | solution.py:424
  102.1 0.9 add.5.refs_0_
  103.0 0.0 copy-start
  103.0 0.8 collective-permute-start.12
  103.7 1.5 %collective-permute-start.11 = (f32[160,128]{1,0:T(8,128)S(1)}, f32[160,128]{1,0:T(8,128)S(1)}, u32[]{:S(2)}, u32[]{:S(2)}) collective-permute-start(f32[160,128]{1,0:T(8,128)S(1)} %add.5.refs_0_), channel_id=1, source_target_pairs={{0,16},{4,20},{8,24},{12,28},{16,0},{20,4},{24,8},{28,12},{1,17},{... | collective-permute-start | bytes 245768 | tf_op jit(solution)/shard_map/ppermute | solution.py:424
  105.2 2.2 %collective-permute-start.10 = (f32[160,128]{1,0:T(8,128)S(1)}, f32[160,128]{1,0:T(8,128)S(1)}, u32[]{:S(2)}, u32[]{:S(2)}) collective-permute-start(f32[160,128]{1,0:T(8,128)S(1)} %add.5.refs_0_), channel_id=1, source_target_pairs={{0,8},{4,12},{8,0},{12,4},{16,24},{20,28},{24,16},{28,20},{1,9},{5... | collective-permute-start | bytes 245768 | tf_op jit(solution)/shard_map/ppermute | solution.py:424
  107.4 0.0 copy-done.14
  107.4 2.0 %collective-permute-start.7 = (f32[16,128]{1,0:T(8,128)S(1)}, f32[16,128]{1,0:T(8,128)S(1)}, u32[]{:S(2)}, u32[]{:S(2)}) collective-permute-start(f32[16,128]{1,0:T(8,128)S(1)} %copy-done.14), channel_id=1, source_target_pairs={{0,4},{4,0},{8,12},{12,8},{16,20},{20,16},{24,28},{28,24},{1,5},{5... | collective-permute-start | bytes 24584 | tf_op jit(solution)/shard_map/ppermute | solution.py:424
  109.4 0.0 copy-done.13
  109.4 0.1 collective-permute-start.8
  109.6 1.5 %collective-permute-done.7.near_ref = f32[16,128]{1,0:T(8,128)S(1)} collective-permute-done((f32[16,128]{1,0:T(8,128)S(1)}, f32[16,128]{1,0:T(8,128)S(1)}, u32[]{:S(2)}, u32[]{:S(2)}) %collective-permute-start.7) | collective-permute-done | bytes 8224 | tf_op jit(solution)/shard_map/ppermute | solution.py:424
  111.1 0.0 copy-start.11
  111.1 4.7 %collective-permute-done.8.far_ref = f32[16,128]{1,0:T(8,128)S(1)} collective-permute-done((f32[16,128]{1,0:T(8,128)S(1)}, f32[16,128]{1,0:T(8,128)S(1)}, u32[]{:S(2)}, u32[]{:S(2)}) %collective-permute-start.8) | collective-permute-done | bytes 8224 | tf_op jit(solution)/shard_map/ppermute | solution.py:424
  115.8 0.0 copy-start.12
  115.8 0.0 copy-done.11
  115.8 0.6 copy-done.12
  116.4 1.6 %finish.1 = (f32[1,256,128]{2,1,0:T(8,128)}, f32[3,1,256]{2,1,0:T(1,128)}) custom-call(s32[1,1]{1,0:T(1,128)S(6)} %copy.19.count_ref, f32[272,128]{1,0:T(8,128)} %get-tuple-element.32.block_ref, f32[16,128]{1,0:T(8,128)} %copy-done.11, f32[16,128]{1,0:T(8,128)} %copy-done.12), custom_call_target="tpu_custom_call" | custom-call | tf_op jit(solution)/shard_map/finish/pallas_call | solution.py:562
  118.0 0.0 collective-permute-done.12.refs_3_
  118.0 0.0 copy-start.3
  118.0 0.0 collective-permute-done.11.refs_2_
  118.0 0.0 copy-start.4
  118.0 0.0 collective-permute-done.10.refs_1_
  118.0 0.0 copy-done
  118.0 0.6 copy-done.3
  118.6 0.0 copy-done.4
  118.7 0.0 copy-start.5
  118.7 0.6 copy-done.5
  119.3 1.8 %weights.1 = (f32[16,128]{1,0:T(8,128)}, f32[1,128]{1,0:T(1,128)}, f32[128,128]{1,0:T(8,128)}, f32[1,128]{1,0:T(1,128)}) custom-call(f32[160,128]{1,0:T(8,128)} %copy-done, f32[160,128]{1,0:T(8,128)} %copy-done.5, f32[160,128]{1,0:T(8,128)} %copy-done.4, f32[160,128]{1,0:T(8,128)} %copy-done.3), custom_call_target="tpu_custom_call" | custom-call | tf_op jit(solution)/shard_map/weights/pallas_call | solution.py:577
  (1 shorter events, 0.0 us)
Async XLA Ops:
  4.1 9.1 %collective-permute-start.1 = (bf16[272,128]{1,0:T(8,128)(2,1)}, bf16[272,128]{1,0:T(8,128)(2,1)S(1)}, u32[]{:S(2)}, u32[]{:S(2)}) collective-permute-start(bf16[272,128]{1,0:T(8,128)(2,1)} %get-tuple-element.24.refs_0_), channel_id=1, source_target_pairs={{0,28},{4,8},{8,4},{12,16},{16,12},{20,24},{24,20},{28,0},{1,29},{... | collective-permute-start | bytes 208904 | tf_op jit(solution)/shard_map/ppermute | solution.py:424
  10.1 4.5 %collective-permute-start = (bf16[272,128]{1,0:T(8,128)(2,1)}, bf16[272,128]{1,0:T(8,128)(2,1)S(1)}, u32[]{:S(2)}, u32[]{:S(2)}) collective-permute-start(bf16[272,128]{1,0:T(8,128)(2,1)} %get-tuple-element.24.refs_0_), channel_id=1, source_target_pairs={{0,4},{4,0},{8,12},{12,8},{16,20},{20,16},{24,28},{28,24},{1,5},{5... | collective-permute-start | bytes 208904 | tf_op jit(solution)/shard_map/ppermute | solution.py:424
  10.1 4.6 %collective-permute-start.4 = (bf16[272,128]{1,0:T(8,128)(2,1)}, bf16[272,128]{1,0:T(8,128)(2,1)S(1)}, u32[]{:S(2)}, u32[]{:S(2)}) collective-permute-start(bf16[272,128]{1,0:T(8,128)(2,1)} %get-tuple-element.25.refs_3_), channel_id=1, source_target_pairs={{0,3},{1,2},{2,1},{3,0},{4,7},{5,6},{6,5},{7,4},{8,11},{9,10},{10,... | collective-permute-start | bytes 208904 | tf_op jit(solution)/shard_map/ppermute | solution.py:424
  10.8 5.5 %collective-permute-start.3 = (bf16[272,128]{1,0:T(8,128)(2,1)}, bf16[272,128]{1,0:T(8,128)(2,1)S(1)}, u32[]{:S(2)}, u32[]{:S(2)}) collective-permute-start(bf16[272,128]{1,0:T(8,128)(2,1)} %get-tuple-element.25.refs_3_), channel_id=1, source_target_pairs={{0,2},{1,3},{2,0},{3,1},{4,6},{5,7},{6,4},{7,5},{8,10},{9,11},{10,... | collective-permute-start | bytes 208904 | tf_op jit(solution)/shard_map/ppermute | solution.py:424
  11.6 4.7 %collective-permute-start.2 = (bf16[272,128]{1,0:T(8,128)(2,1)}, bf16[272,128]{1,0:T(8,128)(2,1)S(1)}, u32[]{:S(2)}, u32[]{:S(2)}) collective-permute-start(bf16[272,128]{1,0:T(8,128)(2,1)} %get-tuple-element.25.refs_3_), channel_id=1, source_target_pairs={{0,1},{1,0},{2,3},{3,2},{4,5},{5,4},{6,7},{7,6},{8,9},{9,8},{10,11... | collective-permute-start | bytes 208904 | tf_op jit(solution)/shard_map/ppermute | solution.py:424
  13.2 3.1 %copy-start.6 = (bf16[272,128]{1,0:T(8,128)(2,1)}, bf16[272,128]{1,0:T(8,128)(2,1)S(1)}, u32[]{:S(2)}) copy-start(bf16[272,128]{1,0:T(8,128)(2,1)S(1)} %collective-permute-done.1.refs_2_) | copy-start | bytes 208900
  14.6 1.7 %copy-start.7 = (bf16[272,128]{1,0:T(8,128)(2,1)}, bf16[272,128]{1,0:T(8,128)(2,1)S(1)}, u32[]{:S(2)}) copy-start(bf16[272,128]{1,0:T(8,128)(2,1)S(1)} %collective-permute-done.refs_1_) | copy-start | bytes 208900
  14.7 1.6 %copy-start.8 = (bf16[272,128]{1,0:T(8,128)(2,1)}, bf16[272,128]{1,0:T(8,128)(2,1)S(1)}, u32[]{:S(2)}) copy-start(bf16[272,128]{1,0:T(8,128)(2,1)S(1)} %collective-permute-done.4.refs_6_) | copy-start | bytes 208900
  16.3 0.6 copy-start.9
  16.3 0.7 copy-start.10
  57.2 1.7 %collective-permute-start.5 = (bf16[864,128]{1,0:T(8,128)(2,1)}, bf16[864,128]{1,0:T(8,128)(2,1)S(1)}, u32[]{:S(2)}, u32[]{:S(2)}) collective-permute-start(bf16[864,128]{1,0:T(8,128)(2,1)} %get-tuple-element.28), channel_id=1, source_target_pairs={{0,1},{1,0},{2,3},{3,2},{4,5},{5,4},{6,7},{7,6},{8,9},{9,8},{10,11... | collective-permute-start | bytes 663560 | tf_op jit(solution)/shard_map/ppermute | solution.py:424
  59.0 0.7 copy-start.1
  61.5 6.2 %collective-permute-start.6 = (bf16[592,128]{1,0:T(8,128)(2,1)}, bf16[592,128]{1,0:T(8,128)(2,1)S(1)}, u32[]{:S(2)}, u32[]{:S(2)}) collective-permute-start(bf16[592,128]{1,0:T(8,128)(2,1)} %get-tuple-element.31), channel_id=1, source_target_pairs={{0,2},{1,3},{2,0},{3,1},{4,6},{5,7},{6,4},{7,5},{8,10},{9,11},{10,... | collective-permute-start | bytes 454664 | tf_op jit(solution)/shard_map/ppermute | solution.py:424
  67.7 0.7 copy-start.2
  70.1 37.4 %copy-start.14 = (f32[16,128]{1,0:T(8,128)S(1)}, f32[16,128]{1,0:T(8,128)}, u32[]{:S(2)}) copy-start(f32[16,128]{1,0:T(8,128)} %get-tuple-element.33) | copy-start | bytes 24580
  70.1 39.4 %copy-start.13 = (f32[16,128]{1,0:T(8,128)S(1)}, f32[16,128]{1,0:T(8,128)}, u32[]{:S(2)}) copy-start(f32[16,128]{1,0:T(8,128)} %get-tuple-element.34) | copy-start | bytes 24580
  70.1 32.0 %collective-permute-start.9 = (f32[160,128]{1,0:T(8,128)}, f32[160,128]{1,0:T(8,128)S(1)}, u32[]{:S(2)}, u32[]{:S(2)}) collective-permute-start(f32[160,128]{1,0:T(8,128)} %get-tuple-element.37), channel_id=1, source_target_pairs={{0,4},{4,0},{8,12},{12,8},{16,20},{20,16},{24,28},{28,24},{1,5},{5... | collective-permute-start | bytes 245768 | tf_op jit(solution)/shard_map/ppermute | solution.py:424
  103.0 15.1 %copy-start = (f32[160,128]{1,0:T(8,128)}, f32[160,128]{1,0:T(8,128)S(1)}, u32[]{:S(2)}) copy-start(f32[160,128]{1,0:T(8,128)S(1)} %add.5.refs_0_) | copy-start | bytes 245764
  103.0 15.0 %collective-permute-start.12 = (f32[160,128]{1,0:T(8,128)S(1)}, f32[160,128]{1,0:T(8,128)S(1)}, u32[]{:S(2)}, u32[]{:S(2)}) collective-permute-start(f32[160,128]{1,0:T(8,128)S(1)} %add.5.refs_0_), channel_id=1, source_target_pairs={{0,24},{4,28},{8,16},{12,20},{16,8},{20,12},{24,0},{28,4},{1,25},{... | collective-permute-start | bytes 245768 | tf_op jit(solution)/shard_map/ppermute | solution.py:424
  103.7 14.3 %collective-permute-start.11 = (f32[160,128]{1,0:T(8,128)S(1)}, f32[160,128]{1,0:T(8,128)S(1)}, u32[]{:S(2)}, u32[]{:S(2)}) collective-permute-start(f32[160,128]{1,0:T(8,128)S(1)} %add.5.refs_0_), channel_id=1, source_target_pairs={{0,16},{4,20},{8,24},{12,28},{16,0},{20,4},{24,8},{28,12},{1,17},{... | collective-permute-start | bytes 245768 | tf_op jit(solution)/shard_map/ppermute | solution.py:424
  105.2 12.8 %collective-permute-start.10 = (f32[160,128]{1,0:T(8,128)S(1)}, f32[160,128]{1,0:T(8,128)S(1)}, u32[]{:S(2)}, u32[]{:S(2)}) collective-permute-start(f32[160,128]{1,0:T(8,128)S(1)} %add.5.refs_0_), channel_id=1, source_target_pairs={{0,8},{4,12},{8,0},{12,4},{16,24},{20,28},{24,16},{28,20},{1,9},{5... | collective-permute-start | bytes 245768 | tf_op jit(solution)/shard_map/ppermute | solution.py:424
  107.4 3.7 %collective-permute-start.7 = (f32[16,128]{1,0:T(8,128)S(1)}, f32[16,128]{1,0:T(8,128)S(1)}, u32[]{:S(2)}, u32[]{:S(2)}) collective-permute-start(f32[16,128]{1,0:T(8,128)S(1)} %copy-done.14), channel_id=1, source_target_pairs={{0,4},{4,0},{8,12},{12,8},{16,20},{20,16},{24,28},{28,24},{1,5},{5... | collective-permute-start | bytes 24584 | tf_op jit(solution)/shard_map/ppermute | solution.py:424
  109.4 6.3 %collective-permute-start.8 = (f32[16,128]{1,0:T(8,128)S(1)}, f32[16,128]{1,0:T(8,128)S(1)}, u32[]{:S(2)}, u32[]{:S(2)}) collective-permute-start(f32[16,128]{1,0:T(8,128)S(1)} %copy-done.13), channel_id=1, source_target_pairs={{0,28},{4,8},{8,4},{12,16},{16,12},{20,24},{24,20},{28,0},{1,29},{... | collective-permute-start | bytes 24584 | tf_op jit(solution)/shard_map/ppermute | solution.py:424
  111.1 4.7 %copy-start.11 = (f32[16,128]{1,0:T(8,128)}, f32[16,128]{1,0:T(8,128)S(1)}, u32[]{:S(2)}) copy-start(f32[16,128]{1,0:T(8,128)S(1)} %collective-permute-done.7.near_ref) | copy-start | bytes 24580
  115.8 0.6 copy-start.12
  118.0 0.6 copy-start.3
  118.0 0.7 copy-start.4
  118.7 0.6 copy-start.5

commit v2 on v1

--- a/solution.py
+++ b/solution.py
@@ -8,8 +8,10 @@
 from jax.experimental.pallas import tpu as pltpu
 from jax.sharding import PartitionSpec as P
 
+
 TILE = 32
 LANES = 128
+PART = 32
 
 box_side = 1.0
 brick_height = 1.0
@@ -74,8 +76,8 @@
     parts = [
         pos_ref[axis, :, r * LANES : (r + 1) * LANES] for axis in range(3) for r in range(rows)
     ]
-    parts.append(jnp.zeros((extra - len(parts), width), BF16))
-    tail = jnp.concatenate([part.astype(F32) for part in parts], axis=0).astype(BF16)
+    parts.append(jnp.zeros((extra - len(parts), width), F32))
+    tail = jnp.concatenate(parts, axis=0).astype(BF16)
     for source, target in ((feat_ref, out_feat), (adj_ref, out_adj)):
         kept = jnp.where(live, source[0].astype(F32), 0.0)
         target[:atoms] = kept.astype(BF16)
@@ -97,7 +99,6 @@
     (keep_out, send_out, weight_out, near_out, far_out), refs = refs[:5], refs[5:]
     (
         adj_wide,
-        adj_full,
         feat_wide,
         recv_wide,
         send_wide,
@@ -110,8 +111,10 @@
         lhs_f,
         lhs_a,
         lhs_d,
-    ), refs = refs[:14], refs[14:]
-    slots = (refs[: len(refs) // 2], refs[len(refs) // 2 :])
+    ), refs = refs[:13], refs[13:]
+    stack_buf, soft_buf, gate_buf, pair_buf, both_buf, refs = *refs[:5], refs[5:]
+    basis_buf, slant_buf, inner_buf, geo_buf, pull_buf, *refs = refs
+    half_buf, back_buf, filt_buf = refs
     width = w_filter_ref.shape[0]
     nbasis = w_rbf_ref.shape[0]
     block_rows = own_adj.shape[0]
@@ -138,8 +141,8 @@
                 start = pl.multiple_of(t * TILE, TILE)
                 part = source[pl.ds(start, TILE), :].astype(F32).T.astype(BF16)
                 wide = nn(part, pick_recv)
-                adj_full[slot * per_brick + t] = wide
-                adj_wide[slot * per_brick + t] = wide.astype(BF16)
+                for c in range(chunks):
+                    adj_wide[slot * per_brick + t, c] = wide[:, c * LANES : (c + 1) * LANES]
             return carry
 
         lax.fori_loop(0, per_brick // 2, widen_adj, 0)
@@ -161,7 +164,7 @@
                 t = 4 * half + t
                 start = pl.multiple_of(t * TILE, TILE)
                 part = source[pl.ds(start, TILE), :].astype(F32).T.astype(BF16)
-                feat_wide[brick * per_brick + t] = nn(part, pick_send).astype(BF16)
+                feat_wide[brick * per_brick + t] = nn(part, pick_send)
             return carry
 
         lax.fori_loop(0, per_brick // 4, widen_feat, 0)
@@ -175,14 +178,14 @@
     w_filter = w_filter_ref[...].astype(F32)
     bias = [piece.astype(F32) for piece in split(b_filter_ref[...], 3)]
     bias = jnp.concatenate(bias + [jnp.zeros((LANES - 3, width), F32)], axis=0)
-    lhs_f[:, :width] = w_filter.T.astype(BF16)
-    lhs_f[:, width:] = bias.T.astype(BF16)
+    lhs_f[0] = w_filter.T.astype(BF16)
+    lhs_f[1] = bias.T.astype(BF16)
     lhs_a[:width] = w_filter_ref[...]
     lhs_a[width:] = bias[:16].astype(BF16)
-    lhs_d[:nbasis, :width] = w_rbf_ref[...]
-    lhs_d[nbasis:, :width] = jnp.zeros((nbasis, width), BF16)
-    lhs_d[:nbasis, width:] = jnp.zeros((nbasis, width), BF16)
-    lhs_d[nbasis:, width:] = one_hot(iota((nbasis, width), 0) == 0)
+    lhs_d[0, :nbasis] = w_rbf_ref[...]
+    lhs_d[0, nbasis:] = jnp.zeros((nbasis, width), BF16)
+    lhs_d[1, :nbasis] = jnp.zeros((nbasis, width), BF16)
+    lhs_d[1, nbasis:] = one_hot(iota((nbasis, width), 0) == 0)
 
     grad_feat[...] = jnp.zeros_like(grad_feat)
     grad_recv[...] = jnp.zeros_like(grad_recv)
@@ -192,8 +195,8 @@
 
     count = count_ref[0, 0]
     span = 2 * LANES
-    centres = iota((nbasis, span), 0).astype(F32) * (cutoff_radius / (nbasis - 1))
-    ones_rows = jnp.ones((nbasis, span), BF16)
+    centres = iota((nbasis, LANES), 0).astype(F32) * (cutoff_radius / (nbasis - 1))
+    ones_rows = jnp.ones((nbasis, LANES), BF16)
 
     def places(entry):
         entry = jnp.minimum(entry, count - 1)
@@ -205,8 +208,16 @@
         send = (plate_tile // per_brick, send_t % groups, send_t // groups)
         return tower_tile, plate_tile, recv, send, shift_ref[0, 0, entry]
 
-    def start_tile(entry, slot):
-        stack_ref, soft_ref, gate_ref, basis_ref, slant_ref, geo_ref, _ = slot
+    per_tile = pairs // span
+    ring = 2 * per_tile
+
+    def blocks_of(at):
+        return (at % ring * 2, at % ring * 2 + 1)
+
+    def wide(ref, blocks, rows=slice(None)):
+        return jnp.concatenate([ref[n, rows] for n in blocks], axis=1)
+
+    def geometry(entry, tile):
         _, _, recv_at, send_at, code = places(entry)
         shifts = (
             (code // 3 - 1).astype(F32) * box_side,
@@ -218,99 +229,129 @@
             recv = recv_wide[recv_at[0], recv_at[1], axis * rows + recv_at[2]]
             send = send_wide[send_at[0], send_at[1], pl.ds(axis * rows + send_at[2], 1), :]
             disp = recv + shifts[axis] - send
-            geo_ref[axis] = disp
+            geo_buf[tile, axis] = disp
             square = square + disp * disp
         dist = jnp.sqrt(square)
-        reach = jnp.where(entry < count, cutoff_radius, 0.0)
-        inside = dist < reach
+        inside = dist < jnp.where(entry < count, cutoff_radius, 0.0)
         angle = (0.5 * math.pi / cutoff_radius) * (cutoff_radius - dist)
         square = angle * angle
         sine = angle * poly(square, SIN)
         cosine = poly(square, COS)
-        envelope = jnp.where(inside, sine * sine, 0.0)
-        geo_ref[3] = jnp.where(inside, (-math.pi / cutoff_radius) * sine * cosine, 0.0)
-        geo_ref[4] = 1.0 / dist
-
-        def chunk(c):
-            def row(value):
-                return jnp.concatenate([value[c : c + 1], value[c + 1 : c + 2]], axis=1)
-
-            at = slice(c * LANES, c * LANES + span)
-            offsets = row(dist) - centres
+        geo_buf[tile, 3] = jnp.where(inside, (-math.pi / cutoff_radius) * sine * cosine, 0.0)
+        geo_buf[tile, 4] = 1.0 / dist
+        geo_buf[tile, 5] = dist
+        geo_buf[tile, 6] = jnp.where(inside, sine * sine, 0.0)
+
+    def geo_row(at, which):
+        tile, c = at // per_tile % 2, at % per_tile * 2
+        return [geo_buf[tile, which, n : n + 1] for n in (c, c + 1)]
+
+    def basis_stage(at):
+        for n, dist in zip(blocks_of(at), geo_row(at, 5)):
+            offsets = dist - centres
             basis = jnp.exp(-sharpness * offsets * offsets)
-            basis_b = jnp.concatenate([basis.astype(BF16), ones_rows], axis=0)
-            basis_ref[:, at] = basis_b
-            slant_ref[:, at] = (-2.0 * sharpness) * basis * offsets
-            tanh = jnp.tanh(nn(lhs_x[...], basis_b))
-            neg_soft = jnp.log(1.0 - tanh).astype(BF16)
-            env = row(envelope)
-            env16 = jnp.broadcast_to(env, (16, span))
-            soft_ref[:, at] = neg_soft
-            gate_ref[:, at] = (tanh + 1.0) * (0.5 * env)
-            stack_ref[:width, at] = (
-                neg_soft.reshape(-1, 16, span) * (-env16).astype(BF16)[None]
-            ).reshape(width, span)
-            stack_ref[width:, at] = env16.astype(BF16)
-
-        return chunk
-
-    def finish_tile(entry, slot):
-        stack_ref, soft_ref, gate_ref, basis_ref, slant_ref, geo_ref, pull_ref = slot
-        tower_tile, plate_tile, recv_at, send_at, _ = places(entry)
-        sums = []
-
-        def chunk(c):
-            at = slice(c * LANES, c * LANES + span)
-            feat = feat_wide[plate_tile]
-            pair = adj_wide[tower_tile, :, at] * jnp.concatenate([feat, feat], axis=1)
-            stack = stack_ref[:, at]
-            filt = nn(lhs_f[:, : width + 16], stack)
-            back = nn(lhs_a[...], pair)
-            part_wf = nt(stack, pair)
-            prod = filt * adj_full[tower_tile, :, at]
-            prod = prod[:, :LANES] + prod[:, LANES:]
-            d_pre = (back[:width] * gate_ref[:, at]).astype(BF16)
-            both = jnp.concatenate([d_pre, soft_ref[:, at] * back[:width].astype(BF16)], axis=0)
-            part_wr = nt(basis_ref[:, at], d_pre)
-            d_basis = nn(lhs_d[...], both)
-            direct = jnp.sum(d_basis[:nbasis] * slant_ref[:, at], axis=0, keepdims=True)
-            inner = jnp.sum(back[width : width + 8], axis=0, keepdims=True)
-            inner = inner - d_basis[nbasis : nbasis + 1]
-            pull_ref[c : c + 1, :] = direct[:, :LANES] + geo_ref[3, c : c + 1] * inner[:, :LANES]
-            pull_ref[c + 1 : c + 2, :] = (
-                direct[:, LANES:] + geo_ref[3, c + 1 : c + 2] * inner[:, LANES:]
-            )
-            parts = [prod, part_wf, part_wr]
-            sums[:] = [a + b for a, b in zip(sums, parts)] if sums else parts
-
-        def end():
-            radial = pull_ref[...] * geo_ref[4]
-            for axis in range(3):
-                pull = geo_ref[axis] * radial
-                grad_recv[recv_at[0], recv_at[1], axis * rows + recv_at[2]] += pull
-                grad_send[send_at[0], send_at[1], axis * rows + send_at[2]] += pull
-            grad_feat[plate_tile] += sums[0]
-            acc_wf[...] += sums[1]
-            acc_wr[...] += sums[2]
-
-        return chunk, end
-
-    first = start_tile(0, slots[0])
-    for c in range(0, chunks, 2):
-        first(c)
+            slant_buf[n] = (-2.0 * sharpness) * basis * offsets
+            basis_buf[n] = jnp.concatenate([basis.astype(BF16), ones_rows], axis=0)
+        half = nn(lhs_x[...], wide(basis_buf, blocks_of(at)))
+        half_buf[at % 2 * 2] = half[:, :LANES]
+        half_buf[at % 2 * 2 + 1] = half[:, LANES:]
+
+    def soft_stage(at, entry):
+        tower_tile, plate_tile = places(entry)[:2]
+        c = at % per_tile * 2
+        for n, block in enumerate(blocks_of(at)):
+            env_rows = jnp.broadcast_to(geo_row(at, 6)[n], (PART, LANES))
+            half_env = 0.5 * env_rows
+            log_env = -math.log(2.0) * env_rows
+            stack_buf[block, width:] = env_rows[:16].astype(BF16)
+            for r in parts:
+                tanh = jnp.tanh(half_buf[at % 2 * 2 + n, r])
+                soft = jnp.log2(1.0 - tanh)
+                soft_buf[block, r] = soft
+                stack_buf[block, r] = (soft * log_env).astype(BF16)
+                gate_buf[block, r] = (tanh + 1.0) * half_env
+                pair = adj_wide[tower_tile, c + n, r] * feat_wide[plate_tile, r]
+                pair_buf[block, r] = pair.astype(BF16)
+
+    def product_stage(at):
+        blocks = blocks_of(at)
+        back = nn(lhs_a[...], wide(pair_buf, blocks))
+        lhs = jnp.concatenate([lhs_f[0], lhs_f[1, :, :16]], axis=1)
+        filt = nn(lhs, wide(stack_buf, blocks))
+        for n in range(2):
+            back_buf[at % 2 * 2 + n] = back[:, n * LANES : (n + 1) * LANES]
+            filt_buf[at % 2 * 2 + n] = filt[:, n * LANES : (n + 1) * LANES]
+
+    def feature_stage(at, entry):
+        tower_tile, plate_tile = places(entry)[:2]
+        c = at % per_tile * 2
+        for r in parts:
+            total = grad_feat[plate_tile, r]
+            for n, block in enumerate(blocks_of(at)):
+                back = back_buf[at % 2 * 2 + n, r]
+                low = slice(width + r.start, width + r.stop)
+                both_buf[block, r] = (back * gate_buf[block, r]).astype(BF16)
+                both_buf[block, low] = (back * soft_buf[block, r]).astype(BF16)
+                total = total + filt_buf[at % 2 * 2 + n, r] * adj_wide[tower_tile, c + n, r]
+            grad_feat[plate_tile, r] = total
+        for n, block in enumerate(blocks_of(at)):
+            inner_buf[block] = back_buf[at % 2 * 2 + n, width : width + 8]
+
+    def radial_stage(at, entry):
+        tile, c = at // per_tile % 2, at % per_tile * 2
+        lhs = jnp.concatenate([lhs_d[0], lhs_d[1]], axis=1)
+        d_basis = nn(lhs, wide(both_buf, blocks_of(at)))
+        for n, block in enumerate(blocks_of(at)):
+            part = d_basis[:, n * LANES : (n + 1) * LANES]
+            direct = jnp.sum(part[:nbasis] * slant_buf[block], axis=0, keepdims=True)
+            inner = jnp.sum(inner_buf[block], axis=0, keepdims=True)
+            inner = inner - math.log(2.0) * part[nbasis : nbasis + 1]
+            pull_buf[c + n : c + n + 1] = direct + geo_row(at, 3)[n] * inner
+        whole = blocks_of(at)
+        acc_wf[...] += nt(wide(stack_buf, whole), wide(pair_buf, whole))
+        acc_wr[...] += nt(wide(basis_buf, whole), wide(both_buf, whole, slice(0, width)))
+        if at % per_tile < per_tile - 1:
+            return
+        _, _, recv_at, send_at, _ = places(entry)
+        radial = pull_buf[...] * geo_buf[tile, 4]
+        for axis in range(3):
+            pull = geo_buf[tile, axis] * radial
+            grad_recv[recv_at[0], recv_at[1], axis * rows + recv_at[2]] += pull
+            grad_send[send_at[0], send_at[1], axis * rows + send_at[2]] += pull
+
+    parts = [slice(r, r + PART) for r in range(0, width, PART)]
+    for ref in (soft_buf, gate_buf):
+        ref[2 * ring - 2 :] = jnp.zeros((2, *ref.shape[1:]), ref.dtype)
+    for ref in (basis_buf, slant_buf, stack_buf, pair_buf, both_buf, inner_buf):
+        ref[ring:] = jnp.zeros((ring, *ref.shape[1:]), ref.dtype)
+    for ref in (back_buf, filt_buf, pull_buf):
+        ref[...] = jnp.zeros_like(ref)
+    geo_buf[1] = jnp.zeros(geo_buf.shape[1:], F32)
+    geometry(0, 0)
+    basis_stage(0)
+    soft_stage(0, 0)
+    basis_stage(1)
 
     def visit(step, carry):
-        for n in range(2):
-            entry = 2 * step + n
-            ahead = start_tile(entry + 1, slots[1 - n])
-            chunk, end = finish_tile(entry, slots[n])
-            for c in range(0, chunks, 2):
-                ahead(c)
-                chunk(c)
-            end()
+        def entry_of(at):
+            return jnp.maximum(2 * step + at // per_tile, 0)
+
+        for at in range(ring):
+            radial_stage(at - 2, entry_of(at - 2))
+            feature_stage(at - 1, entry_of(at - 1))
+            if at % per_tile == 1:
+                geometry(entry_of(at) + 1, (at // per_tile + 1) % 2)
+            product_stage(at)
+            soft_stage(at + 1, entry_of(at + 1))
+            basis_stage(at + 2)
         return carry
 
-    lax.fori_loop(0, (count + 1) // 2, visit, 0)
+    steps = (count + 1) // 2
+    lax.fori_loop(0, steps, visit, 0)
+    last = 2 * steps - 1
+    radial_stage(-2, last)
+    feature_stage(-1, last)
+    radial_stage(-1, last)
 
     digit = iota((1, width), 1)
     count_row = jnp.where(digit == 0, lax.rem(count, 16), 0)
@@ -380,23 +421,32 @@
     target[end - count :] = low
 
 
-def add_kernel(cut, kept_ref, weight_ref, got_ref, kept_out, *outs):
+def add_kernel(cut, kept_ref, weight_ref, got_ref, kept_out, send_out, weight_out):
     held, count = kept_ref.shape[0], weight_ref.shape[0]
     got = got_ref[...].astype(F32)
     total = kept_ref[...] + got[:held]
     weights = weight_ref[...] + got[held : held + count] + got[held + count :]
     kept_out[...] = total[:cut]
-    outs[-1][...] = weights
-    if len(outs) == 2:
-        outs[0][: held - cut] = total[cut:].astype(BF16)
-        put_split(outs[0], weights)
-
-
-def finish_kernel(atoms, count_ref, block_ref, near_ref, far_ref, feat_out, pos_out):
-    width = block_ref.shape[1]
+    send_out[: held - cut] = total[cut:].astype(BF16)
+    put_split(send_out, weights)
+    weight_out[...] = weights
+
+
+def join_kernel(weight_ref, got_ref, near_ref, both_ref, weight_out, near_out):
+    count = weight_ref.shape[0]
+    start = got_ref.shape[0] - 2 * count
+    got = got_ref[start:].astype(F32)
+    weights = weight_ref[...] + got[:count] + got[count:]
+    weight_out[...] = weights + (near_ref[:count] + both_ref[...])
+    near_out[...] = near_ref[count:]
+
+
+def finish_kernel(atoms, count_ref, block_ref, got_ref, near_ref, far_ref, feat_out, pos_out):
+    block, width = block_ref.shape
     live = iota((atoms, width), 0) < count_ref[0, 0]
-    feat_out[0] = jnp.where(live, block_ref[:atoms], 0.0)
-    spots = block_ref[atoms:] + near_ref[...] + far_ref[...]
+    total = block_ref[...] + got_ref[:block].astype(F32)
+    feat_out[0] = jnp.where(live, total[:atoms], 0.0)
+    spots = total[atoms:] + near_ref[...] + far_ref[...]
     rows = atoms // LANES
     for axis in range(3):
         for r in range(rows):
@@ -436,10 +486,9 @@
 SMEM = pl.BlockSpec(memory_space=pltpu.SMEM)
 
 
-def call(kernel, name, shapes, places, **extra):
+def call(kernel, shapes, places, **extra):
     return pl.pallas_call(
         kernel,
-        name=name,
         out_shape=[jax.ShapeDtypeStruct(shape, kind) for shape, kind in shapes],
         in_specs=places,
         out_specs=[VMEM] * len(shapes),
@@ -468,20 +517,18 @@
     chunks = TILE // groups
     plate_count = lax.axis_size("plate")
     tower_count = lax.axis_size("tower")
-    if plate_count & (plate_count - 1) or tower_count & (tower_count - 1):
+    if min(plate_count // 4, tower_count // 2) < 1 or any(
+        size & (size - 1) for size in (plate_count, tower_count)
+    ):
         raise ValueError("axis sizes")
-    pairs = TILE * TILE
     spots = 3 * (atoms // LANES)
     spot_rows = up(spots, 16)
     block = atoms + spot_rows
     weight_rows = up(width + nbasis + 3, 16)
 
     feat_block, adj_block = call(
-        pack_kernel,
-        "pack",
-        [((block, width), BF16)] * 2,
-        [SMEM, VMEM, VMEM, VMEM],
-    )(atom_counts, features, adjoint, positions)
+        pack_kernel, [((block, width), BF16)] * 2, [SMEM, VMEM, VMEM, VMEM]
+    )(atom_counts, features, adjoint, positions.astype(F32))
     peers = [swap(feat_block, "plate", across(step)) for step in range(1, plate_count)]
     near_adj = swap(adj_block, "tower", across(1))
     far_adj = swap(adj_block, "tower", beyond)
@@ -490,7 +537,6 @@
     half = plate_count // 2
     keep, send, weights, near_pos, far_pos = call(
         functools.partial(tile_kernel, plate_count),
-        "tiles",
         [
             ((half * block, width), F32),
             ((half * block + 2 * weight_rows, width), BF16),
@@ -500,9 +546,8 @@
         ],
         [SMEM] * 5 + [VMEM] * (3 + plate_count + 4),
         scratch_shapes=[
-            pltpu.VMEM((3 * per_brick, width, pairs), BF16),
-            pltpu.VMEM((3 * per_brick, width, pairs), F32),
-            pltpu.VMEM((plate_count * per_brick, width, LANES), BF16),
+            pltpu.VMEM((3 * per_brick, chunks, width, LANES), F32),
+            pltpu.VMEM((plate_count * per_brick, width, LANES), F32),
             pltpu.VMEM((3, groups, spots, chunks, LANES), F32),
             pltpu.VMEM((plate_count, groups, spot_rows, LANES), F32),
             pltpu.VMEM((plate_count * per_brick, width, LANES), F32),
@@ -511,20 +556,25 @@
             pltpu.VMEM((width + 16, width), F32),
             pltpu.VMEM((2 * nbasis, width), F32),
             pltpu.VMEM((width, 2 * nbasis), BF16),
-            pltpu.VMEM((width, 2 * width), BF16),
+            pltpu.VMEM((2, width, width), BF16),
             pltpu.VMEM((width + 16, width), BF16),
-            pltpu.VMEM((2 * nbasis, 2 * width), BF16),
+            pltpu.VMEM((2, 2 * nbasis, width), BF16),
         ]
         + [
-            pltpu.VMEM((width + 16, pairs), BF16),
-            pltpu.VMEM((width, pairs), BF16),
-            pltpu.VMEM((width, pairs), F32),
-            pltpu.VMEM((2 * nbasis, pairs), BF16),
-            pltpu.VMEM((nbasis, pairs), F32),
-            pltpu.VMEM((5, chunks, LANES), F32),
+            pltpu.VMEM((2 * chunks, width + 16, LANES), BF16),
+            pltpu.VMEM((2 * chunks, width, LANES), F32),
+            pltpu.VMEM((2 * chunks, width, LANES), F32),
+            pltpu.VMEM((2 * chunks, width, LANES), BF16),
+            pltpu.VMEM((2 * chunks, 2 * width, LANES), BF16),
+            pltpu.VMEM((2 * chunks, 2 * nbasis, LANES), BF16),
+            pltpu.VMEM((2 * chunks, nbasis, LANES), F32),
+            pltpu.VMEM((2 * chunks, 8, LANES), F32),
+            pltpu.VMEM((2, 7, chunks, LANES), F32),
             pltpu.VMEM((chunks, LANES), F32),
-        ]
-        * 2,
+            pltpu.VMEM((4, width, LANES), F32),
+            pltpu.VMEM((4, width + 16, LANES), F32),
+            pltpu.VMEM((4, width, LANES), F32),
+        ],
     )(
         at,
         tile_counts,
@@ -542,31 +592,27 @@
         b_filter[None],
     )
 
-    got_near, got_far = None, None
-    for step in [1] + [1 << n for n in reversed(range(1, plate_count.bit_length() - 1))]:
+    got_far = swap(far_pos, "tower", beyond)
+    for step in [1] + [1 << n for n in range(plate_count.bit_length() - 2, 1, -1)]:
         got = swap(send, "plate", across(step))
-        if got_near is None:
-            got_near = swap(near_pos, "tower", across(1))
-            got_far = swap(far_pos, "tower", beyond)
         held = keep.shape[0]
-        cut = max(held // 2, block)
-        shapes = [((cut, width), F32)]
-        if held > cut:
-            shapes.append(((held - cut + 2 * weight_rows, width), BF16))
-        shapes.append(((weight_rows, width), F32))
-        keep, *rest = call(functools.partial(add_kernel, cut), "add", shapes, [VMEM] * 3)(
-            keep, weights, got
-        )
-        weights = rest[-1]
-        send = rest[0]
-    grad_features, grad_positions = call(
-        functools.partial(finish_kernel, atoms),
-        "finish",
-        [((1, atoms, width), F32), ((3, 1, atoms), F32)],
-        [SMEM, VMEM, VMEM, VMEM],
-    )(atom_counts, keep, got_near, got_far)
-
-    weights = weights + swap(weights, "tower", across(1))
+        cut = held // 2
+        keep, send, weights = call(
+            functools.partial(add_kernel, cut),
+            [
+                ((cut, width), F32),
+                ((held - cut + 2 * weight_rows, width), BF16),
+                ((weight_rows, width), F32),
+            ],
+            [VMEM] * 3,
+        )(keep, weights, got)
+    both = swap(weights, ("tower", "plate"), across(plate_count + 2))
+    near = swap(jnp.concatenate([weights, near_pos], axis=0), "tower", across(1))
+    got = swap(send, "plate", across(2))
+    weights, got_near = call(
+        join_kernel, [((weight_rows, width), F32), ((spot_rows, width), F32)], [VMEM] * 4
+    )(weights, got, near, both)
+
     bits = 2
     parts = [weights]
     while bits < tower_count:
@@ -574,9 +620,13 @@
         stride = [s * bits for s in (1, 2, 3) if s * bits < tower_count]
         parts = [weights] + [swap(weights, "tower", across(s)) for s in stride]
         bits *= 4
+    grad_features, grad_positions = call(
+        functools.partial(finish_kernel, atoms),
+        [((1, atoms, width), F32), ((3, 1, atoms), F32)],
+        [SMEM] + [VMEM] * 4,
+    )(atom_counts, keep, got, got_near, got_far)
     out_wr, out_br, out_wf, out_bf = call(
         weight_kernel,
-        "weights",
         [((nbasis, width), F32), ((1, width), F32), ((width, width), F32), ((1, width), F32)],
         [VMEM] * len(parts),
     )(*parts)

time: 122 us -> 96.1 us (0.79)
  Pallas kernels: 48.8 us -> 31.7 us
  starting transfers between devices: 44.9 us -> 39.9 us
  waiting for transfers between devices: 18.8 us -> 14.7 us
  other arithmetic: 1.49 us -> 2.81 us
    pallas_call x6, Pallas kernels: 48.8 us -> 31.7 us  [the longest x1 23.1 us: local(): call(functools.partial(tile_kernel, plate_count), [((half * block, width)...]
    ppermute x13, starting transfers between devices: 44.9 us -> 39.9 us  [swap(): lax.ppermute(value, axis, [(i, route(i) % size) for i in range(size)])]
    ppermute x13, waiting for transfers between devices: 18.8 us -> 14.7 us  [swap(): lax.ppermute(value, axis, [(i, route(i) % size) for i in range(size)])]
    convert_element_type x0 -> x1, other arithmetic: none -> 1.26 us  [local(): positions.astype(F32)]
    unnamed x31 -> x32, local copies, waits for them, and re-layouts: 5.13 us -> 4.49 us
  transfers between devices with their start and end apart: 13 -> 13, of which waited for: 8 -> 6; matrix products, arithmetic and copies ran while one was open for 0% -> 2% of each run, Pallas kernels for 1% -> 2%
where the time goes in v2:
time: 96.1 us; the launch traced here: 95.7 us
  starting transfers between devices  39.9 us (42%)
  Pallas kernels  31.7 us (33%)
  waiting for transfers between devices  14.7 us (15%)
  local copies, waits for them, and re-layouts  4.49 us (5%)
  other arithmetic  2.81 us (3%)
  between operations  2.01 us (2%)
    ppermute x13, starting transfers between devices, swap(): lax.ppermute(value, axis, [(i, route(i) % size) for i in range(size)])  39.9 us
    pallas_call x1, Pallas kernels, local(): call(functools.partial(tile_kernel, plate_count), [((half * block, width)...  23.1 us
    ppermute x13, waiting for transfers between devices, swap(): lax.ppermute(value, axis, [(i, route(i) % size) for i in range(size)])  14.7 us
    unnamed x32, local copies, waits for them, and re-layouts  4.49 us
  transfers between devices with their start and end apart: 13, of which 6 were waited for; matrix products, arithmetic and copies ran while one was open for 2% of the time, Pallas kernels for 2%

profile of v2, /device:TPU:0, one launch (start us, length us, event | category | flops | bytes accessed | tf_op | source)
XLA Modules:
  0.0 95.7 jit_solution(10638632987600592436)
XLA Ops:
  1.3 1.3 %copy_convert_fusion.pos_ref = f32[3,1,256]{2,1,0:T(1,128)} fusion(bf16[3,1,256]{2,0,1:T(4,128)(2,1)} %param.14), kind=kLoop, calls=%fused_computation.1 | loop fusion | flops 768 | bytes 4608 | tf_op jit(solution)/shard_map/convert_element_type | solution.py:531
  2.5 1.6 %shard_map.163 = (bf16[272,128]{1,0:T(8,128)(2,1)}, bf16[272,128]{1,0:T(8,128)(2,1)}) custom-call(s32[1,1]{1,0:T(1,128)S(6)} %copy.20.count_ref, bf16[1,256,128]{2,1,0:T(8,128)(2,1)} %feat_ref.1, bf16[1,256,128]{2,1,0:T(8,128)(2,1)} %adj_ref.1, f32[3,1,256]{2,1,0:T(1,128)} %copy_convert_fusion.pos_ref), custom_call_target="tpu_custom_call" | custom-call | tf_op jit(solution)/shard_map/pallas_call | solution.py:529
  4.1 6.0 %collective-permute-start.1 = (bf16[272,128]{1,0:T(8,128)(2,1)}, bf16[272,128]{1,0:T(8,128)(2,1)S(1)}, u32[]{:S(2)}, u32[]{:S(2)}) collective-permute-start(bf16[272,128]{1,0:T(8,128)(2,1)} %get-tuple-element.24.refs_0_), channel_id=1, source_target_pairs={{0,28},{4,8},{8,4},{12,16},{16,12},{20,24},{24,20},{28,0},{1,29},{... | collective-permute-start | bytes 208904 | tf_op jit(solution)/shard_map/ppermute | solution.py:474
  10.1 0.0 collective-permute-start
  10.1 0.7 collective-permute-start.4
  10.8 0.8 collective-permute-start.3
  11.6 0.3 collective-permute-start.2
  12.6 0.6 pad_add_fusion.where_ref
  13.2 0.0 collective-permute-done.1.refs_2_
  13.2 1.4 %collective-permute-done.refs_1_ = bf16[272,128]{1,0:T(8,128)(2,1)S(1)} collective-permute-done((bf16[272,128]{1,0:T(8,128)(2,1)}, bf16[272,128]{1,0:T(8,128)(2,1)S(1)}, u32[]{:S(2)}, u32[]{:S(2)}) %collective-permute-start) | collective-permute-done | bytes 69664 | tf_op jit(solution)/shard_map/ppermute | solution.py:474
  14.6 0.0 copy-start.9
  14.6 0.1 collective-permute-done.4.refs_6_
  14.7 0.0 copy-start.10
  14.7 1.6 %collective-permute-done.3.refs_5_ = bf16[272,128]{1,0:T(8,128)(2,1)S(1)} collective-permute-done((bf16[272,128]{1,0:T(8,128)(2,1)}, bf16[272,128]{1,0:T(8,128)(2,1)S(1)}, u32[]{:S(2)}, u32[]{:S(2)}) %collective-permute-start.3) | collective-permute-done | bytes 69664 | tf_op jit(solution)/shard_map/ppermute | solution.py:474
  16.3 0.0 copy-start.11
  16.3 0.0 collective-permute-done.2.refs_4_
  16.3 0.0 copy-start.12
  16.3 0.0 copy-done.8
  16.3 0.0 copy-done.9
  16.3 0.0 copy-done.10
  16.3 0.6 copy-done.11
  16.9 0.0 copy-done.12
  16.9 23.1 %shard_map.164 = (f32[544,128]{1,0:T(8,128)}, bf16[864,128]{1,0:T(8,128)(2,1)}, f32[160,128]{1,0:T(8,128)}, f32[16,128]{1,0:T(8,128)}, f32[16,128]{1,0:T(8,128)}) custom-call(s32[2]{0:T(128)} %pad_add_fusion.where_ref, s32[1,1]{1,0:T(1,128)S(6)} %copy.21.count_ref, s32[1,1,56]{2,1,0:T(1,128)} %tower_ref.1, s32[1,1,56]{2,1,0:T(1,128)} %plate_ref.1, ...), custom_call_target="tpu_custom_call" | custom-call | tf_op jit(solution)/shard_map/pallas_call | solution.py:538
  40.1 0.1 collective-permute-start.5
  40.2 1.6 %collective-permute-done.5.got_ref = bf16[864,128]{1,0:T(8,128)(2,1)S(1)} collective-permute-done((bf16[864,128]{1,0:T(8,128)(2,1)}, bf16[864,128]{1,0:T(8,128)(2,1)S(1)}, u32[]{:S(2)}, u32[]{:S(2)}) %collective-permute-start.5) | collective-permute-done | bytes 221216 | tf_op jit(solution)/shard_map/ppermute | solution.py:474
  41.8 0.0 copy-start.2
  41.8 0.7 copy-done.2
  42.5 0.0 copy-start.13
  42.5 1.8 %shard_map.165 = (f32[272,128]{1,0:T(8,128)}, bf16[592,128]{1,0:T(8,128)(2,1)}, f32[160,128]{1,0:T(8,128)}) custom-call(f32[544,128]{1,0:T(8,128)} %get-tuple-element.26.kept_ref, f32[160,128]{1,0:T(8,128)} %get-tuple-element.27.weight_ref, bf16[864,128]{1,0:T(8,128)(2,1)} %copy-done.2), custom_call_target="tpu_custom_call" | custom-call | tf_op jit(solution)/shard_map/pallas_call | solution.py:600
  44.4 24.2 %collective-permute-start.6 = (bf16[592,128]{1,0:T(8,128)(2,1)}, bf16[592,128]{1,0:T(8,128)(2,1)S(1)}, u32[]{:S(2)}, u32[]{:S(2)}) collective-permute-start(bf16[592,128]{1,0:T(8,128)(2,1)} %get-tuple-element.30), channel_id=1, source_target_pairs={{0,2},{1,3},{2,0},{3,1},{4,6},{5,7},{6,4},{7,5},{8,10},{9,11},{10,... | collective-permute-start | bytes 454664 | tf_op jit(solution)/shard_map/ppermute | solution.py:474
  68.6 0.0 copy-done.13
  68.6 0.0 copy-start.1
  68.6 1.0 %pad_maximum_fusion = f32[176,128]{1,0:T(8,128)S(1)} fusion(f32[16,128]{1,0:T(8,128)S(1)} %copy-done.13, f32[160,128]{1,0:T(8,128)} %get-tuple-element.31.weight_ref), kind=kLoop, calls=%fused_computation | loop fusion | flops 22528 | bytes 180224 | tf_op jit(solution)/shard_map/concatenate | solution.py:610
  69.6 0.0 copy-start.15
  69.6 1.7 %collective-permute-start.7 = (f32[176,128]{1,0:T(8,128)S(1)}, f32[176,128]{1,0:T(8,128)S(1)}, u32[]{:S(2)}, u32[]{:S(2)}) collective-permute-start(f32[176,128]{1,0:T(8,128)S(1)} %pad_maximum_fusion), channel_id=1, source_target_pairs={{0,4},{4,0},{8,12},{12,8},{16,20},{20,16},{24,28},{28,24},{1,5},{5... | collective-permute-start | bytes 270344 | tf_op jit(solution)/shard_map/ppermute | solution.py:474
  71.2 0.0 copy-done.1
  71.2 0.7 collective-permute-start.8
  71.9 4.7 %collective-permute-done.8.both_ref = f32[160,128]{1,0:T(8,128)S(1)} collective-permute-done((f32[160,128]{1,0:T(8,128)S(1)}, f32[160,128]{1,0:T(8,128)S(1)}, u32[]{:S(2)}, u32[]{:S(2)}) %collective-permute-start.8) | collective-permute-done | bytes 81952 | tf_op jit(solution)/shard_map/ppermute | solution.py:474
  76.6 0.0 copy-start.7
  76.6 0.0 collective-permute-done.7.near_ref
  76.6 0.0 copy-start.3
  76.6 0.0 collective-permute-done.6.got_ref
  76.6 0.6 copy-done.7
  77.2 0.0 copy-done.3
  77.2 0.0 copy-start
  77.2 0.6 copy-done
  77.9 1.7 %shard_map.166 = (f32[160,128]{1,0:T(8,128)}, f32[16,128]{1,0:T(8,128)}) custom-call(f32[160,128]{1,0:T(8,128)} %get-tuple-element.31.weight_ref, bf16[592,128]{1,0:T(8,128)(2,1)} %copy-done, f32[176,128]{1,0:T(8,128)} %copy-done.3, f32[160,128]{1,0:T(8,128)} %copy-done.7), custom_call_target="tpu_custom_call" | custom-call | tf_op jit(solution)/shard_map/pallas_call | solution.py:612
  79.6 0.1 collective-permute-start.12
  79.7 1.1 %collective-permute-start.11 = (f32[160,128]{1,0:T(8,128)}, f32[160,128]{1,0:T(8,128)S(1)}, u32[]{:S(2)}, u32[]{:S(2)}) collective-permute-start(f32[160,128]{1,0:T(8,128)} %get-tuple-element.37.refs_0_), channel_id=1, source_target_pairs={{0,16},{4,20},{8,24},{12,28},{16,0},{20,4},{24,8},{28,12},{1,17},{... | collective-permute-start | bytes 245768 | tf_op jit(solution)/shard_map/ppermute | solution.py:474
  80.8 3.2 %collective-permute-start.10 = (f32[160,128]{1,0:T(8,128)}, f32[160,128]{1,0:T(8,128)S(1)}, u32[]{:S(2)}, u32[]{:S(2)}) collective-permute-start(f32[160,128]{1,0:T(8,128)} %get-tuple-element.37.refs_0_), channel_id=1, source_target_pairs={{0,8},{4,12},{8,0},{12,4},{16,24},{20,28},{24,16},{28,20},{1,9},{5... | collective-permute-start | bytes 245768 | tf_op jit(solution)/shard_map/ppermute | solution.py:474
  84.0 0.0 copy-done.15
  84.0 1.0 %collective-permute-start.9 = (f32[16,128]{1,0:T(8,128)S(1)}, f32[16,128]{1,0:T(8,128)S(1)}, u32[]{:S(2)}, u32[]{:S(2)}) collective-permute-start(f32[16,128]{1,0:T(8,128)S(1)} %copy-done.15), channel_id=1, source_target_pairs={{0,28},{4,8},{8,4},{12,16},{16,12},{20,24},{24,20},{28,0},{1,29},{... | collective-permute-start | bytes 24584 | tf_op jit(solution)/shard_map/ppermute | solution.py:474
  85.0 5.3 %collective-permute-done.9.far_ref = f32[16,128]{1,0:T(8,128)S(1)} collective-permute-done((f32[16,128]{1,0:T(8,128)S(1)}, f32[16,128]{1,0:T(8,128)S(1)}, u32[]{:S(2)}, u32[]{:S(2)}) %collective-permute-start.9) | collective-permute-done | bytes 8224 | tf_op jit(solution)/shard_map/ppermute | solution.py:474
  90.3 0.0 copy-start.14
  90.3 0.6 copy-done.14
  90.9 1.7 %shard_map.167 = (f32[1,256,128]{2,1,0:T(8,128)}, f32[3,1,256]{2,1,0:T(1,128)}) custom-call(s32[1,1]{1,0:T(1,128)S(6)} %copy.20.count_ref, f32[272,128]{1,0:T(8,128)} %get-tuple-element.29.block_ref, bf16[592,128]{1,0:T(8,128)(2,1)} %copy-done, f32[16,128]{1,0:T(8,128)} %get-tuple-element.33.near_ref, f32[16,128]{1,0:T(8,128)} %copy-done.14), custom_call_target="tpu_custom_call" | custom-call | tf_op jit(solution)/shard_map/pallas_call | solution.py:623
  92.6 0.0 collective-permute-done.12.refs_3_
  92.6 0.0 collective-permute-done.11.refs_2_
  92.6 0.0 copy-start.5
  92.6 0.0 collective-permute-done.10.refs_1_
  92.6 0.6 copy-done.4
  93.2 0.0 copy-done.5
  93.3 0.6 copy-done.6
  93.9 1.8 %shard_map.168 = (f32[16,128]{1,0:T(8,128)}, f32[1,128]{1,0:T(1,128)}, f32[128,128]{1,0:T(8,128)}, f32[1,128]{1,0:T(1,128)}) custom-call(f32[160,128]{1,0:T(8,128)} %get-tuple-element.37.refs_0_, f32[160,128]{1,0:T(8,128)} %copy-done.6, f32[160,128]{1,0:T(8,128)} %copy-done.5, f32[160,128]{1,0:T(8,128)} %copy-done.4), custom_call_target="tpu_custom_call" | custom-call | tf_op jit(solution)/shard_map/pallas_call | solution.py:628
  (3 shorter events, 0.0 us)
Async XLA Ops:
  4.1 9.1 %collective-permute-start.1 = (bf16[272,128]{1,0:T(8,128)(2,1)}, bf16[272,128]{1,0:T(8,128)(2,1)S(1)}, u32[]{:S(2)}, u32[]{:S(2)}) collective-permute-start(bf16[272,128]{1,0:T(8,128)(2,1)} %get-tuple-element.24.refs_0_), channel_id=1, source_target_pairs={{0,28},{4,8},{8,4},{12,16},{16,12},{20,24},{24,20},{28,0},{1,29},{... | collective-permute-start | bytes 208904 | tf_op jit(solution)/shard_map/ppermute | solution.py:474
  10.1 4.5 %collective-permute-start = (bf16[272,128]{1,0:T(8,128)(2,1)}, bf16[272,128]{1,0:T(8,128)(2,1)S(1)}, u32[]{:S(2)}, u32[]{:S(2)}) collective-permute-start(bf16[272,128]{1,0:T(8,128)(2,1)} %get-tuple-element.24.refs_0_), channel_id=1, source_target_pairs={{0,4},{4,0},{8,12},{12,8},{16,20},{20,16},{24,28},{28,24},{1,5},{5... | collective-permute-start | bytes 208904 | tf_op jit(solution)/shard_map/ppermute | solution.py:474
  10.1 4.6 %collective-permute-start.4 = (bf16[272,128]{1,0:T(8,128)(2,1)}, bf16[272,128]{1,0:T(8,128)(2,1)S(1)}, u32[]{:S(2)}, u32[]{:S(2)}) collective-permute-start(bf16[272,128]{1,0:T(8,128)(2,1)} %get-tuple-element.25.refs_3_), channel_id=1, source_target_pairs={{0,3},{1,2},{2,1},{3,0},{4,7},{5,6},{6,5},{7,4},{8,11},{9,10},{10,... | collective-permute-start | bytes 208904 | tf_op jit(solution)/shard_map/ppermute | solution.py:474
  10.8 5.5 %collective-permute-start.3 = (bf16[272,128]{1,0:T(8,128)(2,1)}, bf16[272,128]{1,0:T(8,128)(2,1)S(1)}, u32[]{:S(2)}, u32[]{:S(2)}) collective-permute-start(bf16[272,128]{1,0:T(8,128)(2,1)} %get-tuple-element.25.refs_3_), channel_id=1, source_target_pairs={{0,2},{1,3},{2,0},{3,1},{4,6},{5,7},{6,4},{7,5},{8,10},{9,11},{10,... | collective-permute-start | bytes 208904 | tf_op jit(solution)/shard_map/ppermute | solution.py:474
  11.6 4.7 %collective-permute-start.2 = (bf16[272,128]{1,0:T(8,128)(2,1)}, bf16[272,128]{1,0:T(8,128)(2,1)S(1)}, u32[]{:S(2)}, u32[]{:S(2)}) collective-permute-start(bf16[272,128]{1,0:T(8,128)(2,1)} %get-tuple-element.25.refs_3_), channel_id=1, source_target_pairs={{0,1},{1,0},{2,3},{3,2},{4,5},{5,4},{6,7},{7,6},{8,9},{9,8},{10,11... | collective-permute-start | bytes 208904 | tf_op jit(solution)/shard_map/ppermute | solution.py:474
  13.2 3.1 %copy-start.8 = (bf16[272,128]{1,0:T(8,128)(2,1)}, bf16[272,128]{1,0:T(8,128)(2,1)S(1)}, u32[]{:S(2)}) copy-start(bf16[272,128]{1,0:T(8,128)(2,1)S(1)} %collective-permute-done.1.refs_2_) | copy-start | bytes 208900
  14.6 1.7 %copy-start.9 = (bf16[272,128]{1,0:T(8,128)(2,1)}, bf16[272,128]{1,0:T(8,128)(2,1)S(1)}, u32[]{:S(2)}) copy-start(bf16[272,128]{1,0:T(8,128)(2,1)S(1)} %collective-permute-done.refs_1_) | copy-start | bytes 208900
  14.7 1.6 %copy-start.10 = (bf16[272,128]{1,0:T(8,128)(2,1)}, bf16[272,128]{1,0:T(8,128)(2,1)S(1)}, u32[]{:S(2)}) copy-start(bf16[272,128]{1,0:T(8,128)(2,1)S(1)} %collective-permute-done.4.refs_6_) | copy-start | bytes 208900
  16.3 0.6 copy-start.11
  16.3 0.7 copy-start.12
  40.1 1.7 %collective-permute-start.5 = (bf16[864,128]{1,0:T(8,128)(2,1)}, bf16[864,128]{1,0:T(8,128)(2,1)S(1)}, u32[]{:S(2)}, u32[]{:S(2)}) collective-permute-start(bf16[864,128]{1,0:T(8,128)(2,1)} %get-tuple-element.28), channel_id=1, source_target_pairs={{0,1},{1,0},{2,3},{3,2},{4,5},{5,4},{6,7},{7,6},{8,9},{9,8},{10,11... | collective-permute-start | bytes 663560 | tf_op jit(solution)/shard_map/ppermute | solution.py:474
  41.8 0.7 copy-start.2
  42.5 26.1 %copy-start.13 = (f32[16,128]{1,0:T(8,128)S(1)}, f32[16,128]{1,0:T(8,128)}, u32[]{:S(2)}) copy-start(f32[16,128]{1,0:T(8,128)} %get-tuple-element.32) | copy-start | bytes 24580
  44.4 32.2 %collective-permute-start.6 = (bf16[592,128]{1,0:T(8,128)(2,1)}, bf16[592,128]{1,0:T(8,128)(2,1)S(1)}, u32[]{:S(2)}, u32[]{:S(2)}) collective-permute-start(bf16[592,128]{1,0:T(8,128)(2,1)} %get-tuple-element.30), channel_id=1, source_target_pairs={{0,2},{1,3},{2,0},{3,1},{4,6},{5,7},{6,4},{7,5},{8,10},{9,11},{10,... | collective-permute-start | bytes 454664 | tf_op jit(solution)/shard_map/ppermute | solution.py:474
  68.6 2.7 %copy-start.1 = (f32[160,128]{1,0:T(8,128)S(1)}, f32[160,128]{1,0:T(8,128)}, u32[]{:S(2)}) copy-start(f32[160,128]{1,0:T(8,128)} %get-tuple-element.31.weight_ref) | copy-start | bytes 245764
  69.6 14.4 %copy-start.15 = (f32[16,128]{1,0:T(8,128)S(1)}, f32[16,128]{1,0:T(8,128)}, u32[]{:S(2)}) copy-start(f32[16,128]{1,0:T(8,128)} %get-tuple-element.34) | copy-start | bytes 24580
  69.6 7.0 %collective-permute-start.7 = (f32[176,128]{1,0:T(8,128)S(1)}, f32[176,128]{1,0:T(8,128)S(1)}, u32[]{:S(2)}, u32[]{:S(2)}) collective-permute-start(f32[176,128]{1,0:T(8,128)S(1)} %pad_maximum_fusion), channel_id=1, source_target_pairs={{0,4},{4,0},{8,12},{12,8},{16,20},{20,16},{24,28},{28,24},{1,5},{5... | collective-permute-start | bytes 270344 | tf_op jit(solution)/shard_map/ppermute | solution.py:474
  71.2 5.3 %collective-permute-start.8 = (f32[160,128]{1,0:T(8,128)S(1)}, f32[160,128]{1,0:T(8,128)S(1)}, u32[]{:S(2)}, u32[]{:S(2)}) collective-permute-start(f32[160,128]{1,0:T(8,128)S(1)} %copy-done.1), channel_id=1, source_target_pairs={{0,6},{1,7},{2,4},{3,5},{4,2},{5,3},{6,0},{7,1},{8,14},{9,15},{10,... | collective-permute-start | bytes 245768 | tf_op jit(solution)/shard_map/ppermute | solution.py:474
  76.6 0.6 copy-start.7
  76.6 0.7 copy-start.3
  77.2 0.7 copy-start
  79.6 13.0 %collective-permute-start.12 = (f32[160,128]{1,0:T(8,128)}, f32[160,128]{1,0:T(8,128)S(1)}, u32[]{:S(2)}, u32[]{:S(2)}) collective-permute-start(f32[160,128]{1,0:T(8,128)} %get-tuple-element.37.refs_0_), channel_id=1, source_target_pairs={{0,24},{4,28},{8,16},{12,20},{16,8},{20,12},{24,0},{28,4},{1,25},{... | collective-permute-start | bytes 245768 | tf_op jit(solution)/shard_map/ppermute | solution.py:474
  79.7 12.9 %collective-permute-start.11 = (f32[160,128]{1,0:T(8,128)}, f32[160,128]{1,0:T(8,128)S(1)}, u32[]{:S(2)}, u32[]{:S(2)}) collective-permute-start(f32[160,128]{1,0:T(8,128)} %get-tuple-element.37.refs_0_), channel_id=1, source_target_pairs={{0,16},{4,20},{8,24},{12,28},{16,0},{20,4},{24,8},{28,12},{1,17},{... | collective-permute-start | bytes 245768 | tf_op jit(solution)/shard_map/ppermute | solution.py:474
  80.8 11.8 %collective-permute-start.10 = (f32[160,128]{1,0:T(8,128)}, f32[160,128]{1,0:T(8,128)S(1)}, u32[]{:S(2)}, u32[]{:S(2)}) collective-permute-start(f32[160,128]{1,0:T(8,128)} %get-tuple-element.37.refs_0_), channel_id=1, source_target_pairs={{0,8},{4,12},{8,0},{12,4},{16,24},{20,28},{24,16},{28,20},{1,9},{5... | collective-permute-start | bytes 245768 | tf_op jit(solution)/shard_map/ppermute | solution.py:474
  84.0 6.3 %collective-permute-start.9 = (f32[16,128]{1,0:T(8,128)S(1)}, f32[16,128]{1,0:T(8,128)S(1)}, u32[]{:S(2)}, u32[]{:S(2)}) collective-permute-start(f32[16,128]{1,0:T(8,128)S(1)} %copy-done.15), channel_id=1, source_target_pairs={{0,28},{4,8},{8,4},{12,16},{16,12},{20,24},{24,20},{28,0},{1,29},{... | collective-permute-start | bytes 24584 | tf_op jit(solution)/shard_map/ppermute | solution.py:474
  90.3 0.6 copy-start.14
  92.6 0.6 copy-start.4
  92.6 0.7 copy-start.5
  93.3 0.6 copy-start.6

commit v3 on v2

--- a/solution.py
+++ b/solution.py
@@ -12,6 +12,7 @@
 TILE = 32
 LANES = 128
 PART = 32
+TILES = 4
 
 box_side = 1.0
 brick_height = 1.0
@@ -137,7 +138,8 @@
     for source, slot in sources:
 
         def widen_adj(half, carry, source=source, slot=slot):
-            for t in (2 * half, 2 * half + 1):
+            for t in range(4):
+                t = 4 * half + t
                 start = pl.multiple_of(t * TILE, TILE)
                 part = source[pl.ds(start, TILE), :].astype(F32).T.astype(BF16)
                 wide = nn(part, pick_recv)
@@ -145,7 +147,7 @@
                     adj_wide[slot * per_brick + t, c] = wide[:, c * LANES : (c + 1) * LANES]
             return carry
 
-        lax.fori_loop(0, per_brick // 2, widen_adj, 0)
+        lax.fori_loop(0, per_brick // 4, widen_adj, 0)
     for q in range(groups):
         pick = one_hot(iota((LANES, pairs), 0) == q * TILE + iota((LANES, pairs), 1) // TILE)
         for source, slot in sources:
@@ -323,7 +325,7 @@
     for ref in (soft_buf, gate_buf):
         ref[2 * ring - 2 :] = jnp.zeros((2, *ref.shape[1:]), ref.dtype)
     for ref in (basis_buf, slant_buf, stack_buf, pair_buf, both_buf, inner_buf):
-        ref[ring:] = jnp.zeros((ring, *ref.shape[1:]), ref.dtype)
+        ref[2 * ring - 4 :] = jnp.zeros((4, *ref.shape[1:]), ref.dtype)
     for ref in (back_buf, filt_buf, pull_buf):
         ref[...] = jnp.zeros_like(ref)
     geo_buf[1] = jnp.zeros(geo_buf.shape[1:], F32)
@@ -334,9 +336,9 @@
 
     def visit(step, carry):
         def entry_of(at):
-            return jnp.maximum(2 * step + at // per_tile, 0)
-
-        for at in range(ring):
+            return jnp.maximum(TILES * step + at // per_tile, 0)
+
+        for at in range(TILES * per_tile):
             radial_stage(at - 2, entry_of(at - 2))
             feature_stage(at - 1, entry_of(at - 1))
             if at % per_tile == 1:
@@ -346,9 +348,9 @@
             basis_stage(at + 2)
         return carry
 
-    steps = (count + 1) // 2
+    steps = (count + TILES - 1) // TILES
     lax.fori_loop(0, steps, visit, 0)
-    last = 2 * steps - 1
+    last = TILES * steps - 1
     radial_stage(-2, last)
     feature_stage(-1, last)
     radial_stage(-1, last)
@@ -421,23 +423,24 @@
     target[end - count :] = low
 
 
-def add_kernel(cut, kept_ref, weight_ref, got_ref, kept_out, send_out, weight_out):
-    held, count = kept_ref.shape[0], weight_ref.shape[0]
+def add_kernel(cut, kept_ref, weight_ref, got_ref, near_ref, kept_out, send_out, weight_out):
+    held, count = kept_ref.shape[0], weight_out.shape[0] - near_ref.shape[0]
     got = got_ref[...].astype(F32)
     total = kept_ref[...] + got[:held]
-    weights = weight_ref[...] + got[held : held + count] + got[held + count :]
+    weights = weight_ref[:count] + got[held : held + count] + got[held + count :]
     kept_out[...] = total[:cut]
     send_out[: held - cut] = total[cut:].astype(BF16)
     put_split(send_out, weights)
-    weight_out[...] = weights
+    weight_out[:count] = weights
+    weight_out[count:] = near_ref[...]
 
 
 def join_kernel(weight_ref, got_ref, near_ref, both_ref, weight_out, near_out):
-    count = weight_ref.shape[0]
+    count = weight_out.shape[0]
     start = got_ref.shape[0] - 2 * count
     got = got_ref[start:].astype(F32)
-    weights = weight_ref[...] + got[:count] + got[count:]
-    weight_out[...] = weights + (near_ref[:count] + both_ref[...])
+    weights = weight_ref[:count] + got[:count] + got[count:]
+    weight_out[...] = weights + (near_ref[:count] + both_ref[:count])
     near_out[...] = near_ref[count:]
 
 
@@ -602,12 +605,12 @@
             [
                 ((cut, width), F32),
                 ((held - cut + 2 * weight_rows, width), BF16),
-                ((weight_rows, width), F32),
+                ((weight_rows + spot_rows, width), F32),
             ],
-            [VMEM] * 3,
-        )(keep, weights, got)
+            [VMEM] * 4,
+        )(keep, weights, got, near_pos)
     both = swap(weights, ("tower", "plate"), across(plate_count + 2))
-    near = swap(jnp.concatenate([weights, near_pos], axis=0), "tower", across(1))
+    near = swap(weights, "tower", across(1))
     got = swap(send, "plate", across(2))
     weights, got_near = call(
         join_kernel, [((weight_rows, width), F32), ((spot_rows, width), F32)], [VMEM] * 4

time: 96.1 us -> 91.5 us (0.952)
  starting transfers between devices: 39.9 us -> 37.6 us
    ppermute x13, starting transfers between devices: 39.9 us -> 37.6 us  [swap(): lax.ppermute(value, axis, [(i, route(i) % size) for i in range(size)])]
    concatenate x1 -> x0, other arithmetic: 0.97 us -> none  [local(): jnp.concatenate([weights, near_pos], axis=0)]
    unnamed x32 -> x28, local copies, waits for them, and re-layouts: 4.49 us -> 4.47 us
  transfers between devices with their start and end apart: 13 -> 13, of which waited for: 6 -> 7; matrix products, arithmetic and copies ran while one was open for 2% -> 1% of each run, Pallas kernels for 2% -> 2%
where the time goes in v3:
time: 91.5 us; the launch traced here: 91.1 us
  starting transfers between devices  37.6 us (41%)
  Pallas kernels  30.8 us (34%)
  waiting for transfers between devices  14.4 us (16%)
  local copies, waits for them, and re-layouts  4.47 us (5%)
  between operations  2.01 us (2%)
  other arithmetic  1.85 us (2%)
    ppermute x13, starting transfers between devices, swap(): lax.ppermute(value, axis, [(i, route(i) % size) for i in range(size)])  37.6 us
    pallas_call x1, Pallas kernels, local(): call(functools.partial(tile_kernel, plate_count), [((half * block, width)...  22.3 us
    ppermute x13, waiting for transfers between devices, swap(): lax.ppermute(value, axis, [(i, route(i) % size) for i in range(size)])  14.4 us
    unnamed x28, local copies, waits for them, and re-layouts  4.47 us
    pallas_call x1, Pallas kernels, local(): call(functools.partial(add_kernel, cut), [((cut, width), F32), ((held - c...  1.84 us
  transfers between devices with their start and end apart: 13, of which 7 were waited for; matrix products, arithmetic and copies ran while one was open for 1% of the time, Pallas kernels for 2%

profile of v3, /device:TPU:0, one launch (start us, length us, event | category | flops | bytes accessed | tf_op | source)
XLA Modules:
  0.0 91.1 jit_solution(15069816294578512382)
XLA Ops:
  1.3 1.3 %copy_convert_fusion.pos_ref = f32[3,1,256]{2,1,0:T(1,128)} fusion(bf16[3,1,256]{2,0,1:T(4,128)(2,1)} %param.14), kind=kLoop, calls=%fused_computation | loop fusion | flops 768 | bytes 4608 | tf_op jit(solution)/shard_map/convert_element_type | solution.py:534
  2.5 1.5 %shard_map.163 = (bf16[272,128]{1,0:T(8,128)(2,1)}, bf16[272,128]{1,0:T(8,128)(2,1)}) custom-call(s32[1,1]{1,0:T(1,128)S(6)} %copy.20.count_ref, bf16[1,256,128]{2,1,0:T(8,128)(2,1)} %feat_ref.1, bf16[1,256,128]{2,1,0:T(8,128)(2,1)} %adj_ref.1, f32[3,1,256]{2,1,0:T(1,128)} %copy_convert_fusion.pos_ref), custom_call_target="tpu_custom_call" | custom-call | tf_op jit(solution)/shard_map/pallas_call | solution.py:532
  4.1 6.0 %collective-permute-start.1 = (bf16[272,128]{1,0:T(8,128)(2,1)}, bf16[272,128]{1,0:T(8,128)(2,1)S(1)}, u32[]{:S(2)}, u32[]{:S(2)}) collective-permute-start(bf16[272,128]{1,0:T(8,128)(2,1)} %get-tuple-element.24.refs_0_), channel_id=1, source_target_pairs={{0,28},{4,8},{8,4},{12,16},{16,12},{20,24},{24,20},{28,0},{1,29},{... | collective-permute-start | bytes 208904 | tf_op jit(solution)/shard_map/ppermute | solution.py:477
  10.1 0.0 collective-permute-start
  10.1 0.7 collective-permute-start.4
  10.8 0.8 collective-permute-start.3
  11.6 0.3 collective-permute-start.2
  12.6 0.6 pad_add_fusion.where_ref
  13.2 0.0 collective-permute-done.1.refs_2_
  13.2 0.0 copy-start.7
  13.2 1.4 %collective-permute-done.refs_1_ = bf16[272,128]{1,0:T(8,128)(2,1)S(1)} collective-permute-done((bf16[272,128]{1,0:T(8,128)(2,1)}, bf16[272,128]{1,0:T(8,128)(2,1)S(1)}, u32[]{:S(2)}, u32[]{:S(2)}) %collective-permute-start) | collective-permute-done | bytes 69664 | tf_op jit(solution)/shard_map/ppermute | solution.py:477
  14.6 0.0 copy-start.8
  14.6 0.1 collective-permute-done.4.refs_6_
  14.7 0.0 copy-start.9
  14.7 1.6 %collective-permute-done.3.refs_5_ = bf16[272,128]{1,0:T(8,128)(2,1)S(1)} collective-permute-done((bf16[272,128]{1,0:T(8,128)(2,1)}, bf16[272,128]{1,0:T(8,128)(2,1)S(1)}, u32[]{:S(2)}, u32[]{:S(2)}) %collective-permute-start.3) | collective-permute-done | bytes 69664 | tf_op jit(solution)/shard_map/ppermute | solution.py:477
  16.3 0.0 copy-start.10
  16.3 0.0 collective-permute-done.2.refs_4_
  16.3 0.0 copy-start.11
  16.3 0.0 copy-done.7
  16.3 0.0 copy-done.8
  16.3 0.0 copy-done.9
  16.3 0.6 copy-done.10
  16.9 0.0 copy-done.11
  16.9 22.3 %shard_map.164 = (f32[544,128]{1,0:T(8,128)}, bf16[864,128]{1,0:T(8,128)(2,1)}, f32[160,128]{1,0:T(8,128)}, f32[16,128]{1,0:T(8,128)}, f32[16,128]{1,0:T(8,128)}) custom-call(s32[2]{0:T(128)} %pad_add_fusion.where_ref, s32[1,1]{1,0:T(1,128)S(6)} %copy.21.count_ref, s32[1,1,56]{2,1,0:T(1,128)} %tower_ref.1, s32[1,1,56]{2,1,0:T(1,128)} %plate_ref.1, ...), custom_call_target="tpu_custom_call" | custom-call | tf_op jit(solution)/shard_map/pallas_call | solution.py:541
  39.2 0.1 collective-permute-start.5
  39.3 1.6 %collective-permute-done.5.got_ref = bf16[864,128]{1,0:T(8,128)(2,1)S(1)} collective-permute-done((bf16[864,128]{1,0:T(8,128)(2,1)}, bf16[864,128]{1,0:T(8,128)(2,1)S(1)}, u32[]{:S(2)}, u32[]{:S(2)}) %collective-permute-start.5) | collective-permute-done | bytes 221216 | tf_op jit(solution)/shard_map/ppermute | solution.py:477
  41.0 0.0 copy-start.1
  41.0 0.7 copy-done.1
  41.6 1.8 %shard_map.165 = (f32[272,128]{1,0:T(8,128)}, bf16[592,128]{1,0:T(8,128)(2,1)}, f32[176,128]{1,0:T(8,128)}) custom-call(f32[544,128]{1,0:T(8,128)} %get-tuple-element.26.kept_ref, f32[160,128]{1,0:T(8,128)} %get-tuple-element.27.weight_ref, bf16[864,128]{1,0:T(8,128)(2,1)} %copy-done.1, f32[16,128]{1,0:T(8,128)} %get-tuple-element.29.near_ref), custom_call_target="tpu_custom_call" | custom-call | tf_op jit(solution)/shard_map/pallas_call | solution.py:603
  43.5 21.6 %collective-permute-start.6 = (bf16[592,128]{1,0:T(8,128)(2,1)}, bf16[592,128]{1,0:T(8,128)(2,1)S(1)}, u32[]{:S(2)}, u32[]{:S(2)}) collective-permute-start(bf16[592,128]{1,0:T(8,128)(2,1)} %get-tuple-element.31), channel_id=1, source_target_pairs={{0,2},{1,3},{2,0},{3,1},{4,6},{5,7},{6,4},{7,5},{8,10},{9,11},{10,... | collective-permute-start | bytes 454664 | tf_op jit(solution)/shard_map/ppermute | solution.py:477
  65.1 0.0 copy-start.13
  65.1 2.2 %collective-permute-start.8 = (f32[176,128]{1,0:T(8,128)}, f32[176,128]{1,0:T(8,128)S(1)}, u32[]{:S(2)}, u32[]{:S(2)}) collective-permute-start(f32[176,128]{1,0:T(8,128)} %get-tuple-element.32.weight_ref), channel_id=1, source_target_pairs={{0,6},{1,7},{2,4},{3,5},{4,2},{5,3},{6,0},{7,1},{8,14},{9,15},{10,... | collective-permute-start | bytes 270344 | tf_op jit(solution)/shard_map/ppermute | solution.py:477
  67.3 0.0 collective-permute-start.7
  67.3 4.1 %collective-permute-done.8.both_ref = f32[176,128]{1,0:T(8,128)S(1)} collective-permute-done((f32[176,128]{1,0:T(8,128)}, f32[176,128]{1,0:T(8,128)S(1)}, u32[]{:S(2)}, u32[]{:S(2)}) %collective-permute-start.8) | collective-permute-done | bytes 90144 | tf_op jit(solution)/shard_map/ppermute | solution.py:477
  71.4 0.0 copy-start.2
  71.4 0.6 collective-permute-done.7.near_ref
  72.0 0.0 copy-start.3
  72.0 0.0 collective-permute-done.6.got_ref
  72.0 0.0 copy-done.2
  72.0 0.6 copy-done.3
  72.6 0.0 copy-start
  72.6 0.7 copy-done
  73.3 1.7 %shard_map.166 = (f32[160,128]{1,0:T(8,128)}, f32[16,128]{1,0:T(8,128)}) custom-call(f32[176,128]{1,0:T(8,128)} %get-tuple-element.32.weight_ref, bf16[592,128]{1,0:T(8,128)(2,1)} %copy-done, f32[176,128]{1,0:T(8,128)} %copy-done.3, f32[176,128]{1,0:T(8,128)} %copy-done.2), custom_call_target="tpu_custom_call" | custom-call | tf_op jit(solution)/shard_map/pallas_call | solution.py:615
  75.0 0.6 collective-permute-start.12
  75.6 1.0 %collective-permute-start.11 = (f32[160,128]{1,0:T(8,128)}, f32[160,128]{1,0:T(8,128)S(1)}, u32[]{:S(2)}, u32[]{:S(2)}) collective-permute-start(f32[160,128]{1,0:T(8,128)} %get-tuple-element.37.refs_0_), channel_id=1, source_target_pairs={{0,16},{4,20},{8,24},{12,28},{16,0},{20,4},{24,8},{28,12},{1,17},{... | collective-permute-start | bytes 245768 | tf_op jit(solution)/shard_map/ppermute | solution.py:477
  76.6 2.7 %collective-permute-start.10 = (f32[160,128]{1,0:T(8,128)}, f32[160,128]{1,0:T(8,128)S(1)}, u32[]{:S(2)}, u32[]{:S(2)}) collective-permute-start(f32[160,128]{1,0:T(8,128)} %get-tuple-element.37.refs_0_), channel_id=1, source_target_pairs={{0,8},{4,12},{8,0},{12,4},{16,24},{20,28},{24,16},{28,20},{1,9},{5... | collective-permute-start | bytes 245768 | tf_op jit(solution)/shard_map/ppermute | solution.py:477
  79.4 0.0 copy-done.13
  79.4 1.5 %collective-permute-start.9 = (f32[16,128]{1,0:T(8,128)S(1)}, f32[16,128]{1,0:T(8,128)S(1)}, u32[]{:S(2)}, u32[]{:S(2)}) collective-permute-start(f32[16,128]{1,0:T(8,128)S(1)} %copy-done.13), channel_id=1, source_target_pairs={{0,28},{4,8},{8,4},{12,16},{16,12},{20,24},{24,20},{28,0},{1,29},{... | collective-permute-start | bytes 24584 | tf_op jit(solution)/shard_map/ppermute | solution.py:477
  80.9 4.9 %collective-permute-done.9.far_ref = f32[16,128]{1,0:T(8,128)S(1)} collective-permute-done((f32[16,128]{1,0:T(8,128)S(1)}, f32[16,128]{1,0:T(8,128)S(1)}, u32[]{:S(2)}, u32[]{:S(2)}) %collective-permute-start.9) | collective-permute-done | bytes 8224 | tf_op jit(solution)/shard_map/ppermute | solution.py:477
  85.8 0.0 copy-start.12
  85.8 0.6 copy-done.12
  86.4 1.7 %shard_map.167 = (f32[1,256,128]{2,1,0:T(8,128)}, f32[3,1,256]{2,1,0:T(1,128)}) custom-call(s32[1,1]{1,0:T(1,128)S(6)} %copy.20.count_ref, f32[272,128]{1,0:T(8,128)} %get-tuple-element.30.block_ref, bf16[592,128]{1,0:T(8,128)(2,1)} %copy-done, f32[16,128]{1,0:T(8,128)} %get-tuple-element.33.near_ref, f32[16,128]{1,0:T(8,128)} %copy-done.12), custom_call_target="tpu_custom_call" | custom-call | tf_op jit(solution)/shard_map/pallas_call | solution.py:626
  88.0 0.0 collective-permute-done.12.refs_3_
  88.0 0.0 copy-start.4
  88.0 0.0 collective-permute-done.11.refs_2_
  88.1 0.0 copy-start.5
  88.1 0.0 collective-permute-done.10.refs_1_
  88.1 0.6 copy-done.4
  88.7 0.0 copy-done.5
  88.7 0.0 copy-start.6
  88.7 0.6 copy-done.6
  89.3 1.8 %shard_map.168 = (f32[16,128]{1,0:T(8,128)}, f32[1,128]{1,0:T(1,128)}, f32[128,128]{1,0:T(8,128)}, f32[1,128]{1,0:T(1,128)}) custom-call(f32[160,128]{1,0:T(8,128)} %get-tuple-element.37.refs_0_, f32[160,128]{1,0:T(8,128)} %copy-done.6, f32[160,128]{1,0:T(8,128)} %copy-done.5, f32[160,128]{1,0:T(8,128)} %copy-done.4), custom_call_target="tpu_custom_call" | custom-call | tf_op jit(solution)/shard_map/pallas_call | solution.py:631
Async XLA Ops:
  4.1 9.1 %collective-permute-start.1 = (bf16[272,128]{1,0:T(8,128)(2,1)}, bf16[272,128]{1,0:T(8,128)(2,1)S(1)}, u32[]{:S(2)}, u32[]{:S(2)}) collective-permute-start(bf16[272,128]{1,0:T(8,128)(2,1)} %get-tuple-element.24.refs_0_), channel_id=1, source_target_pairs={{0,28},{4,8},{8,4},{12,16},{16,12},{20,24},{24,20},{28,0},{1,29},{... | collective-permute-start | bytes 208904 | tf_op jit(solution)/shard_map/ppermute | solution.py:477
  10.1 4.5 %collective-permute-start = (bf16[272,128]{1,0:T(8,128)(2,1)}, bf16[272,128]{1,0:T(8,128)(2,1)S(1)}, u32[]{:S(2)}, u32[]{:S(2)}) collective-permute-start(bf16[272,128]{1,0:T(8,128)(2,1)} %get-tuple-element.24.refs_0_), channel_id=1, source_target_pairs={{0,4},{4,0},{8,12},{12,8},{16,20},{20,16},{24,28},{28,24},{1,5},{5... | collective-permute-start | bytes 208904 | tf_op jit(solution)/shard_map/ppermute | solution.py:477
  10.1 4.6 %collective-permute-start.4 = (bf16[272,128]{1,0:T(8,128)(2,1)}, bf16[272,128]{1,0:T(8,128)(2,1)S(1)}, u32[]{:S(2)}, u32[]{:S(2)}) collective-permute-start(bf16[272,128]{1,0:T(8,128)(2,1)} %get-tuple-element.25.refs_3_), channel_id=1, source_target_pairs={{0,3},{1,2},{2,1},{3,0},{4,7},{5,6},{6,5},{7,4},{8,11},{9,10},{10,... | collective-permute-start | bytes 208904 | tf_op jit(solution)/shard_map/ppermute | solution.py:477
  10.8 5.5 %collective-permute-start.3 = (bf16[272,128]{1,0:T(8,128)(2,1)}, bf16[272,128]{1,0:T(8,128)(2,1)S(1)}, u32[]{:S(2)}, u32[]{:S(2)}) collective-permute-start(bf16[272,128]{1,0:T(8,128)(2,1)} %get-tuple-element.25.refs_3_), channel_id=1, source_target_pairs={{0,2},{1,3},{2,0},{3,1},{4,6},{5,7},{6,4},{7,5},{8,10},{9,11},{10,... | collective-permute-start | bytes 208904 | tf_op jit(solution)/shard_map/ppermute | solution.py:477
  11.6 4.7 %collective-permute-start.2 = (bf16[272,128]{1,0:T(8,128)(2,1)}, bf16[272,128]{1,0:T(8,128)(2,1)S(1)}, u32[]{:S(2)}, u32[]{:S(2)}) collective-permute-start(bf16[272,128]{1,0:T(8,128)(2,1)} %get-tuple-element.25.refs_3_), channel_id=1, source_target_pairs={{0,1},{1,0},{2,3},{3,2},{4,5},{5,4},{6,7},{7,6},{8,9},{9,8},{10,11... | collective-permute-start | bytes 208904 | tf_op jit(solution)/shard_map/ppermute | solution.py:477
  13.2 3.1 %copy-start.7 = (bf16[272,128]{1,0:T(8,128)(2,1)}, bf16[272,128]{1,0:T(8,128)(2,1)S(1)}, u32[]{:S(2)}) copy-start(bf16[272,128]{1,0:T(8,128)(2,1)S(1)} %collective-permute-done.1.refs_2_) | copy-start | bytes 208900
  14.6 1.7 %copy-start.8 = (bf16[272,128]{1,0:T(8,128)(2,1)}, bf16[272,128]{1,0:T(8,128)(2,1)S(1)}, u32[]{:S(2)}) copy-start(bf16[272,128]{1,0:T(8,128)(2,1)S(1)} %collective-permute-done.refs_1_) | copy-start | bytes 208900
  14.7 1.6 %copy-start.9 = (bf16[272,128]{1,0:T(8,128)(2,1)}, bf16[272,128]{1,0:T(8,128)(2,1)S(1)}, u32[]{:S(2)}) copy-start(bf16[272,128]{1,0:T(8,128)(2,1)S(1)} %collective-permute-done.4.refs_6_) | copy-start | bytes 208900
  16.3 0.6 copy-start.10
  16.3 0.7 copy-start.11
  39.2 1.7 %collective-permute-start.5 = (bf16[864,128]{1,0:T(8,128)(2,1)}, bf16[864,128]{1,0:T(8,128)(2,1)S(1)}, u32[]{:S(2)}, u32[]{:S(2)}) collective-permute-start(bf16[864,128]{1,0:T(8,128)(2,1)} %get-tuple-element.28), channel_id=1, source_target_pairs={{0,1},{1,0},{2,3},{3,2},{4,5},{5,4},{6,7},{7,6},{8,9},{9,8},{10,11... | collective-permute-start | bytes 663560 | tf_op jit(solution)/shard_map/ppermute | solution.py:477
  41.0 0.7 copy-start.1
  43.5 28.5 %collective-permute-start.6 = (bf16[592,128]{1,0:T(8,128)(2,1)}, bf16[592,128]{1,0:T(8,128)(2,1)S(1)}, u32[]{:S(2)}, u32[]{:S(2)}) collective-permute-start(bf16[592,128]{1,0:T(8,128)(2,1)} %get-tuple-element.31), channel_id=1, source_target_pairs={{0,2},{1,3},{2,0},{3,1},{4,6},{5,7},{6,4},{7,5},{8,10},{9,11},{10,... | collective-permute-start | bytes 454664 | tf_op jit(solution)/shard_map/ppermute | solution.py:477
  65.1 14.3 %copy-start.13 = (f32[16,128]{1,0:T(8,128)S(1)}, f32[16,128]{1,0:T(8,128)}, u32[]{:S(2)}) copy-start(f32[16,128]{1,0:T(8,128)} %get-tuple-element.34) | copy-start | bytes 24580
  65.1 6.3 %collective-permute-start.8 = (f32[176,128]{1,0:T(8,128)}, f32[176,128]{1,0:T(8,128)S(1)}, u32[]{:S(2)}, u32[]{:S(2)}) collective-permute-start(f32[176,128]{1,0:T(8,128)} %get-tuple-element.32.weight_ref), channel_id=1, source_target_pairs={{0,6},{1,7},{2,4},{3,5},{4,2},{5,3},{6,0},{7,1},{8,14},{9,15},{10,... | collective-permute-start | bytes 270344 | tf_op jit(solution)/shard_map/ppermute | solution.py:477
  67.3 4.7 %collective-permute-start.7 = (f32[176,128]{1,0:T(8,128)}, f32[176,128]{1,0:T(8,128)S(1)}, u32[]{:S(2)}, u32[]{:S(2)}) collective-permute-start(f32[176,128]{1,0:T(8,128)} %get-tuple-element.32.weight_ref), channel_id=1, source_target_pairs={{0,4},{4,0},{8,12},{12,8},{16,20},{20,16},{24,28},{28,24},{1,5},{5... | collective-permute-start | bytes 270344 | tf_op jit(solution)/shard_map/ppermute | solution.py:477
  71.4 0.6 copy-start.2
  72.0 0.6 copy-start.3
  72.6 0.7 copy-start
  75.0 13.1 %collective-permute-start.12 = (f32[160,128]{1,0:T(8,128)}, f32[160,128]{1,0:T(8,128)S(1)}, u32[]{:S(2)}, u32[]{:S(2)}) collective-permute-start(f32[160,128]{1,0:T(8,128)} %get-tuple-element.37.refs_0_), channel_id=1, source_target_pairs={{0,24},{4,28},{8,16},{12,20},{16,8},{20,12},{24,0},{28,4},{1,25},{... | collective-permute-start | bytes 245768 | tf_op jit(solution)/shard_map/ppermute | solution.py:477
  75.6 12.4 %collective-permute-start.11 = (f32[160,128]{1,0:T(8,128)}, f32[160,128]{1,0:T(8,128)S(1)}, u32[]{:S(2)}, u32[]{:S(2)}) collective-permute-start(f32[160,128]{1,0:T(8,128)} %get-tuple-element.37.refs_0_), channel_id=1, source_target_pairs={{0,16},{4,20},{8,24},{12,28},{16,0},{20,4},{24,8},{28,12},{1,17},{... | collective-permute-start | bytes 245768 | tf_op jit(solution)/shard_map/ppermute | solution.py:477
  76.6 11.4 %collective-permute-start.10 = (f32[160,128]{1,0:T(8,128)}, f32[160,128]{1,0:T(8,128)S(1)}, u32[]{:S(2)}, u32[]{:S(2)}) collective-permute-start(f32[160,128]{1,0:T(8,128)} %get-tuple-element.37.refs_0_), channel_id=1, source_target_pairs={{0,8},{4,12},{8,0},{12,4},{16,24},{20,28},{24,16},{28,20},{1,9},{5... | collective-permute-start | bytes 245768 | tf_op jit(solution)/shard_map/ppermute | solution.py:477
  79.4 6.4 %collective-permute-start.9 = (f32[16,128]{1,0:T(8,128)S(1)}, f32[16,128]{1,0:T(8,128)S(1)}, u32[]{:S(2)}, u32[]{:S(2)}) collective-permute-start(f32[16,128]{1,0:T(8,128)S(1)} %copy-done.13), channel_id=1, source_target_pairs={{0,28},{4,8},{8,4},{12,16},{16,12},{20,24},{24,20},{28,0},{1,29},{... | collective-permute-start | bytes 24584 | tf_op jit(solution)/shard_map/ppermute | solution.py:477
  85.8 0.6 copy-start.12
  88.0 0.6 copy-start.4
  88.1 0.6 copy-start.5
  88.7 0.6 copy-start.6

commit v4 on v3

--- a/solution.py
+++ b/solution.py
@@ -12,7 +12,7 @@
 TILE = 32
 LANES = 128
 PART = 32
-TILES = 4
+TILES = 8
 
 box_side = 1.0
 brick_height = 1.0
@@ -74,8 +74,11 @@
     live = iota((atoms, width), 0) < count_ref[0, 0]
     rows = atoms // LANES
     extra = out_feat.shape[0] - atoms
+    spots = pos_ref[...].astype(F32)
     parts = [
-        pos_ref[axis, :, r * LANES : (r + 1) * LANES] for axis in range(3) for r in range(rows)
+        spots[axis : axis + 1, r * LANES : (r + 1) * LANES]
+        for axis in range(3)
+        for r in range(rows)
     ]
     parts.append(jnp.zeros((extra - len(parts), width), F32))
     tail = jnp.concatenate(parts, axis=0).astype(BF16)
@@ -133,21 +136,16 @@
     far_slot = 2 * odd
     sources = ((far_adj, far_slot), (own_adj, 1), (near_adj, near_slot))
 
-    pick_recv = one_hot(iota((TILE, pairs), 0) == iota((TILE, pairs), 1) // TILE)
     pick_send = one_hot(iota((TILE, LANES), 0) == iota((TILE, LANES), 1) % TILE)
     for source, slot in sources:
-
-        def widen_adj(half, carry, source=source, slot=slot):
-            for t in range(4):
-                t = 4 * half + t
-                start = pl.multiple_of(t * TILE, TILE)
-                part = source[pl.ds(start, TILE), :].astype(F32).T.astype(BF16)
-                wide = nn(part, pick_recv)
+        for half in range(rows):
+            turned = source[half * LANES : (half + 1) * LANES].astype(F32).T
+            for q in range(groups):
                 for c in range(chunks):
-                    adj_wide[slot * per_brick + t, c] = wide[:, c * LANES : (c + 1) * LANES]
-            return carry
-
-        lax.fori_loop(0, per_brick // 4, widen_adj, 0)
+                    lane = q * TILE + c * groups + iota((width, LANES), 1) // TILE
+                    adj_wide[slot * per_brick + half * groups + q, c] = jnp.take_along_axis(
+                        turned, lane, axis=1
+                    )
     for q in range(groups):
         pick = one_hot(iota((LANES, pairs), 0) == q * TILE + iota((LANES, pairs), 1) // TILE)
         for source, slot in sources:
@@ -162,14 +160,13 @@
         brick = plate_at ^ step
 
         def widen_feat(half, carry, source=source, brick=brick):
-            for t in range(4):
-                t = 4 * half + t
+            for t in range(per_brick):
                 start = pl.multiple_of(t * TILE, TILE)
                 part = source[pl.ds(start, TILE), :].astype(F32).T.astype(BF16)
                 feat_wide[brick * per_brick + t] = nn(part, pick_send)
             return carry
 
-        lax.fori_loop(0, per_brick // 4, widen_feat, 0)
+        lax.fori_loop(0, 1, widen_feat, 0)
 
     w_rbf = w_rbf_ref[...].astype(F32)
     half_bias = [piece.astype(F32) for piece in split(0.5 * b_rbf_ref[...], 3)]
@@ -384,8 +381,7 @@
         kind = target.dtype
 
         def fold_feat(half, carry, brick=brick, at=at, target=target, kind=kind):
-            for t in range(4):
-                t = 4 * half + t
+            for t in range(per_brick):
                 pieces = split(grad_feat[brick * per_brick + t], 2)
                 start = pl.multiple_of(at + t * TILE, 16)
                 target[pl.ds(start, TILE), :] = (
@@ -393,7 +389,7 @@
                 ).astype(kind)
             return carry
 
-        lax.fori_loop(0, per_brick // 4, fold_feat, 0)
+        lax.fori_loop(0, 1, fold_feat, 0)
         total = jnp.zeros((spots, LANES), F32)
         for q in range(groups):
             summed = nn_split(jnp.sum(grad_send[brick, q], axis=1), same_slot)
@@ -435,21 +431,12 @@
     weight_out[count:] = near_ref[...]
 
 
-def join_kernel(weight_ref, got_ref, near_ref, both_ref, weight_out, near_out):
-    count = weight_out.shape[0]
-    start = got_ref.shape[0] - 2 * count
-    got = got_ref[start:].astype(F32)
-    weights = weight_ref[:count] + got[:count] + got[count:]
-    weight_out[...] = weights + (near_ref[:count] + both_ref[:count])
-    near_out[...] = near_ref[count:]
-
-
 def finish_kernel(atoms, count_ref, block_ref, got_ref, near_ref, far_ref, feat_out, pos_out):
     block, width = block_ref.shape
     live = iota((atoms, width), 0) < count_ref[0, 0]
     total = block_ref[...] + got_ref[:block].astype(F32)
     feat_out[0] = jnp.where(live, total[:atoms], 0.0)
-    spots = total[atoms:] + near_ref[...] + far_ref[...]
+    spots = total[atoms:] + near_ref[near_ref.shape[0] - block + atoms :] + far_ref[...]
     rows = atoms // LANES
     for axis in range(3):
         for r in range(rows):
@@ -531,7 +518,7 @@
 
     feat_block, adj_block = call(
         pack_kernel, [((block, width), BF16)] * 2, [SMEM, VMEM, VMEM, VMEM]
-    )(atom_counts, features, adjoint, positions.astype(F32))
+    )(atom_counts, features, adjoint, positions.reshape(3, atoms))
     peers = [swap(feat_block, "plate", across(step)) for step in range(1, plate_count)]
     near_adj = swap(adj_block, "tower", across(1))
     far_adj = swap(adj_block, "tower", beyond)
@@ -612,9 +599,9 @@
     both = swap(weights, ("tower", "plate"), across(plate_count + 2))
     near = swap(weights, "tower", across(1))
     got = swap(send, "plate", across(2))
-    weights, got_near = call(
-        join_kernel, [((weight_rows, width), F32), ((spot_rows, width), F32)], [VMEM] * 4
-    )(weights, got, near, both)
+    high, low = (got[-n * weight_rows :][:weight_rows].astype(F32) for n in (2, 1))
+    weights = weights[:weight_rows] + high + low
+    weights = weights + (near[:weight_rows] + both[:weight_rows])
 
     bits = 2
     parts = [weights]
@@ -627,7 +614,7 @@
         functools.partial(finish_kernel, atoms),
         [((1, atoms, width), F32), ((3, 1, atoms), F32)],
         [SMEM] + [VMEM] * 4,
-    )(atom_counts, keep, got, got_near, got_far)
+    )(atom_counts, keep, got, near, got_far)
     out_wr, out_br, out_wf, out_bf = call(
         weight_kernel,
         [((nbasis, width), F32), ((1, width), F32), ((width, width), F32), ((1, width), F32)],

time: 91.5 us -> 83.1 us (0.908)
  Pallas kernels: 30.8 us -> 26.8 us
  starting transfers between devices: 37.6 us -> 34.6 us
  local copies, waits for them, and re-layouts: 4.47 us -> 3.22 us
    ppermute x13, starting transfers between devices: 37.6 us -> 34.6 us  [swap(): lax.ppermute(value, axis, [(i, route(i) % size) for i in range(size)])]
    pallas_call x1, Pallas kernels: 22.3 us -> 19.9 us  [local(): call(functools.partial(tile_kernel, plate_count), [((half * block, width)...]
    pallas_call x1 -> x0, Pallas kernels: 1.71 us -> none  [local(): call(join_kernel, [((weight_rows, width), F32), ((spot_rows, width), F32)...]
    convert_element_type x1 -> x0, other arithmetic: 1.26 us -> none  [local(): positions.astype(F32)]
    unnamed x28, local copies, waits for them, and re-layouts: 4.47 us -> 3.22 us
    add x0 -> x1, other arithmetic: none -> 0.99 us  [local(): weights = weights + (near[:weight_rows] + both[:weight_rows])]
where the time goes in v4:
time: 83.1 us; the launch traced here: 82.7 us
  starting transfers between devices  34.6 us (42%)
  Pallas kernels  26.8 us (32%)
  waiting for transfers between devices  14.4 us (17%)
  local copies, waits for them, and re-layouts  3.22 us (4%)
  between operations  2.04 us (2%)
  other arithmetic  1.57 us (2%)
    ppermute x13, starting transfers between devices, swap(): lax.ppermute(value, axis, [(i, route(i) % size) for i in range(size)])  34.6 us
    pallas_call x1, Pallas kernels, local(): call(functools.partial(tile_kernel, plate_count), [((half * block, width)...  19.9 us
    ppermute x13, waiting for transfers between devices, swap(): lax.ppermute(value, axis, [(i, route(i) % size) for i in range(size)])  14.4 us
    unnamed x28, local copies, waits for them, and re-layouts  3.22 us
    pallas_call x1, Pallas kernels, local(): call(functools.partial(add_kernel, cut), [((cut, width), F32), ((held - c...  1.83 us
    pallas_call x1, Pallas kernels, local(): call(weight_kernel, [((nbasis, width), F32), ((1, width), F32), ((width,...  1.79 us
    pallas_call x1, Pallas kernels, local(): call(functools.partial(finish_kernel, atoms), [((1, atoms, width), F32),...  1.71 us
  transfers between devices with their start and end apart: 13, of which 7 were waited for; matrix products, arithmetic and copies ran while one was open for 1% of the time, Pallas kernels for 2%

profile of v4, /device:TPU:0, one launch (start us, length us, event | category | flops | bytes accessed | tf_op | source)
XLA Modules:
  0.0 82.7 jit_solution(4697955707467018480)
XLA Ops:
  1.3 1.6 %shard_map.163 = (bf16[272,128]{1,0:T(8,128)(2,1)}, bf16[272,128]{1,0:T(8,128)(2,1)}) custom-call(s32[1,1]{1,0:T(1,128)S(6)} %copy.18.count_ref, bf16[1,256,128]{2,1,0:T(8,128)(2,1)} %feat_ref.1, bf16[1,256,128]{2,1,0:T(8,128)(2,1)} %adj_ref.1, bf16[3,256]{1,0:T(4,128)(2,1)} %bitcast.7), custom_call_target="tpu_custom_call" | custom-call | tf_op jit(solution)/shard_map/pallas_call | solution.py:519
  2.8 6.0 %collective-permute-start.1 = (bf16[272,128]{1,0:T(8,128)(2,1)}, bf16[272,128]{1,0:T(8,128)(2,1)S(1)}, u32[]{:S(2)}, u32[]{:S(2)}) collective-permute-start(bf16[272,128]{1,0:T(8,128)(2,1)} %get-tuple-element.22.refs_0_), channel_id=1, source_target_pairs={{0,28},{4,8},{8,4},{12,16},{16,12},{20,24},{24,20},{28,0},{1,29},{... | collective-permute-start | bytes 208904 | tf_op jit(solution)/shard_map/ppermute | solution.py:464
  8.8 0.0 collective-permute-start
  8.8 0.7 collective-permute-start.4
  9.5 0.8 %collective-permute-start.3 = (bf16[272,128]{1,0:T(8,128)(2,1)}, bf16[272,128]{1,0:T(8,128)(2,1)S(1)}, u32[]{:S(2)}, u32[]{:S(2)}) collective-permute-start(bf16[272,128]{1,0:T(8,128)(2,1)} %get-tuple-element.23.refs_3_), channel_id=1, source_target_pairs={{0,2},{1,3},{2,0},{3,1},{4,6},{5,7},{6,4},{7,5},{8,10},{9,11},{10,... | collective-permute-start | bytes 208904 | tf_op jit(solution)/shard_map/ppermute | solution.py:464
  10.4 0.3 collective-permute-start.2
  11.4 0.6 pad_add_fusion.where_ref
  11.9 0.0 collective-permute-done.1.refs_2_
  11.9 0.0 copy-start.7
  11.9 1.4 %collective-permute-done.refs_1_ = bf16[272,128]{1,0:T(8,128)(2,1)S(1)} collective-permute-done((bf16[272,128]{1,0:T(8,128)(2,1)}, bf16[272,128]{1,0:T(8,128)(2,1)S(1)}, u32[]{:S(2)}, u32[]{:S(2)}) %collective-permute-start) | collective-permute-done | bytes 69664 | tf_op jit(solution)/shard_map/ppermute | solution.py:464
  13.4 0.0 copy-start.8
  13.4 0.1 collective-permute-done.4.refs_6_
  13.5 0.0 copy-start.9
  13.5 1.6 %collective-permute-done.3.refs_5_ = bf16[272,128]{1,0:T(8,128)(2,1)S(1)} collective-permute-done((bf16[272,128]{1,0:T(8,128)(2,1)}, bf16[272,128]{1,0:T(8,128)(2,1)S(1)}, u32[]{:S(2)}, u32[]{:S(2)}) %collective-permute-start.3) | collective-permute-done | bytes 69664 | tf_op jit(solution)/shard_map/ppermute | solution.py:464
  15.0 0.0 copy-start.10
  15.0 0.0 collective-permute-done.2.refs_4_
  15.0 0.0 copy-start.11
  15.0 0.0 copy-done.7
  15.0 0.0 copy-done.8
  15.1 0.0 copy-done.9
  15.1 0.6 copy-done.10
  15.6 0.1 copy-done.11
  15.7 19.9 %shard_map.164 = (f32[544,128]{1,0:T(8,128)}, bf16[864,128]{1,0:T(8,128)(2,1)}, f32[160,128]{1,0:T(8,128)}, f32[16,128]{1,0:T(8,128)}, f32[16,128]{1,0:T(8,128)}) custom-call(s32[2]{0:T(128)} %pad_add_fusion.where_ref, s32[1,1]{1,0:T(1,128)S(6)} %copy.19.count_ref, s32[1,1,56]{2,1,0:T(1,128)} %tower_ref.1, s32[1,1,56]{2,1,0:T(1,128)} %plate_ref.1, ...), custom_call_target="tpu_custom_call" | custom-call | tf_op jit(solution)/shard_map/pallas_call | solution.py:528
  35.6 0.1 collective-permute-start.5
  35.7 1.7 %collective-permute-done.5.got_ref = bf16[864,128]{1,0:T(8,128)(2,1)S(1)} collective-permute-done((bf16[864,128]{1,0:T(8,128)(2,1)}, bf16[864,128]{1,0:T(8,128)(2,1)S(1)}, u32[]{:S(2)}, u32[]{:S(2)}) %collective-permute-start.5) | collective-permute-done | bytes 221216 | tf_op jit(solution)/shard_map/ppermute | solution.py:464
  37.4 0.0 copy-start.3
  37.4 0.7 copy-done.3
  38.1 1.8 %shard_map.165 = (f32[272,128]{1,0:T(8,128)}, bf16[592,128]{1,0:T(8,128)(2,1)}, f32[176,128]{1,0:T(8,128)}) custom-call(f32[544,128]{1,0:T(8,128)} %get-tuple-element.24.kept_ref, f32[160,128]{1,0:T(8,128)} %get-tuple-element.25.weight_ref, bf16[864,128]{1,0:T(8,128)(2,1)} %copy-done.3, f32[16,128]{1,0:T(8,128)} %get-tuple-element.27.near_ref), custom_call_target="tpu_custom_call" | custom-call | tf_op jit(solution)/shard_map/pallas_call | solution.py:590
  39.9 18.4 %collective-permute-start.6 = (bf16[592,128]{1,0:T(8,128)(2,1)}, bf16[592,128]{1,0:T(8,128)(2,1)S(1)}, u32[]{:S(2)}, u32[]{:S(2)}) collective-permute-start(bf16[592,128]{1,0:T(8,128)(2,1)} %get-tuple-element.29), channel_id=1, source_target_pairs={{0,2},{1,3},{2,0},{3,1},{4,6},{5,7},{6,4},{7,5},{8,10},{9,11},{10,... | collective-permute-start | bytes 454664 | tf_op jit(solution)/shard_map/ppermute | solution.py:464
  58.3 0.0 copy-start.13
  58.3 2.2 %collective-permute-start.9 = (f32[176,128]{1,0:T(8,128)}, f32[176,128]{1,0:T(8,128)S(1)}, u32[]{:S(2)}, u32[]{:S(2)}) collective-permute-start(f32[176,128]{1,0:T(8,128)} %get-tuple-element.30), channel_id=1, source_target_pairs={{0,6},{1,7},{2,4},{3,5},{4,2},{5,3},{6,0},{7,1},{8,14},{9,15},{10,... | collective-permute-start | bytes 270344 | tf_op jit(solution)/shard_map/ppermute | solution.py:464
  60.5 0.0 collective-permute-start.7
  60.5 4.1 %collective-permute-done.9 = f32[176,128]{1,0:T(8,128)S(1)} collective-permute-done((f32[176,128]{1,0:T(8,128)}, f32[176,128]{1,0:T(8,128)S(1)}, u32[]{:S(2)}, u32[]{:S(2)}) %collective-permute-start.9) | collective-permute-done | bytes 90144 | tf_op jit(solution)/shard_map/ppermute | solution.py:464
  64.6 0.7 collective-permute-done.7.near_ref
  65.2 0.0 copy-start.1
  65.2 0.0 collective-permute-done.6.got_ref
  65.2 0.0 copy-start
  65.2 1.0 %fusion.refs_0_ = f32[160,128]{1,0:T(8,128)S(1)} fusion(f32[176,128]{1,0:T(8,128)S(1)} %collective-permute-done.9, f32[176,128]{1,0:T(8,128)S(1)} %collective-permute-done.7.near_ref, f32[176,128]{1,0:T(8,128)} %get-tuple-element.30, bf16[592,128]{1,0:T(8,128)(2,1)S(1)} %collective-permute-done.6.got_ref), kind=kLoop, calls=%fused_computation.1 | loop fusion | flops 122880 | bytes 409600 | tf_op jit(solution)/shard_map/add | solution.py:604
  66.2 0.0 copy-done.1
  66.2 0.0 copy-done
  66.2 0.0 copy-start.2
  66.3 0.7 collective-permute-start.12
  67.0 1.1 %collective-permute-start.11 = (f32[160,128]{1,0:T(8,128)S(1)}, f32[160,128]{1,0:T(8,128)S(1)}, u32[]{:S(2)}, u32[]{:S(2)}) collective-permute-start(f32[160,128]{1,0:T(8,128)S(1)} %fusion.refs_0_), channel_id=1, source_target_pairs={{0,16},{4,20},{8,24},{12,28},{16,0},{20,4},{24,8},{28,12},{1,17},{... | collective-permute-start | bytes 245768 | tf_op jit(solution)/shard_map/ppermute | solution.py:464
  68.1 2.7 %collective-permute-start.10 = (f32[160,128]{1,0:T(8,128)S(1)}, f32[160,128]{1,0:T(8,128)S(1)}, u32[]{:S(2)}, u32[]{:S(2)}) collective-permute-start(f32[160,128]{1,0:T(8,128)S(1)} %fusion.refs_0_), channel_id=1, source_target_pairs={{0,8},{4,12},{8,0},{12,4},{16,24},{20,28},{24,16},{28,20},{1,9},{5... | collective-permute-start | bytes 245768 | tf_op jit(solution)/shard_map/ppermute | solution.py:464
  70.7 0.0 copy-done.13
  70.7 1.6 %collective-permute-start.8 = (f32[16,128]{1,0:T(8,128)S(1)}, f32[16,128]{1,0:T(8,128)S(1)}, u32[]{:S(2)}, u32[]{:S(2)}) collective-permute-start(f32[16,128]{1,0:T(8,128)S(1)} %copy-done.13), channel_id=1, source_target_pairs={{0,28},{4,8},{8,4},{12,16},{16,12},{20,24},{24,20},{28,0},{1,29},{... | collective-permute-start | bytes 24584 | tf_op jit(solution)/shard_map/ppermute | solution.py:464
  72.4 4.9 %collective-permute-done.8.far_ref = f32[16,128]{1,0:T(8,128)S(1)} collective-permute-done((f32[16,128]{1,0:T(8,128)S(1)}, f32[16,128]{1,0:T(8,128)S(1)}, u32[]{:S(2)}, u32[]{:S(2)}) %collective-permute-start.8) | collective-permute-done | bytes 8224 | tf_op jit(solution)/shard_map/ppermute | solution.py:464
  77.3 0.0 copy-start.12
  77.3 0.6 copy-done.12
  77.9 1.7 %shard_map.166 = (f32[1,256,128]{2,1,0:T(8,128)}, f32[3,1,256]{2,1,0:T(1,128)}) custom-call(s32[1,1]{1,0:T(1,128)S(6)} %copy.18.count_ref, f32[272,128]{1,0:T(8,128)} %get-tuple-element.28.block_ref, bf16[592,128]{1,0:T(8,128)(2,1)} %copy-done, f32[176,128]{1,0:T(8,128)} %copy-done.1, f32[16,128]{1,0:T(8,128)} %copy-done.12), custom_call_target="tpu_custom_call" | custom-call | tf_op jit(solution)/shard_map/pallas_call | solution.py:613
  79.6 0.0 copy-done.2
  79.6 0.0 collective-permute-done.12.refs_3_
  79.6 0.0 copy-start.4
  79.6 0.0 collective-permute-done.11.refs_2_
  79.6 0.0 copy-start.5
  79.6 0.0 collective-permute-done.10.refs_1_
  79.6 0.6 copy-done.4
  80.2 0.0 copy-done.5
  80.3 0.0 copy-start.6
  80.3 0.6 copy-done.6
  80.9 1.8 %shard_map.167 = (f32[16,128]{1,0:T(8,128)}, f32[1,128]{1,0:T(1,128)}, f32[128,128]{1,0:T(8,128)}, f32[1,128]{1,0:T(1,128)}) custom-call(f32[160,128]{1,0:T(8,128)} %copy-done.2, f32[160,128]{1,0:T(8,128)} %copy-done.6, f32[160,128]{1,0:T(8,128)} %copy-done.5, f32[160,128]{1,0:T(8,128)} %copy-done.4), custom_call_target="tpu_custom_call" | custom-call | tf_op jit(solution)/shard_map/pallas_call | solution.py:618
Async XLA Ops:
  2.8 9.1 %collective-permute-start.1 = (bf16[272,128]{1,0:T(8,128)(2,1)}, bf16[272,128]{1,0:T(8,128)(2,1)S(1)}, u32[]{:S(2)}, u32[]{:S(2)}) collective-permute-start(bf16[272,128]{1,0:T(8,128)(2,1)} %get-tuple-element.22.refs_0_), channel_id=1, source_target_pairs={{0,28},{4,8},{8,4},{12,16},{16,12},{20,24},{24,20},{28,0},{1,29},{... | collective-permute-start | bytes 208904 | tf_op jit(solution)/shard_map/ppermute | solution.py:464
  8.8 4.5 %collective-permute-start = (bf16[272,128]{1,0:T(8,128)(2,1)}, bf16[272,128]{1,0:T(8,128)(2,1)S(1)}, u32[]{:S(2)}, u32[]{:S(2)}) collective-permute-start(bf16[272,128]{1,0:T(8,128)(2,1)} %get-tuple-element.22.refs_0_), channel_id=1, source_target_pairs={{0,4},{4,0},{8,12},{12,8},{16,20},{20,16},{24,28},{28,24},{1,5},{5... | collective-permute-start | bytes 208904 | tf_op jit(solution)/shard_map/ppermute | solution.py:464
  8.8 4.6 %collective-permute-start.4 = (bf16[272,128]{1,0:T(8,128)(2,1)}, bf16[272,128]{1,0:T(8,128)(2,1)S(1)}, u32[]{:S(2)}, u32[]{:S(2)}) collective-permute-start(bf16[272,128]{1,0:T(8,128)(2,1)} %get-tuple-element.23.refs_3_), channel_id=1, source_target_pairs={{0,3},{1,2},{2,1},{3,0},{4,7},{5,6},{6,5},{7,4},{8,11},{9,10},{10,... | collective-permute-start | bytes 208904 | tf_op jit(solution)/shard_map/ppermute | solution.py:464
  9.5 5.5 %collective-permute-start.3 = (bf16[272,128]{1,0:T(8,128)(2,1)}, bf16[272,128]{1,0:T(8,128)(2,1)S(1)}, u32[]{:S(2)}, u32[]{:S(2)}) collective-permute-start(bf16[272,128]{1,0:T(8,128)(2,1)} %get-tuple-element.23.refs_3_), channel_id=1, source_target_pairs={{0,2},{1,3},{2,0},{3,1},{4,6},{5,7},{6,4},{7,5},{8,10},{9,11},{10,... | collective-permute-start | bytes 208904 | tf_op jit(solution)/shard_map/ppermute | solution.py:464
  10.4 4.7 %collective-permute-start.2 = (bf16[272,128]{1,0:T(8,128)(2,1)}, bf16[272,128]{1,0:T(8,128)(2,1)S(1)}, u32[]{:S(2)}, u32[]{:S(2)}) collective-permute-start(bf16[272,128]{1,0:T(8,128)(2,1)} %get-tuple-element.23.refs_3_), channel_id=1, source_target_pairs={{0,1},{1,0},{2,3},{3,2},{4,5},{5,4},{6,7},{7,6},{8,9},{9,8},{10,11... | collective-permute-start | bytes 208904 | tf_op jit(solution)/shard_map/ppermute | solution.py:464
  11.9 3.1 %copy-start.7 = (bf16[272,128]{1,0:T(8,128)(2,1)}, bf16[272,128]{1,0:T(8,128)(2,1)S(1)}, u32[]{:S(2)}) copy-start(bf16[272,128]{1,0:T(8,128)(2,1)S(1)} %collective-permute-done.1.refs_2_) | copy-start | bytes 208900
  13.4 1.7 %copy-start.8 = (bf16[272,128]{1,0:T(8,128)(2,1)}, bf16[272,128]{1,0:T(8,128)(2,1)S(1)}, u32[]{:S(2)}) copy-start(bf16[272,128]{1,0:T(8,128)(2,1)S(1)} %collective-permute-done.refs_1_) | copy-start | bytes 208900
  13.5 1.6 %copy-start.9 = (bf16[272,128]{1,0:T(8,128)(2,1)}, bf16[272,128]{1,0:T(8,128)(2,1)S(1)}, u32[]{:S(2)}) copy-start(bf16[272,128]{1,0:T(8,128)(2,1)S(1)} %collective-permute-done.4.refs_6_) | copy-start | bytes 208900
  15.0 0.6 copy-start.10
  15.0 0.7 copy-start.11
  35.6 1.7 %collective-permute-start.5 = (bf16[864,128]{1,0:T(8,128)(2,1)}, bf16[864,128]{1,0:T(8,128)(2,1)S(1)}, u32[]{:S(2)}, u32[]{:S(2)}) collective-permute-start(bf16[864,128]{1,0:T(8,128)(2,1)} %get-tuple-element.26), channel_id=1, source_target_pairs={{0,1},{1,0},{2,3},{3,2},{4,5},{5,4},{6,7},{7,6},{8,9},{9,8},{10,11... | collective-permute-start | bytes 663560 | tf_op jit(solution)/shard_map/ppermute | solution.py:464
  37.4 0.7 copy-start.3
  39.9 25.3 %collective-permute-start.6 = (bf16[592,128]{1,0:T(8,128)(2,1)}, bf16[592,128]{1,0:T(8,128)(2,1)S(1)}, u32[]{:S(2)}, u32[]{:S(2)}) collective-permute-start(bf16[592,128]{1,0:T(8,128)(2,1)} %get-tuple-element.29), channel_id=1, source_target_pairs={{0,2},{1,3},{2,0},{3,1},{4,6},{5,7},{6,4},{7,5},{8,10},{9,11},{10,... | collective-permute-start | bytes 454664 | tf_op jit(solution)/shard_map/ppermute | solution.py:464
  58.3 12.4 %copy-start.13 = (f32[16,128]{1,0:T(8,128)S(1)}, f32[16,128]{1,0:T(8,128)}, u32[]{:S(2)}) copy-start(f32[16,128]{1,0:T(8,128)} %get-tuple-element.31) | copy-start | bytes 24580
  58.3 6.3 %collective-permute-start.9 = (f32[176,128]{1,0:T(8,128)}, f32[176,128]{1,0:T(8,128)S(1)}, u32[]{:S(2)}, u32[]{:S(2)}) collective-permute-start(f32[176,128]{1,0:T(8,128)} %get-tuple-element.30), channel_id=1, source_target_pairs={{0,6},{1,7},{2,4},{3,5},{4,2},{5,3},{6,0},{7,1},{8,14},{9,15},{10,... | collective-permute-start | bytes 270344 | tf_op jit(solution)/shard_map/ppermute | solution.py:464
  60.5 4.7 %collective-permute-start.7 = (f32[176,128]{1,0:T(8,128)}, f32[176,128]{1,0:T(8,128)S(1)}, u32[]{:S(2)}, u32[]{:S(2)}) collective-permute-start(f32[176,128]{1,0:T(8,128)} %get-tuple-element.30), channel_id=1, source_target_pairs={{0,4},{4,0},{8,12},{12,8},{16,20},{20,16},{24,28},{28,24},{1,5},{5... | collective-permute-start | bytes 270344 | tf_op jit(solution)/shard_map/ppermute | solution.py:464
  65.2 1.0 %copy-start.1 = (f32[176,128]{1,0:T(8,128)}, f32[176,128]{1,0:T(8,128)S(1)}, u32[]{:S(2)}) copy-start(f32[176,128]{1,0:T(8,128)S(1)} %collective-permute-done.7.near_ref) | copy-start | bytes 270340
  65.2 1.0 %copy-start = (bf16[592,128]{1,0:T(8,128)(2,1)}, bf16[592,128]{1,0:T(8,128)(2,1)S(1)}, u32[]{:S(2)}) copy-start(bf16[592,128]{1,0:T(8,128)(2,1)S(1)} %collective-permute-done.6.got_ref) | copy-start | bytes 454660
  66.2 13.4 %copy-start.2 = (f32[160,128]{1,0:T(8,128)}, f32[160,128]{1,0:T(8,128)S(1)}, u32[]{:S(2)}) copy-start(f32[160,128]{1,0:T(8,128)S(1)} %fusion.refs_0_) | copy-start | bytes 245764
  66.3 13.3 %collective-permute-start.12 = (f32[160,128]{1,0:T(8,128)S(1)}, f32[160,128]{1,0:T(8,128)S(1)}, u32[]{:S(2)}, u32[]{:S(2)}) collective-permute-start(f32[160,128]{1,0:T(8,128)S(1)} %fusion.refs_0_), channel_id=1, source_target_pairs={{0,24},{4,28},{8,16},{12,20},{16,8},{20,12},{24,0},{28,4},{1,25},{... | collective-permute-start | bytes 245768 | tf_op jit(solution)/shard_map/ppermute | solution.py:464
  67.0 12.6 %collective-permute-start.11 = (f32[160,128]{1,0:T(8,128)S(1)}, f32[160,128]{1,0:T(8,128)S(1)}, u32[]{:S(2)}, u32[]{:S(2)}) collective-permute-start(f32[160,128]{1,0:T(8,128)S(1)} %fusion.refs_0_), channel_id=1, source_target_pairs={{0,16},{4,20},{8,24},{12,28},{16,0},{20,4},{24,8},{28,12},{1,17},{... | collective-permute-start | bytes 245768 | tf_op jit(solution)/shard_map/ppermute | solution.py:464
  68.1 11.6 %collective-permute-start.10 = (f32[160,128]{1,0:T(8,128)S(1)}, f32[160,128]{1,0:T(8,128)S(1)}, u32[]{:S(2)}, u32[]{:S(2)}) collective-permute-start(f32[160,128]{1,0:T(8,128)S(1)} %fusion.refs_0_), channel_id=1, source_target_pairs={{0,8},{4,12},{8,0},{12,4},{16,24},{20,28},{24,16},{28,20},{1,9},{5... | collective-permute-start | bytes 245768 | tf_op jit(solution)/shard_map/ppermute | solution.py:464
  70.7 6.6 %collective-permute-start.8 = (f32[16,128]{1,0:T(8,128)S(1)}, f32[16,128]{1,0:T(8,128)S(1)}, u32[]{:S(2)}, u32[]{:S(2)}) collective-permute-start(f32[16,128]{1,0:T(8,128)S(1)} %copy-done.13), channel_id=1, source_target_pairs={{0,28},{4,8},{8,4},{12,16},{16,12},{20,24},{24,20},{28,0},{1,29},{... | collective-permute-start | bytes 24584 | tf_op jit(solution)/shard_map/ppermute | solution.py:464
  77.3 0.6 copy-start.12
  79.6 0.6 copy-start.4
  79.6 0.6 copy-start.5
  80.3 0.6 copy-start.6

commit v5 on v4

--- a/solution.py
+++ b/solution.py
@@ -116,7 +116,7 @@
         lhs_a,
         lhs_d,
     ), refs = refs[:13], refs[13:]
-    stack_buf, soft_buf, gate_buf, pair_buf, both_buf, refs = *refs[:5], refs[5:]
+    stack_buf, soft_buf, gate_buf, pair_buf, d_pre_buf, refs = *refs[:5], refs[5:]
     basis_buf, slant_buf, inner_buf, geo_buf, pull_buf, *refs = refs
     half_buf, back_buf, filt_buf = refs
     width = w_filter_ref.shape[0]
@@ -181,10 +181,7 @@
     lhs_f[1] = bias.T.astype(BF16)
     lhs_a[:width] = w_filter_ref[...]
     lhs_a[width:] = bias[:16].astype(BF16)
-    lhs_d[0, :nbasis] = w_rbf_ref[...]
-    lhs_d[0, nbasis:] = jnp.zeros((nbasis, width), BF16)
-    lhs_d[1, :nbasis] = jnp.zeros((nbasis, width), BF16)
-    lhs_d[1, nbasis:] = one_hot(iota((nbasis, width), 0) == 0)
+    lhs_d[...] = w_rbf_ref[...]
 
     grad_feat[...] = jnp.zeros_like(grad_feat)
     grad_recv[...] = jnp.zeros_like(grad_recv)
@@ -284,31 +281,32 @@
     def feature_stage(at, entry):
         tower_tile, plate_tile = places(entry)[:2]
         c = at % per_tile * 2
+        inner = [None, None]
         for r in parts:
             total = grad_feat[plate_tile, r]
             for n, block in enumerate(blocks_of(at)):
                 back = back_buf[at % 2 * 2 + n, r]
-                low = slice(width + r.start, width + r.stop)
-                both_buf[block, r] = (back * gate_buf[block, r]).astype(BF16)
-                both_buf[block, low] = (back * soft_buf[block, r]).astype(BF16)
+                d_pre_buf[block, r] = (back * gate_buf[block, r]).astype(BF16)
+                part = jnp.sum((back * soft_buf[block, r]).reshape(-1, 8, LANES), axis=0)
+                inner[n] = part if inner[n] is None else inner[n] + part
                 total = total + filt_buf[at % 2 * 2 + n, r] * adj_wide[tower_tile, c + n, r]
             grad_feat[plate_tile, r] = total
         for n, block in enumerate(blocks_of(at)):
-            inner_buf[block] = back_buf[at % 2 * 2 + n, width : width + 8]
+            inner_buf[block] = (
+                back_buf[at % 2 * 2 + n, width : width + 8] - math.log(2.0) * inner[n]
+            )
 
     def radial_stage(at, entry):
         tile, c = at // per_tile % 2, at % per_tile * 2
-        lhs = jnp.concatenate([lhs_d[0], lhs_d[1]], axis=1)
-        d_basis = nn(lhs, wide(both_buf, blocks_of(at)))
+        d_basis = nn(lhs_d[...], wide(d_pre_buf, blocks_of(at)))
         for n, block in enumerate(blocks_of(at)):
             part = d_basis[:, n * LANES : (n + 1) * LANES]
-            direct = jnp.sum(part[:nbasis] * slant_buf[block], axis=0, keepdims=True)
+            direct = jnp.sum(part * slant_buf[block], axis=0, keepdims=True)
             inner = jnp.sum(inner_buf[block], axis=0, keepdims=True)
-            inner = inner - math.log(2.0) * part[nbasis : nbasis + 1]
             pull_buf[c + n : c + n + 1] = direct + geo_row(at, 3)[n] * inner
         whole = blocks_of(at)
         acc_wf[...] += nt(wide(stack_buf, whole), wide(pair_buf, whole))
-        acc_wr[...] += nt(wide(basis_buf, whole), wide(both_buf, whole, slice(0, width)))
+        acc_wr[...] += nt(wide(basis_buf, whole), wide(d_pre_buf, whole))
         if at % per_tile < per_tile - 1:
             return
         _, _, recv_at, send_at, _ = places(entry)
@@ -321,7 +319,7 @@
     parts = [slice(r, r + PART) for r in range(0, width, PART)]
     for ref in (soft_buf, gate_buf):
         ref[2 * ring - 2 :] = jnp.zeros((2, *ref.shape[1:]), ref.dtype)
-    for ref in (basis_buf, slant_buf, stack_buf, pair_buf, both_buf, inner_buf):
+    for ref in (basis_buf, slant_buf, stack_buf, pair_buf, d_pre_buf, inner_buf):
         ref[2 * ring - 4 :] = jnp.zeros((4, *ref.shape[1:]), ref.dtype)
     for ref in (back_buf, filt_buf, pull_buf):
         ref[...] = jnp.zeros_like(ref)
@@ -548,14 +546,14 @@
             pltpu.VMEM((width, 2 * nbasis), BF16),
             pltpu.VMEM((2, width, width), BF16),
             pltpu.VMEM((width + 16, width), BF16),
-            pltpu.VMEM((2, 2 * nbasis, width), BF16),
+            pltpu.VMEM((nbasis, width), BF16),
         ]
         + [
             pltpu.VMEM((2 * chunks, width + 16, LANES), BF16),
             pltpu.VMEM((2 * chunks, width, LANES), F32),
             pltpu.VMEM((2 * chunks, width, LANES), F32),
             pltpu.VMEM((2 * chunks, width, LANES), BF16),
-            pltpu.VMEM((2 * chunks, 2 * width, LANES), BF16),
+            pltpu.VMEM((2 * chunks, width, LANES), BF16),
             pltpu.VMEM((2 * chunks, 2 * nbasis, LANES), BF16),
             pltpu.VMEM((2 * chunks, nbasis, LANES), F32),
             pltpu.VMEM((2 * chunks, 8, LANES), F32),

time: 83.1 us -> 81.3 us (0.978)
  starting transfers between devices: 34.6 us -> 33.7 us
    ppermute x13, starting transfers between devices: 34.6 us -> 33.7 us  [swap(): lax.ppermute(value, axis, [(i, route(i) % size) for i in range(size)])]
where the time goes in v5:
time: 81.3 us; the launch traced here: 81 us
  starting transfers between devices  33.7 us (41%)
  Pallas kernels  26.1 us (32%)
  waiting for transfers between devices  14.4 us (18%)
  local copies, waits for them, and re-layouts  3.22 us (4%)
  between operations  2.04 us (3%)
  other arithmetic  1.57 us (2%)
    ppermute x13, starting transfers between devices, swap(): lax.ppermute(value, axis, [(i, route(i) % size) for i in range(size)])  33.7 us
    pallas_call x1, Pallas kernels, local(): call(functools.partial(tile_kernel, plate_count), [((half * block, width)...  19.2 us
    ppermute x13, waiting for transfers between devices, swap(): lax.ppermute(value, axis, [(i, route(i) % size) for i in range(size)])  14.4 us
    unnamed x28, local copies, waits for them, and re-layouts  3.22 us
    pallas_call x1, Pallas kernels, local(): call(functools.partial(add_kernel, cut), [((cut, width), F32), ((held - c...  1.83 us
    pallas_call x1, Pallas kernels, local(): call(weight_kernel, [((nbasis, width), F32), ((1, width), F32), ((width,...  1.79 us
    pallas_call x1, Pallas kernels, local(): call(functools.partial(finish_kernel, atoms), [((1, atoms, width), F32),...  1.71 us
  transfers between devices with their start and end apart: 13, of which 7 were waited for; matrix products, arithmetic and copies ran while one was open for 1% of the time, Pallas kernels for 2%

profile of v5, /device:TPU:0, one launch (start us, length us, event | category | flops | bytes accessed | tf_op | source)
XLA Modules:
  0.0 81.0 jit_solution(11821598217869424966)
XLA Ops:
  1.3 1.6 %shard_map.163 = (bf16[272,128]{1,0:T(8,128)(2,1)}, bf16[272,128]{1,0:T(8,128)(2,1)}) custom-call(s32[1,1]{1,0:T(1,128)S(6)} %copy.18.count_ref, bf16[1,256,128]{2,1,0:T(8,128)(2,1)} %feat_ref.1, bf16[1,256,128]{2,1,0:T(8,128)(2,1)} %adj_ref.1, bf16[3,256]{1,0:T(4,128)(2,1)} %bitcast.7), custom_call_target="tpu_custom_call" | custom-call | tf_op jit(solution)/shard_map/pallas_call | solution.py:517
  2.8 6.0 %collective-permute-start.1 = (bf16[272,128]{1,0:T(8,128)(2,1)}, bf16[272,128]{1,0:T(8,128)(2,1)S(1)}, u32[]{:S(2)}, u32[]{:S(2)}) collective-permute-start(bf16[272,128]{1,0:T(8,128)(2,1)} %get-tuple-element.22.refs_0_), channel_id=1, source_target_pairs={{0,28},{4,8},{8,4},{12,16},{16,12},{20,24},{24,20},{28,0},{1,29},{... | collective-permute-start | bytes 208904 | tf_op jit(solution)/shard_map/ppermute | solution.py:462
  8.8 0.0 collective-permute-start
  8.8 0.7 collective-permute-start.4
  9.5 0.8 %collective-permute-start.3 = (bf16[272,128]{1,0:T(8,128)(2,1)}, bf16[272,128]{1,0:T(8,128)(2,1)S(1)}, u32[]{:S(2)}, u32[]{:S(2)}) collective-permute-start(bf16[272,128]{1,0:T(8,128)(2,1)} %get-tuple-element.23.refs_3_), channel_id=1, source_target_pairs={{0,2},{1,3},{2,0},{3,1},{4,6},{5,7},{6,4},{7,5},{8,10},{9,11},{10,... | collective-permute-start | bytes 208904 | tf_op jit(solution)/shard_map/ppermute | solution.py:462
  10.4 0.3 collective-permute-start.2
  11.4 0.6 pad_add_fusion.where_ref
  11.9 0.0 collective-permute-done.1.refs_2_
  11.9 0.0 copy-start.7
  11.9 1.4 %collective-permute-done.refs_1_ = bf16[272,128]{1,0:T(8,128)(2,1)S(1)} collective-permute-done((bf16[272,128]{1,0:T(8,128)(2,1)}, bf16[272,128]{1,0:T(8,128)(2,1)S(1)}, u32[]{:S(2)}, u32[]{:S(2)}) %collective-permute-start) | collective-permute-done | bytes 69664 | tf_op jit(solution)/shard_map/ppermute | solution.py:462
  13.4 0.0 copy-start.8
  13.4 0.1 collective-permute-done.4.refs_6_
  13.5 0.0 copy-start.9
  13.5 1.6 %collective-permute-done.3.refs_5_ = bf16[272,128]{1,0:T(8,128)(2,1)S(1)} collective-permute-done((bf16[272,128]{1,0:T(8,128)(2,1)}, bf16[272,128]{1,0:T(8,128)(2,1)S(1)}, u32[]{:S(2)}, u32[]{:S(2)}) %collective-permute-start.3) | collective-permute-done | bytes 69664 | tf_op jit(solution)/shard_map/ppermute | solution.py:462
  15.0 0.0 copy-start.10
  15.0 0.0 collective-permute-done.2.refs_4_
  15.0 0.0 copy-start.11
  15.0 0.0 copy-done.7
  15.0 0.0 copy-done.8
  15.1 0.0 copy-done.9
  15.1 0.6 copy-done.10
  15.6 0.1 copy-done.11
  15.7 19.2 %shard_map.164 = (f32[544,128]{1,0:T(8,128)}, bf16[864,128]{1,0:T(8,128)(2,1)}, f32[160,128]{1,0:T(8,128)}, f32[16,128]{1,0:T(8,128)}, f32[16,128]{1,0:T(8,128)}) custom-call(s32[2]{0:T(128)} %pad_add_fusion.where_ref, s32[1,1]{1,0:T(1,128)S(6)} %copy.19.count_ref, s32[1,1,56]{2,1,0:T(1,128)} %tower_ref.1, s32[1,1,56]{2,1,0:T(1,128)} %plate_ref.1, ...), custom_call_target="tpu_custom_call" | custom-call | tf_op jit(solution)/shard_map/pallas_call | solution.py:526
  34.9 0.1 collective-permute-start.5
  35.0 1.6 %collective-permute-done.5.got_ref = bf16[864,128]{1,0:T(8,128)(2,1)S(1)} collective-permute-done((bf16[864,128]{1,0:T(8,128)(2,1)}, bf16[864,128]{1,0:T(8,128)(2,1)S(1)}, u32[]{:S(2)}, u32[]{:S(2)}) %collective-permute-start.5) | collective-permute-done | bytes 221216 | tf_op jit(solution)/shard_map/ppermute | solution.py:462
  36.6 0.0 copy-start.3
  36.6 0.7 copy-done.3
  37.3 1.8 %shard_map.165 = (f32[272,128]{1,0:T(8,128)}, bf16[592,128]{1,0:T(8,128)(2,1)}, f32[176,128]{1,0:T(8,128)}) custom-call(f32[544,128]{1,0:T(8,128)} %get-tuple-element.24.kept_ref, f32[160,128]{1,0:T(8,128)} %get-tuple-element.25.weight_ref, bf16[864,128]{1,0:T(8,128)(2,1)} %copy-done.3, f32[16,128]{1,0:T(8,128)} %get-tuple-element.27.near_ref), custom_call_target="tpu_custom_call" | custom-call | tf_op jit(solution)/shard_map/pallas_call | solution.py:588
  39.1 17.4 %collective-permute-start.6 = (bf16[592,128]{1,0:T(8,128)(2,1)}, bf16[592,128]{1,0:T(8,128)(2,1)S(1)}, u32[]{:S(2)}, u32[]{:S(2)}) collective-permute-start(bf16[592,128]{1,0:T(8,128)(2,1)} %get-tuple-element.29), channel_id=1, source_target_pairs={{0,2},{1,3},{2,0},{3,1},{4,6},{5,7},{6,4},{7,5},{8,10},{9,11},{10,... | collective-permute-start | bytes 454664 | tf_op jit(solution)/shard_map/ppermute | solution.py:462
  56.6 0.0 copy-start.13
  56.6 2.2 %collective-permute-start.9 = (f32[176,128]{1,0:T(8,128)}, f32[176,128]{1,0:T(8,128)S(1)}, u32[]{:S(2)}, u32[]{:S(2)}) collective-permute-start(f32[176,128]{1,0:T(8,128)} %get-tuple-element.30), channel_id=1, source_target_pairs={{0,6},{1,7},{2,4},{3,5},{4,2},{5,3},{6,0},{7,1},{8,14},{9,15},{10,... | collective-permute-start | bytes 270344 | tf_op jit(solution)/shard_map/ppermute | solution.py:462
  58.8 0.0 collective-permute-start.7
  58.8 4.1 %collective-permute-done.9 = f32[176,128]{1,0:T(8,128)S(1)} collective-permute-done((f32[176,128]{1,0:T(8,128)}, f32[176,128]{1,0:T(8,128)S(1)}, u32[]{:S(2)}, u32[]{:S(2)}) %collective-permute-start.9) | collective-permute-done | bytes 90144 | tf_op jit(solution)/shard_map/ppermute | solution.py:462
  62.9 0.6 collective-permute-done.7.near_ref
  63.5 0.0 copy-start.1
  63.5 0.0 collective-permute-done.6.got_ref
  63.5 0.0 copy-start
  63.5 1.0 %fusion.refs_0_ = f32[160,128]{1,0:T(8,128)S(1)} fusion(f32[176,128]{1,0:T(8,128)S(1)} %collective-permute-done.9, f32[176,128]{1,0:T(8,128)S(1)} %collective-permute-done.7.near_ref, f32[176,128]{1,0:T(8,128)} %get-tuple-element.30, bf16[592,128]{1,0:T(8,128)(2,1)S(1)} %collective-permute-done.6.got_ref), kind=kLoop, calls=%fused_computation.1 | loop fusion | flops 122880 | bytes 409600 | tf_op jit(solution)/shard_map/add | solution.py:602
  64.5 0.0 copy-done.1
  64.5 0.0 copy-done
  64.5 0.0 copy-start.2
  64.5 0.7 collective-permute-start.12
  65.3 1.1 %collective-permute-start.11 = (f32[160,128]{1,0:T(8,128)S(1)}, f32[160,128]{1,0:T(8,128)S(1)}, u32[]{:S(2)}, u32[]{:S(2)}) collective-permute-start(f32[160,128]{1,0:T(8,128)S(1)} %fusion.refs_0_), channel_id=1, source_target_pairs={{0,16},{4,20},{8,24},{12,28},{16,0},{20,4},{24,8},{28,12},{1,17},{... | collective-permute-start | bytes 245768 | tf_op jit(solution)/shard_map/ppermute | solution.py:462
  66.3 2.6 %collective-permute-start.10 = (f32[160,128]{1,0:T(8,128)S(1)}, f32[160,128]{1,0:T(8,128)S(1)}, u32[]{:S(2)}, u32[]{:S(2)}) collective-permute-start(f32[160,128]{1,0:T(8,128)S(1)} %fusion.refs_0_), channel_id=1, source_target_pairs={{0,8},{4,12},{8,0},{12,4},{16,24},{20,28},{24,16},{28,20},{1,9},{5... | collective-permute-start | bytes 245768 | tf_op jit(solution)/shard_map/ppermute | solution.py:462
  69.0 0.0 copy-done.13
  69.0 1.6 %collective-permute-start.8 = (f32[16,128]{1,0:T(8,128)S(1)}, f32[16,128]{1,0:T(8,128)S(1)}, u32[]{:S(2)}, u32[]{:S(2)}) collective-permute-start(f32[16,128]{1,0:T(8,128)S(1)} %copy-done.13), channel_id=1, source_target_pairs={{0,28},{4,8},{8,4},{12,16},{16,12},{20,24},{24,20},{28,0},{1,29},{... | collective-permute-start | bytes 24584 | tf_op jit(solution)/shard_map/ppermute | solution.py:462
  70.6 4.9 %collective-permute-done.8.far_ref = f32[16,128]{1,0:T(8,128)S(1)} collective-permute-done((f32[16,128]{1,0:T(8,128)S(1)}, f32[16,128]{1,0:T(8,128)S(1)}, u32[]{:S(2)}, u32[]{:S(2)}) %collective-permute-start.8) | collective-permute-done | bytes 8224 | tf_op jit(solution)/shard_map/ppermute | solution.py:462
  75.6 0.0 copy-start.12
  75.6 0.6 copy-done.12
  76.2 1.7 %shard_map.166 = (f32[1,256,128]{2,1,0:T(8,128)}, f32[3,1,256]{2,1,0:T(1,128)}) custom-call(s32[1,1]{1,0:T(1,128)S(6)} %copy.18.count_ref, f32[272,128]{1,0:T(8,128)} %get-tuple-element.28.block_ref, bf16[592,128]{1,0:T(8,128)(2,1)} %copy-done, f32[176,128]{1,0:T(8,128)} %copy-done.1, f32[16,128]{1,0:T(8,128)} %copy-done.12), custom_call_target="tpu_custom_call" | custom-call | tf_op jit(solution)/shard_map/pallas_call | solution.py:611
  77.9 0.0 copy-done.2
  77.9 0.0 collective-permute-done.12.refs_3_
  77.9 0.0 copy-start.4
  77.9 0.0 collective-permute-done.11.refs_2_
  77.9 0.0 copy-start.5
  77.9 0.0 collective-permute-done.10.refs_1_
  77.9 0.6 copy-done.4
  78.5 0.0 copy-done.5
  78.5 0.0 copy-start.6
  78.5 0.6 copy-done.6
  79.2 1.8 %shard_map.167 = (f32[16,128]{1,0:T(8,128)}, f32[1,128]{1,0:T(1,128)}, f32[128,128]{1,0:T(8,128)}, f32[1,128]{1,0:T(1,128)}) custom-call(f32[160,128]{1,0:T(8,128)} %copy-done.2, f32[160,128]{1,0:T(8,128)} %copy-done.6, f32[160,128]{1,0:T(8,128)} %copy-done.5, f32[160,128]{1,0:T(8,128)} %copy-done.4), custom_call_target="tpu_custom_call" | custom-call | tf_op jit(solution)/shard_map/pallas_call | solution.py:616
Async XLA Ops:
  2.8 9.1 %collective-permute-start.1 = (bf16[272,128]{1,0:T(8,128)(2,1)}, bf16[272,128]{1,0:T(8,128)(2,1)S(1)}, u32[]{:S(2)}, u32[]{:S(2)}) collective-permute-start(bf16[272,128]{1,0:T(8,128)(2,1)} %get-tuple-element.22.refs_0_), channel_id=1, source_target_pairs={{0,28},{4,8},{8,4},{12,16},{16,12},{20,24},{24,20},{28,0},{1,29},{... | collective-permute-start | bytes 208904 | tf_op jit(solution)/shard_map/ppermute | solution.py:462
  8.8 4.5 %collective-permute-start = (bf16[272,128]{1,0:T(8,128)(2,1)}, bf16[272,128]{1,0:T(8,128)(2,1)S(1)}, u32[]{:S(2)}, u32[]{:S(2)}) collective-permute-start(bf16[272,128]{1,0:T(8,128)(2,1)} %get-tuple-element.22.refs_0_), channel_id=1, source_target_pairs={{0,4},{4,0},{8,12},{12,8},{16,20},{20,16},{24,28},{28,24},{1,5},{5... | collective-permute-start | bytes 208904 | tf_op jit(solution)/shard_map/ppermute | solution.py:462
  8.8 4.6 %collective-permute-start.4 = (bf16[272,128]{1,0:T(8,128)(2,1)}, bf16[272,128]{1,0:T(8,128)(2,1)S(1)}, u32[]{:S(2)}, u32[]{:S(2)}) collective-permute-start(bf16[272,128]{1,0:T(8,128)(2,1)} %get-tuple-element.23.refs_3_), channel_id=1, source_target_pairs={{0,3},{1,2},{2,1},{3,0},{4,7},{5,6},{6,5},{7,4},{8,11},{9,10},{10,... | collective-permute-start | bytes 208904 | tf_op jit(solution)/shard_map/ppermute | solution.py:462
  9.5 5.5 %collective-permute-start.3 = (bf16[272,128]{1,0:T(8,128)(2,1)}, bf16[272,128]{1,0:T(8,128)(2,1)S(1)}, u32[]{:S(2)}, u32[]{:S(2)}) collective-permute-start(bf16[272,128]{1,0:T(8,128)(2,1)} %get-tuple-element.23.refs_3_), channel_id=1, source_target_pairs={{0,2},{1,3},{2,0},{3,1},{4,6},{5,7},{6,4},{7,5},{8,10},{9,11},{10,... | collective-permute-start | bytes 208904 | tf_op jit(solution)/shard_map/ppermute | solution.py:462
  10.4 4.7 %collective-permute-start.2 = (bf16[272,128]{1,0:T(8,128)(2,1)}, bf16[272,128]{1,0:T(8,128)(2,1)S(1)}, u32[]{:S(2)}, u32[]{:S(2)}) collective-permute-start(bf16[272,128]{1,0:T(8,128)(2,1)} %get-tuple-element.23.refs_3_), channel_id=1, source_target_pairs={{0,1},{1,0},{2,3},{3,2},{4,5},{5,4},{6,7},{7,6},{8,9},{9,8},{10,11... | collective-permute-start | bytes 208904 | tf_op jit(solution)/shard_map/ppermute | solution.py:462
  11.9 3.1 %copy-start.7 = (bf16[272,128]{1,0:T(8,128)(2,1)}, bf16[272,128]{1,0:T(8,128)(2,1)S(1)}, u32[]{:S(2)}) copy-start(bf16[272,128]{1,0:T(8,128)(2,1)S(1)} %collective-permute-done.1.refs_2_) | copy-start | bytes 208900
  13.4 1.7 %copy-start.8 = (bf16[272,128]{1,0:T(8,128)(2,1)}, bf16[272,128]{1,0:T(8,128)(2,1)S(1)}, u32[]{:S(2)}) copy-start(bf16[272,128]{1,0:T(8,128)(2,1)S(1)} %collective-permute-done.refs_1_) | copy-start | bytes 208900
  13.5 1.6 %copy-start.9 = (bf16[272,128]{1,0:T(8,128)(2,1)}, bf16[272,128]{1,0:T(8,128)(2,1)S(1)}, u32[]{:S(2)}) copy-start(bf16[272,128]{1,0:T(8,128)(2,1)S(1)} %collective-permute-done.4.refs_6_) | copy-start | bytes 208900
  15.0 0.6 copy-start.10
  15.0 0.7 copy-start.11
  34.9 1.7 %collective-permute-start.5 = (bf16[864,128]{1,0:T(8,128)(2,1)}, bf16[864,128]{1,0:T(8,128)(2,1)S(1)}, u32[]{:S(2)}, u32[]{:S(2)}) collective-permute-start(bf16[864,128]{1,0:T(8,128)(2,1)} %get-tuple-element.26), channel_id=1, source_target_pairs={{0,1},{1,0},{2,3},{3,2},{4,5},{5,4},{6,7},{7,6},{8,9},{9,8},{10,11... | collective-permute-start | bytes 663560 | tf_op jit(solution)/shard_map/ppermute | solution.py:462
  36.6 0.7 copy-start.3
  39.1 24.4 %collective-permute-start.6 = (bf16[592,128]{1,0:T(8,128)(2,1)}, bf16[592,128]{1,0:T(8,128)(2,1)S(1)}, u32[]{:S(2)}, u32[]{:S(2)}) collective-permute-start(bf16[592,128]{1,0:T(8,128)(2,1)} %get-tuple-element.29), channel_id=1, source_target_pairs={{0,2},{1,3},{2,0},{3,1},{4,6},{5,7},{6,4},{7,5},{8,10},{9,11},{10,... | collective-permute-start | bytes 454664 | tf_op jit(solution)/shard_map/ppermute | solution.py:462
  56.6 12.4 %copy-start.13 = (f32[16,128]{1,0:T(8,128)S(1)}, f32[16,128]{1,0:T(8,128)}, u32[]{:S(2)}) copy-start(f32[16,128]{1,0:T(8,128)} %get-tuple-element.31) | copy-start | bytes 24580
  56.6 6.3 %collective-permute-start.9 = (f32[176,128]{1,0:T(8,128)}, f32[176,128]{1,0:T(8,128)S(1)}, u32[]{:S(2)}, u32[]{:S(2)}) collective-permute-start(f32[176,128]{1,0:T(8,128)} %get-tuple-element.30), channel_id=1, source_target_pairs={{0,6},{1,7},{2,4},{3,5},{4,2},{5,3},{6,0},{7,1},{8,14},{9,15},{10,... | collective-permute-start | bytes 270344 | tf_op jit(solution)/shard_map/ppermute | solution.py:462
  58.8 4.7 %collective-permute-start.7 = (f32[176,128]{1,0:T(8,128)}, f32[176,128]{1,0:T(8,128)S(1)}, u32[]{:S(2)}, u32[]{:S(2)}) collective-permute-start(f32[176,128]{1,0:T(8,128)} %get-tuple-element.30), channel_id=1, source_target_pairs={{0,4},{4,0},{8,12},{12,8},{16,20},{20,16},{24,28},{28,24},{1,5},{5... | collective-permute-start | bytes 270344 | tf_op jit(solution)/shard_map/ppermute | solution.py:462
  63.5 1.0 %copy-start.1 = (f32[176,128]{1,0:T(8,128)}, f32[176,128]{1,0:T(8,128)S(1)}, u32[]{:S(2)}) copy-start(f32[176,128]{1,0:T(8,128)S(1)} %collective-permute-done.7.near_ref) | copy-start | bytes 270340
  63.5 1.0 %copy-start = (bf16[592,128]{1,0:T(8,128)(2,1)}, bf16[592,128]{1,0:T(8,128)(2,1)S(1)}, u32[]{:S(2)}) copy-start(bf16[592,128]{1,0:T(8,128)(2,1)S(1)} %collective-permute-done.6.got_ref) | copy-start | bytes 454660
  64.5 13.4 %copy-start.2 = (f32[160,128]{1,0:T(8,128)}, f32[160,128]{1,0:T(8,128)S(1)}, u32[]{:S(2)}) copy-start(f32[160,128]{1,0:T(8,128)S(1)} %fusion.refs_0_) | copy-start | bytes 245764
  64.5 13.3 %collective-permute-start.12 = (f32[160,128]{1,0:T(8,128)S(1)}, f32[160,128]{1,0:T(8,128)S(1)}, u32[]{:S(2)}, u32[]{:S(2)}) collective-permute-start(f32[160,128]{1,0:T(8,128)S(1)} %fusion.refs_0_), channel_id=1, source_target_pairs={{0,24},{4,28},{8,16},{12,20},{16,8},{20,12},{24,0},{28,4},{1,25},{... | collective-permute-start | bytes 245768 | tf_op jit(solution)/shard_map/ppermute | solution.py:462
  65.3 12.6 %collective-permute-start.11 = (f32[160,128]{1,0:T(8,128)S(1)}, f32[160,128]{1,0:T(8,128)S(1)}, u32[]{:S(2)}, u32[]{:S(2)}) collective-permute-start(f32[160,128]{1,0:T(8,128)S(1)} %fusion.refs_0_), channel_id=1, source_target_pairs={{0,16},{4,20},{8,24},{12,28},{16,0},{20,4},{24,8},{28,12},{1,17},{... | collective-permute-start | bytes 245768 | tf_op jit(solution)/shard_map/ppermute | solution.py:462
  66.3 11.6 %collective-permute-start.10 = (f32[160,128]{1,0:T(8,128)S(1)}, f32[160,128]{1,0:T(8,128)S(1)}, u32[]{:S(2)}, u32[]{:S(2)}) collective-permute-start(f32[160,128]{1,0:T(8,128)S(1)} %fusion.refs_0_), channel_id=1, source_target_pairs={{0,8},{4,12},{8,0},{12,4},{16,24},{20,28},{24,16},{28,20},{1,9},{5... | collective-permute-start | bytes 245768 | tf_op jit(solution)/shard_map/ppermute | solution.py:462
  69.0 6.6 %collective-permute-start.8 = (f32[16,128]{1,0:T(8,128)S(1)}, f32[16,128]{1,0:T(8,128)S(1)}, u32[]{:S(2)}, u32[]{:S(2)}) collective-permute-start(f32[16,128]{1,0:T(8,128)S(1)} %copy-done.13), channel_id=1, source_target_pairs={{0,28},{4,8},{8,4},{12,16},{16,12},{20,24},{24,20},{28,0},{1,29},{... | collective-permute-start | bytes 24584 | tf_op jit(solution)/shard_map/ppermute | solution.py:462
  75.6 0.6 copy-start.12
  77.9 0.6 copy-start.4
  77.9 0.6 copy-start.5
  78.5 0.6 copy-start.6

commit v6 on v5

--- a/solution.py
+++ b/solution.py
@@ -350,9 +350,8 @@
     feature_stage(-1, last)
     radial_stage(-1, last)
 
-    digit = iota((1, width), 1)
-    count_row = jnp.where(digit == 0, lax.rem(count, 16), 0)
-    count_row = jnp.where(digit == 1, count // 16, count_row).astype(F32)
+    digit = jnp.minimum(iota((1, width), 1), 16)
+    count_row = jnp.where(digit < 16, (count >> digit) & 1, 0).astype(F32)
     weights = jnp.concatenate(
         [
             acc_wf[:width],
@@ -444,12 +443,14 @@
 
 def weight_kernel(*refs):
     ins, outs = refs[:-4], refs[-4:]
-    total = ins[0][...]
+    total = ins[0][...].astype(F32)
     for other in ins[1:]:
-        total = total + other[...]
+        total = total + other[...].astype(F32)
     nbasis, width = outs[0].shape
     row = total[width + nbasis + 2 : width + nbasis + 3]
-    tiles = row[:, :1] + 16.0 * row[:, 1:2]
+    digit = jnp.minimum(iota((1, width), 1), 16)
+    worth = jnp.where(digit < 16, 1 << digit, 0).astype(F32)
+    tiles = jnp.sum(row * worth, axis=1, keepdims=True)
     scale = lax.rsqrt(tiles * (TILE * TILE))
     outs[0][...] = total[width : width + nbasis] * scale
     outs[1][...] = total[width + nbasis + 1 : width + nbasis + 2] * scale
@@ -604,7 +605,8 @@
     bits = 2
     parts = [weights]
     while bits < tower_count:
-        weights = sum(parts[1:], parts[0])
+        weights = sum((part.astype(F32) for part in parts[1:]), parts[0].astype(F32))
+        weights = weights.astype(BF16)
         stride = [s * bits for s in (1, 2, 3) if s * bits < tower_count]
         parts = [weights] + [swap(weights, "tower", across(s)) for s in stride]
         bits *= 4

time: 81.3 us -> 80.9 us (level)
    convert_element_type x0 -> x1, other arithmetic: none -> 0.99 us  [local(): weights = weights.astype(BF16)]
    add x1 -> x0, other arithmetic: 0.99 us -> none  [local(): weights = weights + (near[:weight_rows] + both[:weight_rows])]
where the time goes in v6:
time: 80.9 us; the launch traced here: 80.5 us
  starting transfers between devices  33.7 us (42%)
  Pallas kernels  25.8 us (32%)
  waiting for transfers between devices  14.2 us (18%)
  local copies, waits for them, and re-layouts  3.16 us (4%)
  between operations  2.04 us (3%)
  other arithmetic  1.57 us (2%)
    ppermute x13, starting transfers between devices, swap(): lax.ppermute(value, axis, [(i, route(i) % size) for i in range(size)])  33.7 us
    pallas_call x1, Pallas kernels, local(): call(functools.partial(tile_kernel, plate_count), [((half * block, width)...  19.2 us
    ppermute x13, waiting for transfers between devices, swap(): lax.ppermute(value, axis, [(i, route(i) % size) for i in range(size)])  14.2 us
    unnamed x28, local copies, waits for them, and re-layouts  3.16 us
    pallas_call x1, Pallas kernels, local(): call(functools.partial(add_kernel, cut), [((cut, width), F32), ((held - c...  1.83 us
    pallas_call x1, Pallas kernels, local(): call(functools.partial(finish_kernel, atoms), [((1, atoms, width), F32),...  1.71 us
  transfers between devices with their start and end apart: 13, of which 7 were waited for; matrix products, arithmetic and copies ran while one was open for 1% of the time, Pallas kernels for 2%

profile of v6, /device:TPU:0, one launch (start us, length us, event | category | flops | bytes accessed | tf_op | source)
XLA Modules:
  0.0 80.5 jit_solution(13301701538113455625)
XLA Ops:
  1.3 1.6 %shard_map.163 = (bf16[272,128]{1,0:T(8,128)(2,1)}, bf16[272,128]{1,0:T(8,128)(2,1)}) custom-call(s32[1,1]{1,0:T(1,128)S(6)} %copy.18.count_ref, bf16[1,256,128]{2,1,0:T(8,128)(2,1)} %feat_ref.1, bf16[1,256,128]{2,1,0:T(8,128)(2,1)} %adj_ref.1, bf16[3,256]{1,0:T(4,128)(2,1)} %bitcast.7), custom_call_target="tpu_custom_call" | custom-call | tf_op jit(solution)/shard_map/pallas_call | solution.py:518
  2.8 6.0 %collective-permute-start.1 = (bf16[272,128]{1,0:T(8,128)(2,1)}, bf16[272,128]{1,0:T(8,128)(2,1)S(1)}, u32[]{:S(2)}, u32[]{:S(2)}) collective-permute-start(bf16[272,128]{1,0:T(8,128)(2,1)} %get-tuple-element.22.refs_0_), channel_id=1, source_target_pairs={{0,28},{4,8},{8,4},{12,16},{16,12},{20,24},{24,20},{28,0},{1,29},{... | collective-permute-start | bytes 208904 | tf_op jit(solution)/shard_map/ppermute | solution.py:463
  8.8 0.0 collective-permute-start
  8.8 0.7 collective-permute-start.4
  9.5 0.8 %collective-permute-start.3 = (bf16[272,128]{1,0:T(8,128)(2,1)}, bf16[272,128]{1,0:T(8,128)(2,1)S(1)}, u32[]{:S(2)}, u32[]{:S(2)}) collective-permute-start(bf16[272,128]{1,0:T(8,128)(2,1)} %get-tuple-element.23.refs_3_), channel_id=1, source_target_pairs={{0,2},{1,3},{2,0},{3,1},{4,6},{5,7},{6,4},{7,5},{8,10},{9,11},{10,... | collective-permute-start | bytes 208904 | tf_op jit(solution)/shard_map/ppermute | solution.py:463
  10.4 0.3 collective-permute-start.2
  11.4 0.6 pad_add_fusion.where_ref
  11.9 0.0 collective-permute-done.1.refs_2_
  11.9 0.0 copy-start.4
  11.9 1.4 %collective-permute-done.refs_1_ = bf16[272,128]{1,0:T(8,128)(2,1)S(1)} collective-permute-done((bf16[272,128]{1,0:T(8,128)(2,1)}, bf16[272,128]{1,0:T(8,128)(2,1)S(1)}, u32[]{:S(2)}, u32[]{:S(2)}) %collective-permute-start) | collective-permute-done | bytes 69664 | tf_op jit(solution)/shard_map/ppermute | solution.py:463
  13.4 0.0 copy-start.5
  13.4 0.1 collective-permute-done.4.refs_6_
  13.5 0.0 copy-start.6
  13.5 1.6 %collective-permute-done.3.refs_5_ = bf16[272,128]{1,0:T(8,128)(2,1)S(1)} collective-permute-done((bf16[272,128]{1,0:T(8,128)(2,1)}, bf16[272,128]{1,0:T(8,128)(2,1)S(1)}, u32[]{:S(2)}, u32[]{:S(2)}) %collective-permute-start.3) | collective-permute-done | bytes 69664 | tf_op jit(solution)/shard_map/ppermute | solution.py:463
  15.0 0.0 copy-start.7
  15.0 0.0 collective-permute-done.2.refs_4_
  15.0 0.0 copy-start.8
  15.0 0.0 copy-done.4
  15.0 0.0 copy-done.5
  15.1 0.0 copy-done.6
  15.1 0.6 copy-done.7
  15.6 0.1 copy-done.8
  15.7 19.2 %shard_map.164 = (f32[544,128]{1,0:T(8,128)}, bf16[864,128]{1,0:T(8,128)(2,1)}, f32[160,128]{1,0:T(8,128)}, f32[16,128]{1,0:T(8,128)}, f32[16,128]{1,0:T(8,128)}) custom-call(s32[2]{0:T(128)} %pad_add_fusion.where_ref, s32[1,1]{1,0:T(1,128)S(6)} %copy.19.count_ref, s32[1,1,56]{2,1,0:T(1,128)} %tower_ref.1, s32[1,1,56]{2,1,0:T(1,128)} %plate_ref.1, ...), custom_call_target="tpu_custom_call" | custom-call | tf_op jit(solution)/shard_map/pallas_call | solution.py:527
  34.9 0.1 collective-permute-start.5
  35.0 1.6 %collective-permute-done.5.got_ref = bf16[864,128]{1,0:T(8,128)(2,1)S(1)} collective-permute-done((bf16[864,128]{1,0:T(8,128)(2,1)}, bf16[864,128]{1,0:T(8,128)(2,1)S(1)}, u32[]{:S(2)}, u32[]{:S(2)}) %collective-permute-start.5) | collective-permute-done | bytes 221216 | tf_op jit(solution)/shard_map/ppermute | solution.py:463
  36.6 0.0 copy-start.2
  36.6 0.7 copy-done.2
  37.3 1.8 %shard_map.165 = (f32[272,128]{1,0:T(8,128)}, bf16[592,128]{1,0:T(8,128)(2,1)}, f32[176,128]{1,0:T(8,128)}) custom-call(f32[544,128]{1,0:T(8,128)} %get-tuple-element.24.kept_ref, f32[160,128]{1,0:T(8,128)} %get-tuple-element.25.weight_ref, bf16[864,128]{1,0:T(8,128)(2,1)} %copy-done.2, f32[16,128]{1,0:T(8,128)} %get-tuple-element.27.near_ref), custom_call_target="tpu_custom_call" | custom-call | tf_op jit(solution)/shard_map/pallas_call | solution.py:589
  39.1 17.4 %collective-permute-start.6 = (bf16[592,128]{1,0:T(8,128)(2,1)}, bf16[592,128]{1,0:T(8,128)(2,1)S(1)}, u32[]{:S(2)}, u32[]{:S(2)}) collective-permute-start(bf16[592,128]{1,0:T(8,128)(2,1)} %get-tuple-element.29), channel_id=1, source_target_pairs={{0,2},{1,3},{2,0},{3,1},{4,6},{5,7},{6,4},{7,5},{8,10},{9,11},{10,... | collective-permute-start | bytes 454664 | tf_op jit(solution)/shard_map/ppermute | solution.py:463
  56.6 0.0 copy-start.13
  56.6 2.2 %collective-permute-start.9 = (f32[176,128]{1,0:T(8,128)}, f32[176,128]{1,0:T(8,128)S(1)}, u32[]{:S(2)}, u32[]{:S(2)}) collective-permute-start(f32[176,128]{1,0:T(8,128)} %get-tuple-element.30), channel_id=1, source_target_pairs={{0,6},{1,7},{2,4},{3,5},{4,2},{5,3},{6,0},{7,1},{8,14},{9,15},{10,... | collective-permute-start | bytes 270344 | tf_op jit(solution)/shard_map/ppermute | solution.py:463
  58.8 0.0 collective-permute-start.7
  58.8 4.1 %collective-permute-done.9 = f32[176,128]{1,0:T(8,128)S(1)} collective-permute-done((f32[176,128]{1,0:T(8,128)}, f32[176,128]{1,0:T(8,128)S(1)}, u32[]{:S(2)}, u32[]{:S(2)}) %collective-permute-start.9) | collective-permute-done | bytes 90144 | tf_op jit(solution)/shard_map/ppermute | solution.py:463
  62.9 0.6 collective-permute-done.7.near_ref
  63.5 0.0 copy-start.1
  63.5 0.0 collective-permute-done.6.got_ref
  63.5 0.0 copy-start
  63.5 1.0 %fusion.1.refs_0_ = bf16[160,128]{1,0:T(8,128)(2,1)S(1)} fusion(f32[176,128]{1,0:T(8,128)S(1)} %collective-permute-done.9, f32[176,128]{1,0:T(8,128)S(1)} %collective-permute-done.7.near_ref, f32[176,128]{1,0:T(8,128)} %get-tuple-element.30, bf16[592,128]{1,0:T(8,128)(2,1)S(1)} %collective-permute-done.6.got_ref), kind=kLoop, calls=%fused_computation.2 | loop fusion | flops 143360 | bytes 368640 | tf_op jit(solution)/shard_map/convert_element_type | solution.py:609
  64.5 0.0 copy-done.1
  64.5 0.0 copy-done
  64.5 0.0 copy-start.3
  64.5 0.7 collective-permute-start.12
  65.3 1.1 %collective-permute-start.11 = (bf16[160,128]{1,0:T(8,128)(2,1)S(1)}, bf16[160,128]{1,0:T(8,128)(2,1)S(1)}, u32[]{:S(2)}, u32[]{:S(2)}) collective-permute-start(bf16[160,128]{1,0:T(8,128)(2,1)S(1)} %fusion.1.refs_0_), channel_id=1, source_target_pairs={{0,16},{4,20},{8,24},{12,28},{16,0},{20,4},{24,8},{28,12},{1,17},{... | collective-permute-start | bytes 122888 | tf_op jit(solution)/shard_map/ppermute | solution.py:463
  66.3 2.6 %collective-permute-start.10 = (bf16[160,128]{1,0:T(8,128)(2,1)S(1)}, bf16[160,128]{1,0:T(8,128)(2,1)S(1)}, u32[]{:S(2)}, u32[]{:S(2)}) collective-permute-start(bf16[160,128]{1,0:T(8,128)(2,1)S(1)} %fusion.1.refs_0_), channel_id=1, source_target_pairs={{0,8},{4,12},{8,0},{12,4},{16,24},{20,28},{24,16},{28,20},{1,9},{5... | collective-permute-start | bytes 122888 | tf_op jit(solution)/shard_map/ppermute | solution.py:463
  69.0 0.0 copy-done.13
  69.0 1.6 %collective-permute-start.8 = (f32[16,128]{1,0:T(8,128)S(1)}, f32[16,128]{1,0:T(8,128)S(1)}, u32[]{:S(2)}, u32[]{:S(2)}) collective-permute-start(f32[16,128]{1,0:T(8,128)S(1)} %copy-done.13), channel_id=1, source_target_pairs={{0,28},{4,8},{8,4},{12,16},{16,12},{20,24},{24,20},{28,0},{1,29},{... | collective-permute-start | bytes 24584 | tf_op jit(solution)/shard_map/ppermute | solution.py:463
  70.6 4.7 %collective-permute-done.8.far_ref = f32[16,128]{1,0:T(8,128)S(1)} collective-permute-done((f32[16,128]{1,0:T(8,128)S(1)}, f32[16,128]{1,0:T(8,128)S(1)}, u32[]{:S(2)}, u32[]{:S(2)}) %collective-permute-start.8) | collective-permute-done | bytes 8224 | tf_op jit(solution)/shard_map/ppermute | solution.py:463
  75.3 0.0 copy-start.12
  75.3 0.6 copy-done.12
  75.9 1.7 %shard_map.166 = (f32[1,256,128]{2,1,0:T(8,128)}, f32[3,1,256]{2,1,0:T(1,128)}) custom-call(s32[1,1]{1,0:T(1,128)S(6)} %copy.18.count_ref, f32[272,128]{1,0:T(8,128)} %get-tuple-element.28.block_ref, bf16[592,128]{1,0:T(8,128)(2,1)} %copy-done, f32[176,128]{1,0:T(8,128)} %copy-done.1, f32[16,128]{1,0:T(8,128)} %copy-done.12), custom_call_target="tpu_custom_call" | custom-call | tf_op jit(solution)/shard_map/pallas_call | solution.py:613
  77.6 0.0 copy-done.3
  77.6 0.0 collective-permute-done.12.refs_3_
  77.7 0.0 copy-start.9
  77.7 0.0 collective-permute-done.11.refs_2_
  77.7 0.0 copy-start.10
  77.7 0.0 collective-permute-done.10.refs_1_
  77.7 0.6 copy-done.9
  78.3 0.0 copy-done.10
  78.3 0.0 copy-start.11
  78.3 0.6 copy-done.11
  78.9 1.6 %shard_map.167 = (f32[16,128]{1,0:T(8,128)}, f32[1,128]{1,0:T(1,128)}, f32[128,128]{1,0:T(8,128)}, f32[1,128]{1,0:T(1,128)}) custom-call(bf16[160,128]{1,0:T(8,128)(2,1)} %copy-done.3, bf16[160,128]{1,0:T(8,128)(2,1)} %copy-done.11, bf16[160,128]{1,0:T(8,128)(2,1)} %copy-done.10, bf16[160,128]{1,0:T(8,128)(2,1)} %copy-done.9), custom_call_target="tpu_custom_call" | custom-call | tf_op jit(solution)/shard_map/pallas_call | solution.py:618
Async XLA Ops:
  2.8 9.1 %collective-permute-start.1 = (bf16[272,128]{1,0:T(8,128)(2,1)}, bf16[272,128]{1,0:T(8,128)(2,1)S(1)}, u32[]{:S(2)}, u32[]{:S(2)}) collective-permute-start(bf16[272,128]{1,0:T(8,128)(2,1)} %get-tuple-element.22.refs_0_), channel_id=1, source_target_pairs={{0,28},{4,8},{8,4},{12,16},{16,12},{20,24},{24,20},{28,0},{1,29},{... | collective-permute-start | bytes 208904 | tf_op jit(solution)/shard_map/ppermute | solution.py:463
  8.8 4.5 %collective-permute-start = (bf16[272,128]{1,0:T(8,128)(2,1)}, bf16[272,128]{1,0:T(8,128)(2,1)S(1)}, u32[]{:S(2)}, u32[]{:S(2)}) collective-permute-start(bf16[272,128]{1,0:T(8,128)(2,1)} %get-tuple-element.22.refs_0_), channel_id=1, source_target_pairs={{0,4},{4,0},{8,12},{12,8},{16,20},{20,16},{24,28},{28,24},{1,5},{5... | collective-permute-start | bytes 208904 | tf_op jit(solution)/shard_map/ppermute | solution.py:463
  8.8 4.6 %collective-permute-start.4 = (bf16[272,128]{1,0:T(8,128)(2,1)}, bf16[272,128]{1,0:T(8,128)(2,1)S(1)}, u32[]{:S(2)}, u32[]{:S(2)}) collective-permute-start(bf16[272,128]{1,0:T(8,128)(2,1)} %get-tuple-element.23.refs_3_), channel_id=1, source_target_pairs={{0,3},{1,2},{2,1},{3,0},{4,7},{5,6},{6,5},{7,4},{8,11},{9,10},{10,... | collective-permute-start | bytes 208904 | tf_op jit(solution)/shard_map/ppermute | solution.py:463
  9.5 5.5 %collective-permute-start.3 = (bf16[272,128]{1,0:T(8,128)(2,1)}, bf16[272,128]{1,0:T(8,128)(2,1)S(1)}, u32[]{:S(2)}, u32[]{:S(2)}) collective-permute-start(bf16[272,128]{1,0:T(8,128)(2,1)} %get-tuple-element.23.refs_3_), channel_id=1, source_target_pairs={{0,2},{1,3},{2,0},{3,1},{4,6},{5,7},{6,4},{7,5},{8,10},{9,11},{10,... | collective-permute-start | bytes 208904 | tf_op jit(solution)/shard_map/ppermute | solution.py:463
  10.4 4.7 %collective-permute-start.2 = (bf16[272,128]{1,0:T(8,128)(2,1)}, bf16[272,128]{1,0:T(8,128)(2,1)S(1)}, u32[]{:S(2)}, u32[]{:S(2)}) collective-permute-start(bf16[272,128]{1,0:T(8,128)(2,1)} %get-tuple-element.23.refs_3_), channel_id=1, source_target_pairs={{0,1},{1,0},{2,3},{3,2},{4,5},{5,4},{6,7},{7,6},{8,9},{9,8},{10,11... | collective-permute-start | bytes 208904 | tf_op jit(solution)/shard_map/ppermute | solution.py:463
  11.9 3.1 %copy-start.4 = (bf16[272,128]{1,0:T(8,128)(2,1)}, bf16[272,128]{1,0:T(8,128)(2,1)S(1)}, u32[]{:S(2)}) copy-start(bf16[272,128]{1,0:T(8,128)(2,1)S(1)} %collective-permute-done.1.refs_2_) | copy-start | bytes 208900
  13.4 1.7 %copy-start.5 = (bf16[272,128]{1,0:T(8,128)(2,1)}, bf16[272,128]{1,0:T(8,128)(2,1)S(1)}, u32[]{:S(2)}) copy-start(bf16[272,128]{1,0:T(8,128)(2,1)S(1)} %collective-permute-done.refs_1_) | copy-start | bytes 208900
  13.5 1.6 %copy-start.6 = (bf16[272,128]{1,0:T(8,128)(2,1)}, bf16[272,128]{1,0:T(8,128)(2,1)S(1)}, u32[]{:S(2)}) copy-start(bf16[272,128]{1,0:T(8,128)(2,1)S(1)} %collective-permute-done.4.refs_6_) | copy-start | bytes 208900
  15.0 0.6 copy-start.7
  15.0 0.7 copy-start.8
  34.9 1.7 %collective-permute-start.5 = (bf16[864,128]{1,0:T(8,128)(2,1)}, bf16[864,128]{1,0:T(8,128)(2,1)S(1)}, u32[]{:S(2)}, u32[]{:S(2)}) collective-permute-start(bf16[864,128]{1,0:T(8,128)(2,1)} %get-tuple-element.26), channel_id=1, source_target_pairs={{0,1},{1,0},{2,3},{3,2},{4,5},{5,4},{6,7},{7,6},{8,9},{9,8},{10,11... | collective-permute-start | bytes 663560 | tf_op jit(solution)/shard_map/ppermute | solution.py:463
  36.6 0.7 copy-start.2
  39.1 24.4 %collective-permute-start.6 = (bf16[592,128]{1,0:T(8,128)(2,1)}, bf16[592,128]{1,0:T(8,128)(2,1)S(1)}, u32[]{:S(2)}, u32[]{:S(2)}) collective-permute-start(bf16[592,128]{1,0:T(8,128)(2,1)} %get-tuple-element.29), channel_id=1, source_target_pairs={{0,2},{1,3},{2,0},{3,1},{4,6},{5,7},{6,4},{7,5},{8,10},{9,11},{10,... | collective-permute-start | bytes 454664 | tf_op jit(solution)/shard_map/ppermute | solution.py:463
  56.6 12.4 %copy-start.13 = (f32[16,128]{1,0:T(8,128)S(1)}, f32[16,128]{1,0:T(8,128)}, u32[]{:S(2)}) copy-start(f32[16,128]{1,0:T(8,128)} %get-tuple-element.31) | copy-start | bytes 24580
  56.6 6.3 %collective-permute-start.9 = (f32[176,128]{1,0:T(8,128)}, f32[176,128]{1,0:T(8,128)S(1)}, u32[]{:S(2)}, u32[]{:S(2)}) collective-permute-start(f32[176,128]{1,0:T(8,128)} %get-tuple-element.30), channel_id=1, source_target_pairs={{0,6},{1,7},{2,4},{3,5},{4,2},{5,3},{6,0},{7,1},{8,14},{9,15},{10,... | collective-permute-start | bytes 270344 | tf_op jit(solution)/shard_map/ppermute | solution.py:463
  58.8 4.7 %collective-permute-start.7 = (f32[176,128]{1,0:T(8,128)}, f32[176,128]{1,0:T(8,128)S(1)}, u32[]{:S(2)}, u32[]{:S(2)}) collective-permute-start(f32[176,128]{1,0:T(8,128)} %get-tuple-element.30), channel_id=1, source_target_pairs={{0,4},{4,0},{8,12},{12,8},{16,20},{20,16},{24,28},{28,24},{1,5},{5... | collective-permute-start | bytes 270344 | tf_op jit(solution)/shard_map/ppermute | solution.py:463
  63.5 1.0 %copy-start.1 = (f32[176,128]{1,0:T(8,128)}, f32[176,128]{1,0:T(8,128)S(1)}, u32[]{:S(2)}) copy-start(f32[176,128]{1,0:T(8,128)S(1)} %collective-permute-done.7.near_ref) | copy-start | bytes 270340
  63.5 1.0 %copy-start = (bf16[592,128]{1,0:T(8,128)(2,1)}, bf16[592,128]{1,0:T(8,128)(2,1)S(1)}, u32[]{:S(2)}) copy-start(bf16[592,128]{1,0:T(8,128)(2,1)S(1)} %collective-permute-done.6.got_ref) | copy-start | bytes 454660
  64.5 13.1 %copy-start.3 = (bf16[160,128]{1,0:T(8,128)(2,1)}, bf16[160,128]{1,0:T(8,128)(2,1)S(1)}, u32[]{:S(2)}) copy-start(bf16[160,128]{1,0:T(8,128)(2,1)S(1)} %fusion.1.refs_0_) | copy-start | bytes 122884
  64.5 13.1 %collective-permute-start.12 = (bf16[160,128]{1,0:T(8,128)(2,1)S(1)}, bf16[160,128]{1,0:T(8,128)(2,1)S(1)}, u32[]{:S(2)}, u32[]{:S(2)}) collective-permute-start(bf16[160,128]{1,0:T(8,128)(2,1)S(1)} %fusion.1.refs_0_), channel_id=1, source_target_pairs={{0,24},{4,28},{8,16},{12,20},{16,8},{20,12},{24,0},{28,4},{1,25},{... | collective-permute-start | bytes 122888 | tf_op jit(solution)/shard_map/ppermute | solution.py:463
  65.3 12.4 %collective-permute-start.11 = (bf16[160,128]{1,0:T(8,128)(2,1)S(1)}, bf16[160,128]{1,0:T(8,128)(2,1)S(1)}, u32[]{:S(2)}, u32[]{:S(2)}) collective-permute-start(bf16[160,128]{1,0:T(8,128)(2,1)S(1)} %fusion.1.refs_0_), channel_id=1, source_target_pairs={{0,16},{4,20},{8,24},{12,28},{16,0},{20,4},{24,8},{28,12},{1,17},{... | collective-permute-start | bytes 122888 | tf_op jit(solution)/shard_map/ppermute | solution.py:463
  66.3 11.4 %collective-permute-start.10 = (bf16[160,128]{1,0:T(8,128)(2,1)S(1)}, bf16[160,128]{1,0:T(8,128)(2,1)S(1)}, u32[]{:S(2)}, u32[]{:S(2)}) collective-permute-start(bf16[160,128]{1,0:T(8,128)(2,1)S(1)} %fusion.1.refs_0_), channel_id=1, source_target_pairs={{0,8},{4,12},{8,0},{12,4},{16,24},{20,28},{24,16},{28,20},{1,9},{5... | collective-permute-start | bytes 122888 | tf_op jit(solution)/shard_map/ppermute | solution.py:463
  69.0 6.3 %collective-permute-start.8 = (f32[16,128]{1,0:T(8,128)S(1)}, f32[16,128]{1,0:T(8,128)S(1)}, u32[]{:S(2)}, u32[]{:S(2)}) collective-permute-start(f32[16,128]{1,0:T(8,128)S(1)} %copy-done.13), channel_id=1, source_target_pairs={{0,28},{4,8},{8,4},{12,16},{16,12},{20,24},{24,20},{28,0},{1,29},{... | collective-permute-start | bytes 24584 | tf_op jit(solution)/shard_map/ppermute | solution.py:463
  75.3 0.6 copy-start.12
  77.7 0.6 copy-start.9
  77.7 0.6 copy-start.10
  78.3 0.6 copy-start.11
